TPU v7x, 32 devices: a whole 2x2x4 slice. The times are simulated.
32 devices in a mesh: seq: 16 (over z, y, x), feat: 2 (over core).
Axes of the slice: x: 2, y: 2, z: 4, core: 2. Of those that a mesh axis runs over, the one named last changes fastest.
Arguments:
- tokens: bfloat16 [131072, 1280], P(('seq', 'feat')), may hold values from -12 to 12
- shot_starts: int32 [32], replicated, may hold values from 0 to 128512, as said below
- seed_offsets: int32 [32, 64], replicated, may hold values from 0 to 1023, as said below
- norm_gain: float32 [1280], replicated, may hold values from 0.5 to 1.5
- proj_weight: bfloat16 [1280, 8192], P(None, 'feat'), may hold values from -0.15625 to 0.15625
Outputs:
- projected: bfloat16 [2048, 8192], P('seq', 'feat')
Inputs may be any that keep to these rules, and one draw needn't show every extreme that they name: shot_starts[0] = 0, the starts rise, and shot s starts within 1536 tokens of s * 4096, so a shot has 1024 to 7168 tokens. `seed_offsets`: each row holds 64 different offsets, all below 1024.
All inputs are finite; a program needn't handle non-finite values.
Results may differ from a plain program's by a relative error of at most 0.0055.
Values may be sent and summed in bfloat16 or wider, within the bound.
No kernel may reach another device: no remote copies, remote signals or barrier semaphores. Data moves between devices by JAX's collectives and lax.ppermute only.
A program may use at most 128 MiB of HBM per device.

v0:
```python
import functools
import math

import jax
import jax.numpy as jnp
from jax import lax
from jax.experimental import pallas as pl
from jax.experimental.pallas import tpu as pltpu
from jax.sharding import PartitionSpec as P

ITERS = 3
AXES = ("seq", "feat")
LANES = 128
TILE = 512
F32 = jnp.float32
BF16 = jnp.bfloat16
VMEM_SPEC = pl.BlockSpec(memory_space=pltpu.VMEM)
HBM_SPEC = pl.BlockSpec(memory_space=pltpu.HBM)
SMEM_SPEC = pl.BlockSpec(memory_space=pltpu.SMEM)


def start_of(starts_ref, shot, shots, total):
    first = starts_ref[jnp.minimum(shot, shots - 1)]
    return jnp.where(shot >= shots, total, first)


def placement(index, starts_ref, rows):
    shots = starts_ref.shape[0]
    total = shots * rows
    second = index % 2 == 1
    here = start_of(starts_ref, index, shots, total)
    after = start_of(starts_ref, index + 1, shots, total)
    base = index * rows
    low = jnp.where(second, here, base)
    high = jnp.where(second, base + rows, after)
    cut = jnp.where(second, after, here)
    split = jnp.where(second, after < base + rows, here > base)
    x_low = jnp.where(split & second, cut, low)
    x_high = jnp.where(split & ~second, cut, high)
    y_low = jnp.where(split, jnp.where(second, low, cut), high)
    y_high = jnp.where(split, jnp.where(second, cut, high), high)
    return split, x_low, x_high, y_low, y_high


def column_of(row):
    n = row.shape[1]
    diagonal = lax.broadcasted_iota(jnp.int32, (n, n), 0) == lax.broadcasted_iota(
        jnp.int32, (n, n), 1
    )
    spread = jnp.where(diagonal, jnp.broadcast_to(row, (n, n)), 0)
    return jnp.sum(spread, axis=1, keepdims=True)


def seed_kernel(
    place_ref,
    starts_hbm,
    seeds_hbm,
    tokens_ref,
    first_ref,
    own_ref,
    give_ref,
    edge_ref,
    meta_ref,
    starts_ref,
    seeds_ref,
    seed_rows_ref,
    picked,
    index_sems,
    pick_sem,
    edge_sem,
):
    rows = tokens_ref.shape[0]
    reach = edge_ref.shape[0]
    shots, count = seeds_ref.shape
    total = shots * rows
    index = place_ref[0]
    second = index % 2 == 1
    base = index * rows
    indices = [
        pltpu.make_async_copy(starts_hbm, starts_ref, index_sems.at[0]),
        pltpu.make_async_copy(seeds_hbm, seeds_ref, index_sems.at[1]),
        pltpu.make_async_copy(seeds_hbm, seed_rows_ref, index_sems.at[2]),
    ]
    for copy in indices:
        copy.start()
    strip_low = pl.multiple_of(jnp.where(second, 0, rows - reach), 8)
    strip = pltpu.make_async_copy(tokens_ref.at[pl.ds(strip_low, reach), :], edge_ref, edge_sem)
    strip.start()
    for copy in indices:
        copy.wait()
    following = jnp.minimum(index + 1, shots - 1)
    here = start_of(starts_ref, index, shots, total)
    after = start_of(starts_ref, index + 1, shots, total)
    later = start_of(starts_ref, index + 2, shots, total)

    def fetch(k, carry):
        for which, (shot, begin) in enumerate(((index, here), (following, after))):
            place = jnp.clip(begin + seeds_ref[shot, k] - base, 0, rows - 1)
            group = pl.multiple_of((place // 8) * 8, 8)
            slot = pl.multiple_of((which * count + k) * 8, 8)
            pltpu.make_async_copy(
                tokens_ref.at[pl.ds(group, 8), :], picked.at[pl.ds(slot, 8), :], pick_sem
            ).start()
        return carry

    lax.fori_loop(0, count, fetch, 0, unroll=8)
    for at, value in enumerate(placement(index, starts_ref, rows)):
        meta_ref[at] = value.astype(jnp.int32)
    choices = []
    for shot, begin in ((index, here), (following, after)):
        place = column_of(seed_rows_ref[pl.ds(shot, 1), :]) + (begin - base)
        valid = (place >= 0) & (place < rows)
        target = lax.broadcasted_iota(jnp.int32, (count, 1), 0) * 8 + place % 8
        lane = lax.broadcasted_iota(jnp.int32, (count, 8 * count), 1)
        choices.append(jnp.where(valid & (lane == target), 1.0, 0.0).astype(BF16))
    pltpu.make_async_copy(tokens_ref.at[pl.ds(0, 16 * count), :], picked, pick_sem).wait()
    own, tail = (
        jnp.dot(
            choose,
            picked[pl.ds(which * 8 * count, 8 * count), :],
            preferred_element_type=F32,
        )
        for which, choose in enumerate(choices)
    )
    ahead = jnp.where(second, after < base + rows, here > base)
    first = jnp.where(ahead, jnp.where(second, tail, 0.0), own)
    first_ref[...] = first.astype(BF16)
    own_ref[...] = own.astype(BF16)
    shared = later >= base + 2 * rows
    give_ref[pl.ds(0, count), :] = jnp.where(shared, tail, 0.0).astype(BF16)
    give_ref[pl.ds(count, count), :] = tail.astype(BF16)
    strip.wait()


def load_kernel(tokens_ref, after_ref, out_ref, sems):
    pieces = sems.shape[0]
    piece = tokens_ref.shape[0] // pieces
    copies = [
        pltpu.make_async_copy(
            tokens_ref.at[pl.ds(i * piece, piece), :],
            out_ref.at[pl.ds(i * piece, piece), :],
            sems.at[i],
        )
        for i in range(pieces)
    ]
    for copy in copies:
        copy.start()
    for copy in copies:
        copy.wait()


def total_mass(block):
    return jnp.sum(block.astype(F32), axis=1, keepdims=True)


def pool_kernel(
    first,
    place_ref,
    meta_ref,
    tokens_ref,
    edge_ref,
    x_ref,
    recv_ref,
    mass_ref,
    y_ref,
    send_out,
    x_out,
    mass_out,
    y_out,
    centroids,
    sums,
    masses,
):
    rows, width = tokens_ref.shape
    count = y_ref.shape[0]
    reach = edge_ref.shape[0]
    index = place_ref[0]
    base = index * rows
    edge_base = jnp.where(index % 2 == 1, base - reach, base + rows)
    x_range = (meta_ref[1], meta_ref[2])
    y_range = (meta_ref[3], meta_ref[4])
    scale = math.log2(math.e) / math.sqrt(width)

    if first:
        centroids[pl.ds(0, count), :] = x_ref[...] + recv_ref[...]
        centroids[pl.ds(count, count), :] = y_ref[...]
    else:
        mass = mass_ref[:, :1] + total_mass(recv_ref[:, width:])
        joined = x_ref[...] + recv_ref[:, :width].astype(F32)
        centroids[pl.ds(0, count), :] = (joined / mass).astype(BF16)
        centroids[pl.ds(count, count), :] = y_ref[...].astype(BF16)
    sums[...] = jnp.zeros_like(sums)
    masses[...] = jnp.zeros_like(masses)

    tiles = [(tokens_ref, i * TILE, base + i * TILE) for i in range(rows // TILE)]
    tiles += [(edge_ref, i * TILE, edge_base + i * TILE) for i in range(reach // TILE)]

    def scores_of(tile):
        ref, row, _ = tile
        return lax.dot_general(
            centroids[...],
            ref[pl.ds(row, TILE), :],
            (((1,), (1,)), ((), ())),
            preferred_element_type=F32,
        )

    def weights_of(tile, scores):
        place = tile[2] + lax.broadcasted_iota(jnp.int32, (1, TILE), 1)
        in_x = (place >= x_range[0]) & (place < x_range[1])
        in_y = (place >= y_range[0]) & (place < y_range[1])
        mine = jnp.where(in_y, scores[count:], scores[:count])
        top = jnp.max(mine, axis=0, keepdims=True)
        powers = jnp.exp2((mine - top) * scale)
        inverse = 1.0 / jnp.sum(powers, axis=0, keepdims=True)
        weights = jnp.concatenate(
            [powers * jnp.where(in_x, inverse, 0.0), powers * jnp.where(in_y, inverse, 0.0)], axis=0
        )
        part = weights[:, :LANES]
        for i in range(1, TILE // LANES):
            part = part + weights[:, i * LANES : (i + 1) * LANES]
        masses[...] += part
        return weights.astype(BF16)

    scores = scores_of(tiles[0])
    for at, tile in enumerate(tiles):
        upcoming = scores_of(tiles[at + 1]) if at + 1 < len(tiles) else None
        weights = weights_of(tile, scores)
        sums[...] += jnp.dot(
            weights, tile[0][pl.ds(tile[1], TILE), :], preferred_element_type=F32
        )
        scores = upcoming

    mass = jnp.sum(masses[...], axis=1, keepdims=True)
    x_mass = mass[:count]
    x_sums = sums[pl.ds(0, count), :]
    x_out[...] = x_sums
    mass_out[...] = jnp.broadcast_to(x_mass, mass_out.shape)
    y_out[...] = sums[pl.ds(count, count), :] / mass[count:]
    send_out[:, :width] = x_sums.astype(BF16)
    high = x_mass.astype(BF16).astype(F32)
    middle = (x_mass - high).astype(BF16).astype(F32)
    low = x_mass - high - middle
    lane = lax.broadcasted_iota(jnp.int32, (count, LANES), 1)
    block = jnp.where(
        lane == 0, high, jnp.where(lane == 1, middle, jnp.where(lane == 2, low, 0.0))
    )
    send_out[:, width:] = block.astype(BF16)


def norm_kernel(meta_ref, x_ref, recv_ref, mass_ref, y_ref, gain_ref, out_ref):
    width = x_ref.shape[1]
    split = meta_ref[0] != 0
    mass = mass_ref[:, :1] + total_mass(recv_ref[:, width:])
    joined = (x_ref[...] + recv_ref[:, :width].astype(F32)) / mass
    centroid = jnp.where(split, y_ref[...], joined)
    spread = jnp.sqrt(jnp.mean(centroid * centroid, axis=-1, keepdims=True) + 1e-06)
    out_ref[...] = (centroid / spread * gain_ref[...]).astype(BF16)


def on_device(tokens, shot_starts, seed_offsets, norm_gain, proj_weight):
    rows, width = tokens.shape
    count = seed_offsets.shape[1]
    reach = 3 * rows // 8
    devices = lax.axis_size(AXES)
    place = lax.axis_index(AXES).astype(jnp.int32).reshape(1)
    across = [(i, i + 1) for i in range(1, devices - 1, 2)]
    across += [(target, source) for source, target in across]

    def shape(*dims, dtype=BF16):
        return jax.ShapeDtypeStruct(dims, dtype)

    far_tokens = pltpu.with_memory_space_constraint(tokens, pltpu.HBM)
    first, own, give, edge, meta = pl.pallas_call(
        seed_kernel,
        out_shape=(
            shape(count, width),
            shape(count, width),
            shape(2 * count, width),
            shape(reach, width),
            shape(8, dtype=jnp.int32),
        ),
        in_specs=[SMEM_SPEC, HBM_SPEC, HBM_SPEC, HBM_SPEC],
        out_specs=[VMEM_SPEC, VMEM_SPEC, VMEM_SPEC, VMEM_SPEC, SMEM_SPEC],
        scratch_shapes=[
            pltpu.SMEM(shot_starts.shape, jnp.int32),
            pltpu.SMEM(seed_offsets.shape, jnp.int32),
            pltpu.VMEM(seed_offsets.shape, jnp.int32),
            pltpu.VMEM((16 * count, width), BF16),
            pltpu.SemaphoreType.DMA((3,)),
            pltpu.SemaphoreType.DMA(()),
            pltpu.SemaphoreType.DMA(()),
        ],
        compiler_params=pltpu.CompilerParams(vmem_limit_bytes=16 << 20),
        name="seeds",
    )(
        place,
        pltpu.with_memory_space_constraint(shot_starts, pltpu.HBM),
        pltpu.with_memory_space_constraint(seed_offsets, pltpu.HBM),
        far_tokens,
    )
    given = lax.ppermute(give, "feat", [(0, 1)])
    edge, given = lax.optimization_barrier((edge, given))
    edge = lax.ppermute(edge, "feat", [(0, 1), (1, 0)])
    x = first + given[:count]
    y = own + given[count:]
    received = lax.ppermute(x, AXES, across)
    near_tokens = pl.pallas_call(
        load_kernel,
        out_shape=shape(rows, width),
        in_specs=[HBM_SPEC, VMEM_SPEC],
        out_specs=VMEM_SPEC,
        scratch_shapes=[pltpu.SemaphoreType.DMA((4,))],
        compiler_params=pltpu.CompilerParams(vmem_limit_bytes=16 << 20),
        name="load",
    )(far_tokens, x)
    mass = jnp.zeros((count, LANES), F32)
    for iteration in range(ITERS):
        send, x, mass, y = pl.pallas_call(
            functools.partial(pool_kernel, iteration == 0),
            out_shape=(
                shape(count, width + LANES),
                shape(count, width, dtype=F32),
                shape(count, LANES, dtype=F32),
                shape(count, width, dtype=F32),
            ),
            in_specs=[SMEM_SPEC] * 2 + [VMEM_SPEC] * 6,
            out_specs=[VMEM_SPEC] * 4,
            scratch_shapes=[
                pltpu.VMEM((2 * count, width), BF16),
                pltpu.VMEM((2 * count, width), F32),
                pltpu.VMEM((2 * count, LANES), F32),
            ],
            compiler_params=pltpu.CompilerParams(vmem_limit_bytes=16 << 20),
            name="pool",
        )(place, meta, near_tokens, edge, x, received, mass, y)
        received = lax.ppermute(send, AXES, across)
    normed = pl.pallas_call(
        norm_kernel,
        out_shape=shape(count, width),
        in_specs=[SMEM_SPEC] + [VMEM_SPEC] * 5,
        out_specs=VMEM_SPEC,
        compiler_params=pltpu.CompilerParams(vmem_limit_bytes=8 << 20),
        name="norm",
    )(meta, x, received, mass, y, norm_gain[None, :])
    projected = jnp.dot(
        lax.all_gather(normed, "feat", axis=0, tiled=True),
        proj_weight,
        preferred_element_type=F32,
    )
    return projected.astype(BF16)


def solution(mesh):
    in_specs = (P(AXES, None), P(), P(), P(), P(None, "feat"))
    out_specs = P("seq", "feat")
    return jax.shard_map(
        on_device, mesh=mesh, in_specs=in_specs, out_specs=out_specs, check_vma=False
    )
```

profile of v0, /device:TPU:29, one launch (start us, length us, event | category | flops | bytes accessed | tf_op | source)
XLA Modules:
  0.0 73.6 jit_solution(10393047598902749900)
XLA Ops:
  0.0 5.8 %seeds.1 = (bf16[64,1280]{1,0:T(8,128)(2,1)S(1)}, bf16[64,1280]{1,0:T(8,128)(2,1)S(1)}, bf16[128,1280]{1,0:T(8,128)(2,1)S(1)}, bf16[1536,1280]{1,0:T(8,128)(2,1)S(1)}, s32[8]{0:T(128)S(1)}) custom-call(s32[1]{0:T(128)} %bitcast.place_ref, s32[32]{0:T(128)} %starts_hbm.1, s32[32,64]{1,0:T(8,128)} %seeds_hbm.1, bf16[4096,1280]{1,0:T(8,128)(2,1)} %tokens_ref.3), custom_call_target="tpu_custom_call" | custom-call | tf_op jit(solution)/shard_map/seeds/pallas_call | solution.py:273
  5.8 1.3 %collective-permute-start = (bf16[128,1280]{1,0:T(8,128)(2,1)S(1)}, bf16[128,1280]{1,0:T(8,128)(2,1)S(1)}, u32[]{:S(2)}, u32[]{:S(2)}) collective-permute-start(bf16[128,1280]{1,0:T(8,128)(2,1)S(1)} %get-tuple-element.27), channel_id=1, source_target_pairs={{0,1},{2,3},{4,5},{6,7},{8,9},{10,11},{12,13},{14,15},{16,17},{18,... | collective-permute-start | bytes 983048 | tf_op jit(solution)/shard_map/ppermute | solution.py:301
  7.1 2.2 %collective-permute-done = bf16[128,1280]{1,0:T(8,128)(2,1)S(1)} collective-permute-done((bf16[128,1280]{1,0:T(8,128)(2,1)S(1)}, bf16[128,1280]{1,0:T(8,128)(2,1)S(1)}, u32[]{:S(2)}, u32[]{:S(2)}) %collective-permute-start) | collective-permute-done | bytes 327712 | tf_op jit(solution)/shard_map/ppermute | solution.py:301
  9.3 0.1 collective-permute-start.1
  9.5 5.2 %collective-permute-start.2 = (bf16[64,1280]{1,0:T(8,128)(2,1)S(1)}, bf16[64,1280]{1,0:T(8,128)(2,1)S(1)}, u32[]{:S(2)}, u32[]{:S(2)}) collective-permute-start(bf16[64,1280]{1,0:T(8,128)(2,1)S(1)} %get-tuple-element.44.after_ref.x_ref), channel_id=1, source_target_pairs={{1,2},{3,4},{5,6},{7,8},{9,10},{11,12},{13,14},{15,16},{17,18},{19... | collective-permute-start | bytes 491528 | tf_op jit(solution)/shard_map/ppermute | solution.py:306
  14.8 4.1 %load.1.tokens_ref = bf16[4096,1280]{1,0:T(8,128)(2,1)S(1)} custom-call(bf16[4096,1280]{1,0:T(8,128)(2,1)} %tokens_ref.3, bf16[64,1280]{1,0:T(8,128)(2,1)S(1)} %get-tuple-element.44.after_ref.x_ref), custom_call_target="tpu_custom_call" | custom-call | tf_op jit(solution)/shard_map/load/pallas_call | solution.py:307
  18.9 0.6 collective-permute-done.2.recv_ref
  19.5 0.0 collective-permute-done.1.edge_ref
  19.5 7.3 %pool.3 = (bf16[64,1408]{1,0:T(8,128)(2,1)S(1)}, f32[64,1280]{1,0:T(8,128)S(1)}, f32[64,128]{1,0:T(8,128)S(1)}, f32[64,1280]{1,0:T(8,128)S(1)}) custom-call(s32[1]{0:T(128)} %bitcast.place_ref, s32[8]{0:T(128)S(1)} %get-tuple-element.24.meta_ref, bf16[4096,1280]{1,0:T(8,128)(2,1)S(1)} %load.1.tokens_ref, ...), custom_call_target="tpu_custom_call" | custom-call | tf_op jit(solution)/shard_map/pool/pallas_call | solution.py:318
  26.8 2.8 %collective-permute-start.3 = (bf16[64,1408]{1,0:T(8,128)(2,1)S(1)}, bf16[64,1408]{1,0:T(8,128)(2,1)S(1)}, u32[]{:S(2)}, u32[]{:S(2)}) collective-permute-start(bf16[64,1408]{1,0:T(8,128)(2,1)S(1)} %get-tuple-element.32), channel_id=1, source_target_pairs={{1,2},{3,4},{5,6},{7,8},{9,10},{11,12},{13,14},{15,16},{17,18},{19... | collective-permute-start | bytes 540680 | tf_op jit(solution)/shard_map/ppermute | solution.py:336
  29.6 5.9 %collective-permute-done.3.recv_ref = bf16[64,1408]{1,0:T(8,128)(2,1)S(1)} collective-permute-done((bf16[64,1408]{1,0:T(8,128)(2,1)S(1)}, bf16[64,1408]{1,0:T(8,128)(2,1)S(1)}, u32[]{:S(2)}, u32[]{:S(2)}) %collective-permute-start.3) | collective-permute-done | bytes 180256 | tf_op jit(solution)/shard_map/ppermute | solution.py:336
  35.5 0.0 slice-start
  35.5 0.0 slice-start.1
  35.5 7.5 %pool.4 = (bf16[64,1408]{1,0:T(8,128)(2,1)S(1)}, f32[64,1280]{1,0:T(8,128)S(1)}, f32[64,128]{1,0:T(8,128)S(1)}, f32[64,1280]{1,0:T(8,128)S(1)}) custom-call(s32[1]{0:T(128)} %bitcast.place_ref, s32[8]{0:T(128)S(1)} %get-tuple-element.24.meta_ref, bf16[4096,1280]{1,0:T(8,128)(2,1)S(1)} %load.1.tokens_ref, ...), custom_call_target="tpu_custom_call" | custom-call | tf_op jit(solution)/shard_map/pool/pallas_call | solution.py:318
  43.0 0.0 copy-start
  43.0 2.9 %collective-permute-start.4 = (bf16[64,1408]{1,0:T(8,128)(2,1)S(1)}, bf16[64,1408]{1,0:T(8,128)(2,1)S(1)}, u32[]{:S(2)}, u32[]{:S(2)}) collective-permute-start(bf16[64,1408]{1,0:T(8,128)(2,1)S(1)} %get-tuple-element.36), channel_id=1, source_target_pairs={{1,2},{3,4},{5,6},{7,8},{9,10},{11,12},{13,14},{15,16},{17,18},{19... | collective-permute-start | bytes 540680 | tf_op jit(solution)/shard_map/ppermute | solution.py:336
  46.0 5.8 %collective-permute-done.4.recv_ref = bf16[64,1408]{1,0:T(8,128)(2,1)S(1)} collective-permute-done((bf16[64,1408]{1,0:T(8,128)(2,1)S(1)}, bf16[64,1408]{1,0:T(8,128)(2,1)S(1)}, u32[]{:S(2)}, u32[]{:S(2)}) %collective-permute-start.4) | collective-permute-done | bytes 180256 | tf_op jit(solution)/shard_map/ppermute | solution.py:336
  51.8 0.0 slice-start.2
  51.8 7.5 %pool.5 = (bf16[64,1408]{1,0:T(8,128)(2,1)S(1)}, f32[64,1280]{1,0:T(8,128)S(1)}, f32[64,128]{1,0:T(8,128)S(1)}, f32[64,1280]{1,0:T(8,128)S(1)}) custom-call(s32[1]{0:T(128)} %bitcast.place_ref, s32[8]{0:T(128)S(1)} %get-tuple-element.24.meta_ref, bf16[4096,1280]{1,0:T(8,128)(2,1)S(1)} %load.1.tokens_ref, ...), custom_call_target="tpu_custom_call" | custom-call | tf_op jit(solution)/shard_map/pool/pallas_call | solution.py:318
  59.3 1.9 %collective-permute-start.5 = (bf16[64,1408]{1,0:T(8,128)(2,1)S(1)}, bf16[64,1408]{1,0:T(8,128)(2,1)S(1)}, u32[]{:S(2)}, u32[]{:S(2)}) collective-permute-start(bf16[64,1408]{1,0:T(8,128)(2,1)S(1)} %get-tuple-element.40), channel_id=1, source_target_pairs={{1,2},{3,4},{5,6},{7,8},{9,10},{11,12},{13,14},{15,16},{17,18},{19... | collective-permute-start | bytes 540680 | tf_op jit(solution)/shard_map/ppermute | solution.py:336
  61.2 0.0 copy-done
  61.2 6.8 %collective-permute-done.5.recv_ref = bf16[64,1408]{1,0:T(8,128)(2,1)S(1)} collective-permute-done((bf16[64,1408]{1,0:T(8,128)(2,1)S(1)}, bf16[64,1408]{1,0:T(8,128)(2,1)S(1)}, u32[]{:S(2)}, u32[]{:S(2)}) %collective-permute-start.5) | collective-permute-done | bytes 180256 | tf_op jit(solution)/shard_map/ppermute | solution.py:336
  68.0 0.9 %norm.1 = bf16[64,1280]{1,0:T(8,128)(2,1)S(1)} custom-call(s32[8]{0:T(128)S(1)} %get-tuple-element.24.meta_ref, f32[64,1280]{1,0:T(8,128)S(1)} %get-tuple-element.39.x_ref, bf16[64,1408]{1,0:T(8,128)(2,1)S(1)} %collective-permute-done.5.recv_ref, f32[64,128]{1,0:T(8,128)S(1)} %get-tuple-element.41.mass_ref, f32[64,1280]{1,0:T(8,128)S(1)} %get-tuple-element.42.y_ref, ...), custom_call_target="tpu_custom_call" | custom-call | tf_op jit(solution)/shard_map/norm/pallas_call | solution.py:337
  68.9 2.0 %all_gather.3 = bf16[128,1280]{1,0:T(8,128)(2,1)S(1)} all-gather(bf16[64,1280]{1,0:T(8,128)(2,1)S(1)} %norm.1), channel_id=1, replica_groups=mesh['seq'=16,'feat'=2] {'feat'}, dimensions={0}, use_global_device_ids=true | all-gather | bytes 491520 | tf_op jit(solution)/shard_map/all_gather | solution.py:346
  70.9 0.0 slice-done
  70.9 0.0 slice-done.1
  70.9 0.0 slice-done.2
  71.0 2.6 %convolution_convert_fusion = bf16[128,4096]{1,0:T(8,128)(2,1)} fusion(bf16[128,1280]{1,0:T(8,128)(2,1)S(1)} %all_gather.3, bf16[1280,4096]{1,0:T(8,128)(2,1)S(1)} %bitcast.4), kind=kOutput, calls=%fused_computation | convolution fusion | flops 1342701568 | bytes 11862016 | tf_op jit(solution)/shard_map/dot_general | solution.py:345
  (4 shorter events, 0.0 us)
Async XLA Ops:
  5.8 3.5 %collective-permute-start = (bf16[128,1280]{1,0:T(8,128)(2,1)S(1)}, bf16[128,1280]{1,0:T(8,128)(2,1)S(1)}, u32[]{:S(2)}, u32[]{:S(2)}) collective-permute-start(bf16[128,1280]{1,0:T(8,128)(2,1)S(1)} %get-tuple-element.27), channel_id=1, source_target_pairs={{0,1},{2,3},{4,5},{6,7},{8,9},{10,11},{12,13},{14,15},{16,17},{18,... | collective-permute-start | bytes 983048 | tf_op jit(solution)/shard_map/ppermute | solution.py:301
  9.3 10.2 %collective-permute-start.1 = (bf16[1536,1280]{1,0:T(8,128)(2,1)S(1)}, bf16[1536,1280]{1,0:T(8,128)(2,1)S(1)}, u32[]{:S(2)}, u32[]{:S(2)}) collective-permute-start(bf16[1536,1280]{1,0:T(8,128)(2,1)S(1)} %get-tuple-element.29), channel_id=1, source_target_pairs={{0,1},{1,0},{2,3},{3,2},{4,5},{5,4},{6,7},{7,6},{8,9},{9,8},{10,11... | collective-permute-start | bytes 11796488 | tf_op jit(solution)/shard_map/ppermute | solution.py:303
  9.5 10.0 %collective-permute-start.2 = (bf16[64,1280]{1,0:T(8,128)(2,1)S(1)}, bf16[64,1280]{1,0:T(8,128)(2,1)S(1)}, u32[]{:S(2)}, u32[]{:S(2)}) collective-permute-start(bf16[64,1280]{1,0:T(8,128)(2,1)S(1)} %get-tuple-element.44.after_ref.x_ref), channel_id=1, source_target_pairs={{1,2},{3,4},{5,6},{7,8},{9,10},{11,12},{13,14},{15,16},{17,18},{19... | collective-permute-start | bytes 491528 | tf_op jit(solution)/shard_map/ppermute | solution.py:306
  26.8 8.7 %collective-permute-start.3 = (bf16[64,1408]{1,0:T(8,128)(2,1)S(1)}, bf16[64,1408]{1,0:T(8,128)(2,1)S(1)}, u32[]{:S(2)}, u32[]{:S(2)}) collective-permute-start(bf16[64,1408]{1,0:T(8,128)(2,1)S(1)} %get-tuple-element.32), channel_id=1, source_target_pairs={{1,2},{3,4},{5,6},{7,8},{9,10},{11,12},{13,14},{15,16},{17,18},{19... | collective-permute-start | bytes 540680 | tf_op jit(solution)/shard_map/ppermute | solution.py:336
  35.5 35.4 %slice-start = ((s8[10485760]{0:T(1024)(128)(4,1)}), s8[4194304]{0:T(1024)(128)(4,1)S(1)}, s32[]{:S(2)}) async-start(s8[10485760]{0:T(1024)(128)(4,1)} %bitcast.3), calls=%async_computation | async-start | bytes 8388608
  35.5 35.4 %slice-start.1 = ((s8[10485760]{0:T(1024)(128)(4,1)}), s8[4194304]{0:T(1024)(128)(4,1)S(1)}, s32[]{:S(2)}) async-start(s8[10485760]{0:T(1024)(128)(4,1)} %bitcast.3), calls=%async_computation.1 | async-start | bytes 8388608
  43.0 18.2 %copy-start = (f32[1280]{0:T(1024)S(1)}, f32[1280]{0:T(1024)}, u32[]{:S(2)}) copy-start(f32[1280]{0:T(1024)} %param.8) | copy-start | bytes 15364
  43.0 8.7 %collective-permute-start.4 = (bf16[64,1408]{1,0:T(8,128)(2,1)S(1)}, bf16[64,1408]{1,0:T(8,128)(2,1)S(1)}, u32[]{:S(2)}, u32[]{:S(2)}) collective-permute-start(bf16[64,1408]{1,0:T(8,128)(2,1)S(1)} %get-tuple-element.36), channel_id=1, source_target_pairs={{1,2},{3,4},{5,6},{7,8},{9,10},{11,12},{13,14},{15,16},{17,18},{19... | collective-permute-start | bytes 540680 | tf_op jit(solution)/shard_map/ppermute | solution.py:336
  51.8 19.2 %slice-start.2 = ((s8[10485760]{0:T(1024)(128)(4,1)}), s8[2097152]{0:T(1024)(128)(4,1)S(1)}, s32[]{:S(2)}) async-start(s8[10485760]{0:T(1024)(128)(4,1)} %bitcast.3), calls=%async_computation.2 | async-start | bytes 4194304
  59.3 8.7 %collective-permute-start.5 = (bf16[64,1408]{1,0:T(8,128)(2,1)S(1)}, bf16[64,1408]{1,0:T(8,128)(2,1)S(1)}, u32[]{:S(2)}, u32[]{:S(2)}) collective-permute-start(bf16[64,1408]{1,0:T(8,128)(2,1)S(1)} %get-tuple-element.40), channel_id=1, source_target_pairs={{1,2},{3,4},{5,6},{7,8},{9,10},{11,12},{13,14},{15,16},{17,18},{19... | collective-permute-start | bytes 540680 | tf_op jit(solution)/shard_map/ppermute | solution.py:336
where the time goes:
time: 74.1 us; the launch traced here: 73.6 us
  Pallas kernels  33 us (45%)
  waiting for transfers between devices  21.4 us (29%)
  starting transfers between devices  14.3 us (19%)
  matrix products  2.59 us (3%)
  blocking collectives  2.04 us (3%)
    pallas_call x3, Pallas kernels, on_device(): pl.pallas_call(functools.partial(pool_kernel, iteration == 0), out_shape=...  22.2 us
    ppermute x3, waiting for transfers between devices, on_device(): received = lax.ppermute(send, AXES, across)  18.5 us
    ppermute x3, starting transfers between devices, on_device(): received = lax.ppermute(send, AXES, across)  7.69 us
    pallas_call x1, Pallas kernels, on_device(): pl.pallas_call(seed_kernel, out_shape=(shape(count, width), shape(count,...  5.81 us
    ppermute x1, starting transfers between devices, on_device(): received = lax.ppermute(x, AXES, across)  5.23 us
    pallas_call x1, Pallas kernels, on_device(): pl.pallas_call(load_kernel, out_shape=shape(rows, width), in_specs=[HBM_S...  4.1 us
    dot_general x1, matrix products, on_device(): jnp.dot(lax.all_gather(normed, 'feat', axis=0, tiled=True), proj_weight,...  2.59 us
    ppermute x1, waiting for transfers between devices, on_device(): given = lax.ppermute(give, 'feat', [(0, 1)])  2.22 us
  transfers between devices with their start and end apart: 6, of which 5 were waited for; matrix products, arithmetic and copies ran while one was open for 0% of the time, Pallas kernels for 6%

commit v1 on v0

--- a/solution.py
+++ b/solution.py
@@ -95,9 +95,10 @@
 
     def fetch(k, carry):
         for which, (shot, begin) in enumerate(((index, here), (following, after))):
-            place = jnp.clip(begin + seeds_ref[shot, k] - base, 0, rows - 1)
-            group = pl.multiple_of((place // 8) * 8, 8)
+            place = begin + seeds_ref[shot, k] - base
             slot = pl.multiple_of((which * count + k) * 8, 8)
+            here_too = (place >= 0) & (place < rows)
+            group = pl.multiple_of(jnp.where(here_too, (place // 8) * 8, slot), 8)
             pltpu.make_async_copy(
                 tokens_ref.at[pl.ds(group, 8), :], picked.at[pl.ds(slot, 8), :], pick_sem
             ).start()
@@ -153,7 +154,13 @@
     return jnp.sum(block.astype(F32), axis=1, keepdims=True)
 
 
-def pool_kernel(
+def pool_kernel(first, role, place_ref, meta_ref, *refs):
+    @pl.when(place_ref[0] % 2 == role)
+    def _():
+        pool_body(first, place_ref, meta_ref, *refs)
+
+
+def pool_body(
     first,
     place_ref,
     meta_ref,
@@ -163,6 +170,7 @@
     recv_ref,
     mass_ref,
     y_ref,
+    order_ref,
     send_out,
     x_out,
     mass_out,
@@ -187,7 +195,7 @@
     else:
         mass = mass_ref[:, :1] + total_mass(recv_ref[:, width:])
         joined = x_ref[...] + recv_ref[:, :width].astype(F32)
-        centroids[pl.ds(0, count), :] = (joined / mass).astype(BF16)
+        centroids[pl.ds(0, count), :] = (joined * (1.0 / mass)).astype(BF16)
         centroids[pl.ds(count, count), :] = y_ref[...].astype(BF16)
     sums[...] = jnp.zeros_like(sums)
     masses[...] = jnp.zeros_like(masses)
@@ -235,7 +243,7 @@
     x_sums = sums[pl.ds(0, count), :]
     x_out[...] = x_sums
     mass_out[...] = jnp.broadcast_to(x_mass, mass_out.shape)
-    y_out[...] = sums[pl.ds(count, count), :] / mass[count:]
+    y_out[...] = sums[pl.ds(count, count), :] * (1.0 / mass[count:])
     send_out[:, :width] = x_sums.astype(BF16)
     high = x_mass.astype(BF16).astype(F32)
     middle = (x_mass - high).astype(BF16).astype(F32)
@@ -247,14 +255,23 @@
     send_out[:, width:] = block.astype(BF16)
 
 
-def norm_kernel(meta_ref, x_ref, recv_ref, mass_ref, y_ref, gain_ref, out_ref):
-    width = x_ref.shape[1]
+def norm_kernel(place_ref, meta_ref, gain_ref, *refs):
+    out_ref = refs[-1]
+    width = out_ref.shape[1]
     split = meta_ref[0] != 0
-    mass = mass_ref[:, :1] + total_mass(recv_ref[:, width:])
-    joined = (x_ref[...] + recv_ref[:, :width].astype(F32)) / mass
-    centroid = jnp.where(split, y_ref[...], joined)
-    spread = jnp.sqrt(jnp.mean(centroid * centroid, axis=-1, keepdims=True) + 1e-06)
-    out_ref[...] = (centroid / spread * gain_ref[...]).astype(BF16)
+
+    def finish(x_ref, recv_ref, mass_ref, y_ref):
+        mass = mass_ref[:, :1] + total_mass(recv_ref[:, width:])
+        joined = (x_ref[...] + recv_ref[:, :width].astype(F32)) * (1.0 / mass)
+        centroid = jnp.where(split, y_ref[...], joined)
+        spread = jnp.sqrt(jnp.mean(centroid * centroid, axis=-1, keepdims=True) + 1e-06)
+        out_ref[...] = (centroid * (1.0 / spread) * gain_ref[...]).astype(BF16)
+
+    for role in range(2):
+
+        @pl.when(place_ref[0] % 2 == role)
+        def _():
+            finish(*refs[4 * role : 4 * role + 4])
 
 
 def on_device(tokens, shot_starts, seed_offsets, norm_gain, proj_weight):
@@ -263,8 +280,8 @@
     reach = 3 * rows // 8
     devices = lax.axis_size(AXES)
     place = lax.axis_index(AXES).astype(jnp.int32).reshape(1)
-    across = [(i, i + 1) for i in range(1, devices - 1, 2)]
-    across += [(target, source) for source, target in across]
+    ahead = [(i, i + 1) for i in range(1, devices - 1, 2)]
+    across = ahead + [(target, source) for source, target in ahead]
 
     def shape(*dims, dtype=BF16):
         return jax.ShapeDtypeStruct(dims, dtype)
@@ -314,34 +331,44 @@
         name="load",
     )(far_tokens, x)
     mass = jnp.zeros((count, LANES), F32)
+    ways = [(target, source) for source, target in ahead], ahead
+    states = [(x, received, mass, y), (x, received, mass, y)]
+    order = mass
     for iteration in range(ITERS):
-        send, x, mass, y = pl.pallas_call(
-            functools.partial(pool_kernel, iteration == 0),
-            out_shape=(
-                shape(count, width + LANES),
-                shape(count, width, dtype=F32),
-                shape(count, LANES, dtype=F32),
-                shape(count, width, dtype=F32),
-            ),
-            in_specs=[SMEM_SPEC] * 2 + [VMEM_SPEC] * 6,
-            out_specs=[VMEM_SPEC] * 4,
-            scratch_shapes=[
-                pltpu.VMEM((2 * count, width), BF16),
-                pltpu.VMEM((2 * count, width), F32),
-                pltpu.VMEM((2 * count, LANES), F32),
-            ],
-            compiler_params=pltpu.CompilerParams(vmem_limit_bytes=16 << 20),
-            name="pool",
-        )(place, meta, near_tokens, edge, x, received, mass, y)
-        received = lax.ppermute(send, AXES, across)
+        sends = [None, None]
+        for role in (1, 0) if iteration % 2 == 0 else (0, 1):
+            send, x, mass, y = pl.pallas_call(
+                functools.partial(pool_kernel, iteration == 0, role),
+                out_shape=(
+                    shape(count, width + LANES),
+                    shape(count, width, dtype=F32),
+                    shape(count, LANES, dtype=F32),
+                    shape(count, width, dtype=F32),
+                ),
+                in_specs=[SMEM_SPEC] * 2 + [VMEM_SPEC] * 7,
+                out_specs=[VMEM_SPEC] * 4,
+                scratch_shapes=[
+                    pltpu.VMEM((2 * count, width), BF16),
+                    pltpu.VMEM((2 * count, width), F32),
+                    pltpu.VMEM((2 * count, LANES), F32),
+                ],
+                compiler_params=pltpu.CompilerParams(vmem_limit_bytes=16 << 20),
+                name="pool",
+            )(place, meta, near_tokens, edge, *states[role], order)
+            order = mass
+            sends[role] = lax.ppermute(send, AXES, ways[role])
+            states[role] = (x, None, mass, y)
+        states = [
+            (x, sends[1 - role], mass, y) for role, (x, _, mass, y) in enumerate(states)
+        ]
     normed = pl.pallas_call(
         norm_kernel,
         out_shape=shape(count, width),
-        in_specs=[SMEM_SPEC] + [VMEM_SPEC] * 5,
+        in_specs=[SMEM_SPEC] * 2 + [VMEM_SPEC] * 9,
         out_specs=VMEM_SPEC,
         compiler_params=pltpu.CompilerParams(vmem_limit_bytes=8 << 20),
         name="norm",
-    )(meta, x, received, mass, y, norm_gain[None, :])
+    )(place, meta, norm_gain[None, :], *states[0], *states[1])
     projected = jnp.dot(
         lax.all_gather(normed, "feat", axis=0, tiled=True),
         proj_weight,

time: 74.1 us -> 68.4 us (0.923)
  the two profiles are of different devices: /device:TPU:29 before, /device:TPU:23 now
where the time goes in v1:
time: 68.4 us; the launch traced here: 68.1 us
  Pallas kernels  33.8 us (49%)
  waiting for transfers between devices  16.5 us (24%)
  starting transfers between devices  12.9 us (19%)
  matrix products  2.6 us (4%)
  blocking collectives  2.04 us (3%)
    pallas_call x6, Pallas kernels, on_device(): pl.pallas_call(functools.partial(pool_kernel, iteration == 0, role), out_...  24.3 us
    ppermute x6, waiting for transfers between devices, on_device(): sends[role] = lax.ppermute(send, AXES, ways[role])  13.3 us
    ppermute x6, starting transfers between devices, on_device(): sends[role] = lax.ppermute(send, AXES, ways[role])  8.1 us
    pallas_call x1, Pallas kernels, on_device(): pl.pallas_call(seed_kernel, out_shape=(shape(count, width), shape(count,...  4.48 us
    pallas_call x1, Pallas kernels, on_device(): pl.pallas_call(load_kernel, out_shape=shape(rows, width), in_specs=[HBM_S...  4.1 us
    ppermute x1, starting transfers between devices, on_device(): received = lax.ppermute(x, AXES, across)  3.38 us
    dot_general x1, matrix products, on_device(): jnp.dot(lax.all_gather(normed, 'feat', axis=0, tiled=True), proj_weight,...  2.6 us
    ppermute x1, waiting for transfers between devices, on_device(): given = lax.ppermute(give, 'feat', [(0, 1)])  2.22 us
  transfers between devices with their start and end apart: 9, of which 7 were waited for; matrix products, arithmetic and copies ran while one was open for 0% of the time, Pallas kernels for 31%

profile of v1, /device:TPU:23, one launch (start us, length us, event | category | flops | bytes accessed | tf_op | source)
XLA Modules:
  0.0 68.1 jit_solution(3714670124348054099)
XLA Ops:
  0.0 4.5 %seeds.1 = (bf16[64,1280]{1,0:T(8,128)(2,1)S(1)}, bf16[64,1280]{1,0:T(8,128)(2,1)S(1)}, bf16[128,1280]{1,0:T(8,128)(2,1)S(1)}, bf16[1536,1280]{1,0:T(8,128)(2,1)S(1)}, s32[8]{0:T(128)S(1)}) custom-call(s32[1]{0:T(128)} %bitcast.place_ref, s32[32]{0:T(128)} %starts_hbm.1, s32[32,64]{1,0:T(8,128)} %seeds_hbm.1, bf16[4096,1280]{1,0:T(8,128)(2,1)} %tokens_ref.3), custom_call_target="tpu_custom_call" | custom-call | tf_op jit(solution)/shard_map/seeds/pallas_call | solution.py:290
  4.5 1.3 %collective-permute-start = (bf16[128,1280]{1,0:T(8,128)(2,1)S(1)}, bf16[128,1280]{1,0:T(8,128)(2,1)S(1)}, u32[]{:S(2)}, u32[]{:S(2)}) collective-permute-start(bf16[128,1280]{1,0:T(8,128)(2,1)S(1)} %get-tuple-element.39), channel_id=1, source_target_pairs={{0,1},{2,3},{4,5},{6,7},{8,9},{10,11},{12,13},{14,15},{16,17},{18,... | collective-permute-start | bytes 983048 | tf_op jit(solution)/shard_map/ppermute | solution.py:318
  5.8 2.2 %collective-permute-done = bf16[128,1280]{1,0:T(8,128)(2,1)S(1)} collective-permute-done((bf16[128,1280]{1,0:T(8,128)(2,1)S(1)}, bf16[128,1280]{1,0:T(8,128)(2,1)S(1)}, u32[]{:S(2)}, u32[]{:S(2)}) %collective-permute-start) | collective-permute-done | bytes 327712 | tf_op jit(solution)/shard_map/ppermute | solution.py:318
  8.0 0.1 collective-permute-start.1
  8.2 3.4 %collective-permute-start.2 = (bf16[64,1280]{1,0:T(8,128)(2,1)S(1)}, bf16[64,1280]{1,0:T(8,128)(2,1)S(1)}, u32[]{:S(2)}, u32[]{:S(2)}) collective-permute-start(bf16[64,1280]{1,0:T(8,128)(2,1)S(1)} %get-tuple-element.68.after_ref.refs_2_), channel_id=1, source_target_pairs={{1,2},{3,4},{5,6},{7,8},{9,10},{11,12},{13,14},{15,16},{17,18},{19... | collective-permute-start | bytes 491528 | tf_op jit(solution)/shard_map/ppermute | solution.py:323
  11.6 4.1 %load.1.refs_0_ = bf16[4096,1280]{1,0:T(8,128)(2,1)S(1)} custom-call(bf16[4096,1280]{1,0:T(8,128)(2,1)} %tokens_ref.3, bf16[64,1280]{1,0:T(8,128)(2,1)S(1)} %get-tuple-element.68.after_ref.refs_2_), custom_call_target="tpu_custom_call" | custom-call | tf_op jit(solution)/shard_map/load/pallas_call | solution.py:324
  15.7 0.9 %collective-permute-done.2.refs_3_ = bf16[64,1280]{1,0:T(8,128)(2,1)S(1)} collective-permute-done((bf16[64,1280]{1,0:T(8,128)(2,1)S(1)}, bf16[64,1280]{1,0:T(8,128)(2,1)S(1)}, u32[]{:S(2)}, u32[]{:S(2)}) %collective-permute-start.2) | collective-permute-done | bytes 163872 | tf_op jit(solution)/shard_map/ppermute | solution.py:323
  16.6 0.0 collective-permute-done.1.refs_1_
  16.6 7.3 %pool.6 = (bf16[64,1408]{1,0:T(8,128)(2,1)S(1)}, f32[64,1280]{1,0:T(8,128)S(1)}, f32[64,128]{1,0:T(8,128)S(1)}, f32[64,1280]{1,0:T(8,128)S(1)}) custom-call(s32[1]{0:T(128)} %bitcast.place_ref, s32[8]{0:T(128)S(1)} %get-tuple-element.36.meta_ref, bf16[4096,1280]{1,0:T(8,128)(2,1)S(1)} %load.1.refs_0_, bf16[1536,1280]{1,0:T(8,128)(2,1)S(1)} %collective-permute-done.1.refs_1_, ...), custom_call_target="tpu_custom_call" | custom-call | tf_op jit(solution)/shard_map/pool/pallas_call | solution.py:340
  23.9 1.3 %collective-permute-start.3 = (bf16[64,1408]{1,0:T(8,128)(2,1)S(1)}, bf16[64,1408]{1,0:T(8,128)(2,1)S(1)}, u32[]{:S(2)}, u32[]{:S(2)}) collective-permute-start(bf16[64,1408]{1,0:T(8,128)(2,1)S(1)} %get-tuple-element.45), channel_id=1, source_target_pairs={{1,2},{3,4},{5,6},{7,8},{9,10},{11,12},{13,14},{15,16},{17,18},{19... | collective-permute-start | bytes 540680 | tf_op jit(solution)/shard_map/ppermute | solution.py:359
  25.2 0.6 pool.7
  25.8 1.3 %collective-permute-start.4 = (bf16[64,1408]{1,0:T(8,128)(2,1)S(1)}, bf16[64,1408]{1,0:T(8,128)(2,1)S(1)}, u32[]{:S(2)}, u32[]{:S(2)}) collective-permute-start(bf16[64,1408]{1,0:T(8,128)(2,1)S(1)} %get-tuple-element.50), channel_id=1, source_target_pairs={{2,1},{4,3},{6,5},{8,7},{10,9},{12,11},{14,13},{16,15},{18,17},{20... | collective-permute-start | bytes 540680 | tf_op jit(solution)/shard_map/ppermute | solution.py:359
  27.1 0.5 collective-permute-done.3.refs_3_
  27.7 0.7 %pool.8 = (bf16[64,1408]{1,0:T(8,128)(2,1)S(1)}, f32[64,1280]{1,0:T(8,128)S(1)}, f32[64,128]{1,0:T(8,128)S(1)}, f32[64,1280]{1,0:T(8,128)S(1)}) custom-call(s32[1]{0:T(128)} %bitcast.place_ref, s32[8]{0:T(128)S(1)} %get-tuple-element.36.meta_ref, bf16[4096,1280]{1,0:T(8,128)(2,1)S(1)} %load.1.refs_0_, bf16[1536,1280]{1,0:T(8,128)(2,1)S(1)} %collective-permute-done.1.refs_1_, ...), custom_call_target="tpu_custom_call" | custom-call | tf_op jit(solution)/shard_map/pool/pallas_call | solution.py:340
  28.4 1.3 %collective-permute-start.6 = (bf16[64,1408]{1,0:T(8,128)(2,1)S(1)}, bf16[64,1408]{1,0:T(8,128)(2,1)S(1)}, u32[]{:S(2)}, u32[]{:S(2)}) collective-permute-start(bf16[64,1408]{1,0:T(8,128)(2,1)S(1)} %get-tuple-element.56), channel_id=1, source_target_pairs={{2,1},{4,3},{6,5},{8,7},{10,9},{12,11},{14,13},{16,15},{18,17},{20... | collective-permute-start | bytes 540680 | tf_op jit(solution)/shard_map/ppermute | solution.py:359
  29.7 4.7 %collective-permute-done.4.refs_3_ = bf16[64,1408]{1,0:T(8,128)(2,1)S(1)} collective-permute-done((bf16[64,1408]{1,0:T(8,128)(2,1)S(1)}, bf16[64,1408]{1,0:T(8,128)(2,1)S(1)}, u32[]{:S(2)}, u32[]{:S(2)}) %collective-permute-start.4) | collective-permute-done | bytes 180256 | tf_op jit(solution)/shard_map/ppermute | solution.py:359
  34.4 7.5 %pool.9 = (bf16[64,1408]{1,0:T(8,128)(2,1)S(1)}, f32[64,1280]{1,0:T(8,128)S(1)}, f32[64,128]{1,0:T(8,128)S(1)}, f32[64,1280]{1,0:T(8,128)S(1)}) custom-call(s32[1]{0:T(128)} %bitcast.place_ref, s32[8]{0:T(128)S(1)} %get-tuple-element.36.meta_ref, bf16[4096,1280]{1,0:T(8,128)(2,1)S(1)} %load.1.refs_0_, bf16[1536,1280]{1,0:T(8,128)(2,1)S(1)} %collective-permute-done.1.refs_1_, ...), custom_call_target="tpu_custom_call" | custom-call | tf_op jit(solution)/shard_map/pool/pallas_call | solution.py:340
  41.9 1.5 %collective-permute-start.5 = (bf16[64,1408]{1,0:T(8,128)(2,1)S(1)}, bf16[64,1408]{1,0:T(8,128)(2,1)S(1)}, u32[]{:S(2)}, u32[]{:S(2)}) collective-permute-start(bf16[64,1408]{1,0:T(8,128)(2,1)S(1)} %get-tuple-element.53), channel_id=1, source_target_pairs={{1,2},{3,4},{5,6},{7,8},{9,10},{11,12},{13,14},{15,16},{17,18},{19... | collective-permute-start | bytes 540680 | tf_op jit(solution)/shard_map/ppermute | solution.py:359
  43.4 0.7 %collective-permute-done.6.refs_3_ = bf16[64,1408]{1,0:T(8,128)(2,1)S(1)} collective-permute-done((bf16[64,1408]{1,0:T(8,128)(2,1)S(1)}, bf16[64,1408]{1,0:T(8,128)(2,1)S(1)}, u32[]{:S(2)}, u32[]{:S(2)}) %collective-permute-start.6) | collective-permute-done | bytes 180256 | tf_op jit(solution)/shard_map/ppermute | solution.py:359
  44.2 0.0 slice-start
  44.2 0.0 slice-start.1
  44.2 7.7 %pool.10 = (bf16[64,1408]{1,0:T(8,128)(2,1)S(1)}, f32[64,1280]{1,0:T(8,128)S(1)}, f32[64,128]{1,0:T(8,128)S(1)}, f32[64,1280]{1,0:T(8,128)S(1)}) custom-call(s32[1]{0:T(128)} %bitcast.place_ref, s32[8]{0:T(128)S(1)} %get-tuple-element.36.meta_ref, bf16[4096,1280]{1,0:T(8,128)(2,1)S(1)} %load.1.refs_0_, ...), custom_call_target="tpu_custom_call" | custom-call | tf_op jit(solution)/shard_map/pool/pallas_call | solution.py:340
  51.9 0.0 copy-start
  51.9 1.3 %collective-permute-start.7 = (bf16[64,1408]{1,0:T(8,128)(2,1)S(1)}, bf16[64,1408]{1,0:T(8,128)(2,1)S(1)}, u32[]{:S(2)}, u32[]{:S(2)}) collective-permute-start(bf16[64,1408]{1,0:T(8,128)(2,1)S(1)} %get-tuple-element.61), channel_id=1, source_target_pairs={{1,2},{3,4},{5,6},{7,8},{9,10},{11,12},{13,14},{15,16},{17,18},{19... | collective-permute-start | bytes 540680 | tf_op jit(solution)/shard_map/ppermute | solution.py:359
  53.2 0.0 collective-permute-done.5.refs_3_
  53.2 0.0 slice-start.2
  53.2 0.6 pool.11
  53.8 1.4 %collective-permute-start.8 = (bf16[64,1408]{1,0:T(8,128)(2,1)S(1)}, bf16[64,1408]{1,0:T(8,128)(2,1)S(1)}, u32[]{:S(2)}, u32[]{:S(2)}) collective-permute-start(bf16[64,1408]{1,0:T(8,128)(2,1)S(1)} %get-tuple-element.65), channel_id=1, source_target_pairs={{2,1},{4,3},{6,5},{8,7},{10,9},{12,11},{14,13},{16,15},{18,17},{20... | collective-permute-start | bytes 540680 | tf_op jit(solution)/shard_map/ppermute | solution.py:359
  55.2 0.0 copy-done
  55.2 0.4 collective-permute-done.7.refs_1_
  55.6 6.9 %collective-permute-done.8.refs_5_ = bf16[64,1408]{1,0:T(8,128)(2,1)S(1)} collective-permute-done((bf16[64,1408]{1,0:T(8,128)(2,1)S(1)}, bf16[64,1408]{1,0:T(8,128)(2,1)S(1)}, u32[]{:S(2)}, u32[]{:S(2)}) %collective-permute-start.8) | collective-permute-done | bytes 180256 | tf_op jit(solution)/shard_map/ppermute | solution.py:359
  62.5 0.9 %norm.1 = bf16[64,1280]{1,0:T(8,128)(2,1)S(1)} custom-call(s32[1]{0:T(128)} %bitcast.place_ref, s32[8]{0:T(128)S(1)} %get-tuple-element.36.meta_ref, f32[1,1280]{1,0:T(1,128)S(1)} %broadcast_in_dim.6.gain_ref, f32[64,1280]{1,0:T(8,128)S(1)} %get-tuple-element.60.refs_0_, bf16[64,1408]{1,0:T(8,128)(2,1)S(1)} %collective-permute-done.7.refs_1_, ...), custom_call_target="tpu_custom_call" | custom-call | tf_op jit(solution)/shard_map/norm/pallas_call | solution.py:364
  63.4 2.0 %all_gather.3 = bf16[128,1280]{1,0:T(8,128)(2,1)S(1)} all-gather(bf16[64,1280]{1,0:T(8,128)(2,1)S(1)} %norm.1), channel_id=1, replica_groups=mesh['seq'=16,'feat'=2] {'feat'}, dimensions={0}, use_global_device_ids=true | all-gather | bytes 491520 | tf_op jit(solution)/shard_map/all_gather | solution.py:373
  65.5 0.0 slice-done
  65.5 0.0 slice-done.1
  65.5 0.0 slice-done.2
  65.5 2.6 %convolution_convert_fusion = bf16[128,4096]{1,0:T(8,128)(2,1)} fusion(bf16[128,1280]{1,0:T(8,128)(2,1)S(1)} %all_gather.3, bf16[1280,4096]{1,0:T(8,128)(2,1)S(1)} %bitcast.4), kind=kOutput, calls=%fused_computation | convolution fusion | flops 1342701568 | bytes 11862016 | tf_op jit(solution)/shard_map/dot_general | solution.py:372
  (4 shorter events, 0.0 us)
Async XLA Ops:
  4.5 3.5 %collective-permute-start = (bf16[128,1280]{1,0:T(8,128)(2,1)S(1)}, bf16[128,1280]{1,0:T(8,128)(2,1)S(1)}, u32[]{:S(2)}, u32[]{:S(2)}) collective-permute-start(bf16[128,1280]{1,0:T(8,128)(2,1)S(1)} %get-tuple-element.39), channel_id=1, source_target_pairs={{0,1},{2,3},{4,5},{6,7},{8,9},{10,11},{12,13},{14,15},{16,17},{18,... | collective-permute-start | bytes 983048 | tf_op jit(solution)/shard_map/ppermute | solution.py:318
  8.0 8.6 %collective-permute-start.1 = (bf16[1536,1280]{1,0:T(8,128)(2,1)S(1)}, bf16[1536,1280]{1,0:T(8,128)(2,1)S(1)}, u32[]{:S(2)}, u32[]{:S(2)}) collective-permute-start(bf16[1536,1280]{1,0:T(8,128)(2,1)S(1)} %get-tuple-element.41), channel_id=1, source_target_pairs={{0,1},{1,0},{2,3},{3,2},{4,5},{5,4},{6,7},{7,6},{8,9},{9,8},{10,11... | collective-permute-start | bytes 11796488 | tf_op jit(solution)/shard_map/ppermute | solution.py:320
  8.2 8.4 %collective-permute-start.2 = (bf16[64,1280]{1,0:T(8,128)(2,1)S(1)}, bf16[64,1280]{1,0:T(8,128)(2,1)S(1)}, u32[]{:S(2)}, u32[]{:S(2)}) collective-permute-start(bf16[64,1280]{1,0:T(8,128)(2,1)S(1)} %get-tuple-element.68.after_ref.refs_2_), channel_id=1, source_target_pairs={{1,2},{3,4},{5,6},{7,8},{9,10},{11,12},{13,14},{15,16},{17,18},{19... | collective-permute-start | bytes 491528 | tf_op jit(solution)/shard_map/ppermute | solution.py:323
  23.9 3.7 %collective-permute-start.3 = (bf16[64,1408]{1,0:T(8,128)(2,1)S(1)}, bf16[64,1408]{1,0:T(8,128)(2,1)S(1)}, u32[]{:S(2)}, u32[]{:S(2)}) collective-permute-start(bf16[64,1408]{1,0:T(8,128)(2,1)S(1)} %get-tuple-element.45), channel_id=1, source_target_pairs={{1,2},{3,4},{5,6},{7,8},{9,10},{11,12},{13,14},{15,16},{17,18},{19... | collective-permute-start | bytes 540680 | tf_op jit(solution)/shard_map/ppermute | solution.py:359
  25.8 8.6 %collective-permute-start.4 = (bf16[64,1408]{1,0:T(8,128)(2,1)S(1)}, bf16[64,1408]{1,0:T(8,128)(2,1)S(1)}, u32[]{:S(2)}, u32[]{:S(2)}) collective-permute-start(bf16[64,1408]{1,0:T(8,128)(2,1)S(1)} %get-tuple-element.50), channel_id=1, source_target_pairs={{2,1},{4,3},{6,5},{8,7},{10,9},{12,11},{14,13},{16,15},{18,17},{20... | collective-permute-start | bytes 540680 | tf_op jit(solution)/shard_map/ppermute | solution.py:359
  28.4 15.8 %collective-permute-start.6 = (bf16[64,1408]{1,0:T(8,128)(2,1)S(1)}, bf16[64,1408]{1,0:T(8,128)(2,1)S(1)}, u32[]{:S(2)}, u32[]{:S(2)}) collective-permute-start(bf16[64,1408]{1,0:T(8,128)(2,1)S(1)} %get-tuple-element.56), channel_id=1, source_target_pairs={{2,1},{4,3},{6,5},{8,7},{10,9},{12,11},{14,13},{16,15},{18,17},{20... | collective-permute-start | bytes 540680 | tf_op jit(solution)/shard_map/ppermute | solution.py:359
  41.9 11.3 %collective-permute-start.5 = (bf16[64,1408]{1,0:T(8,128)(2,1)S(1)}, bf16[64,1408]{1,0:T(8,128)(2,1)S(1)}, u32[]{:S(2)}, u32[]{:S(2)}) collective-permute-start(bf16[64,1408]{1,0:T(8,128)(2,1)S(1)} %get-tuple-element.53), channel_id=1, source_target_pairs={{1,2},{3,4},{5,6},{7,8},{9,10},{11,12},{13,14},{15,16},{17,18},{19... | collective-permute-start | bytes 540680 | tf_op jit(solution)/shard_map/ppermute | solution.py:359
  44.2 21.3 %slice-start = ((s8[10485760]{0:T(1024)(128)(4,1)}), s8[4194304]{0:T(1024)(128)(4,1)S(1)}, s32[]{:S(2)}) async-start(s8[10485760]{0:T(1024)(128)(4,1)} %bitcast.3), calls=%async_computation | async-start | bytes 8388608
  44.2 21.3 %slice-start.1 = ((s8[10485760]{0:T(1024)(128)(4,1)}), s8[4194304]{0:T(1024)(128)(4,1)S(1)}, s32[]{:S(2)}) async-start(s8[10485760]{0:T(1024)(128)(4,1)} %bitcast.3), calls=%async_computation.1 | async-start | bytes 8388608
  51.9 3.3 %copy-start = (f32[1280]{0:T(1024)S(1)}, f32[1280]{0:T(1024)}, u32[]{:S(2)}) copy-start(f32[1280]{0:T(1024)} %param.8) | copy-start | bytes 15364
  51.9 3.7 %collective-permute-start.7 = (bf16[64,1408]{1,0:T(8,128)(2,1)S(1)}, bf16[64,1408]{1,0:T(8,128)(2,1)S(1)}, u32[]{:S(2)}, u32[]{:S(2)}) collective-permute-start(bf16[64,1408]{1,0:T(8,128)(2,1)S(1)} %get-tuple-element.61), channel_id=1, source_target_pairs={{1,2},{3,4},{5,6},{7,8},{9,10},{11,12},{13,14},{15,16},{17,18},{19... | collective-permute-start | bytes 540680 | tf_op jit(solution)/shard_map/ppermute | solution.py:359
  53.2 12.3 %slice-start.2 = ((s8[10485760]{0:T(1024)(128)(4,1)}), s8[2097152]{0:T(1024)(128)(4,1)S(1)}, s32[]{:S(2)}) async-start(s8[10485760]{0:T(1024)(128)(4,1)} %bitcast.3), calls=%async_computation.2 | async-start | bytes 4194304
  53.8 8.7 %collective-permute-start.8 = (bf16[64,1408]{1,0:T(8,128)(2,1)S(1)}, bf16[64,1408]{1,0:T(8,128)(2,1)S(1)}, u32[]{:S(2)}, u32[]{:S(2)}) collective-permute-start(bf16[64,1408]{1,0:T(8,128)(2,1)S(1)} %get-tuple-element.65), channel_id=1, source_target_pairs={{2,1},{4,3},{6,5},{8,7},{10,9},{12,11},{14,13},{16,15},{18,17},{20... | collective-permute-start | bytes 540680 | tf_op jit(solution)/shard_map/ppermute | solution.py:359

commit v2 on v0

--- a/solution.py
+++ b/solution.py
@@ -34,7 +34,7 @@
     low = jnp.where(second, here, base)
     high = jnp.where(second, base + rows, after)
     cut = jnp.where(second, after, here)
-    split = jnp.where(second, after < base + rows, here > base)
+    split = jnp.where(second, after <= base + rows, here > base) | (index == 0)
     x_low = jnp.where(split & second, cut, low)
     x_high = jnp.where(split & ~second, cut, high)
     y_low = jnp.where(split, jnp.where(second, low, cut), high)
@@ -95,9 +95,10 @@
 
     def fetch(k, carry):
         for which, (shot, begin) in enumerate(((index, here), (following, after))):
-            place = jnp.clip(begin + seeds_ref[shot, k] - base, 0, rows - 1)
-            group = pl.multiple_of((place // 8) * 8, 8)
+            place = begin + seeds_ref[shot, k] - base
             slot = pl.multiple_of((which * count + k) * 8, 8)
+            here_too = (place >= 0) & (place < rows)
+            group = pl.multiple_of(jnp.where(here_too, (place // 8) * 8, slot), 8)
             pltpu.make_async_copy(
                 tokens_ref.at[pl.ds(group, 8), :], picked.at[pl.ds(slot, 8), :], pick_sem
             ).start()
@@ -122,13 +123,14 @@
         )
         for which, choose in enumerate(choices)
     )
-    ahead = jnp.where(second, after < base + rows, here > base)
+    ahead = jnp.where(second, after <= base + rows, here > base)
     first = jnp.where(ahead, jnp.where(second, tail, 0.0), own)
     first_ref[...] = first.astype(BF16)
     own_ref[...] = own.astype(BF16)
-    shared = later >= base + 2 * rows
-    give_ref[pl.ds(0, count), :] = jnp.where(shared, tail, 0.0).astype(BF16)
-    give_ref[pl.ds(count, count), :] = tail.astype(BF16)
+    shared = later > base + 2 * rows
+    give = jnp.where(second, 0.0, tail)
+    give_ref[pl.ds(0, count), :] = jnp.where(shared, give, 0.0).astype(BF16)
+    give_ref[pl.ds(count, count), :] = give.astype(BF16)
     strip.wait()
 
 
@@ -153,7 +155,15 @@
     return jnp.sum(block.astype(F32), axis=1, keepdims=True)
 
 
-def pool_kernel(
+def pool_kernel(first, ends, devices, place_ref, meta_ref, *refs):
+    at_end = (place_ref[0] == 0) | (place_ref[0] == devices - 1)
+
+    @pl.when(at_end == ends)
+    def _():
+        pool_body(first, place_ref, meta_ref, *refs)
+
+
+def pool_body(
     first,
     place_ref,
     meta_ref,
@@ -163,6 +173,7 @@
     recv_ref,
     mass_ref,
     y_ref,
+    order_ref,
     send_out,
     x_out,
     mass_out,
@@ -181,13 +192,16 @@
     y_range = (meta_ref[3], meta_ref[4])
     scale = math.log2(math.e) / math.sqrt(width)
 
+    occupied = x_range[0] < x_range[1]
     if first:
-        centroids[pl.ds(0, count), :] = x_ref[...] + recv_ref[...]
+        joined = x_ref[...] + recv_ref[...]
+        centroids[pl.ds(0, count), :] = jnp.where(occupied, joined, jnp.zeros_like(joined))
         centroids[pl.ds(count, count), :] = y_ref[...]
     else:
         mass = mass_ref[:, :1] + total_mass(recv_ref[:, width:])
         joined = x_ref[...] + recv_ref[:, :width].astype(F32)
-        centroids[pl.ds(0, count), :] = (joined / mass).astype(BF16)
+        joined = jnp.where(occupied, joined * (1.0 / mass), 0.0)
+        centroids[pl.ds(0, count), :] = joined.astype(BF16)
         centroids[pl.ds(count, count), :] = y_ref[...].astype(BF16)
     sums[...] = jnp.zeros_like(sums)
     masses[...] = jnp.zeros_like(masses)
@@ -235,7 +249,7 @@
     x_sums = sums[pl.ds(0, count), :]
     x_out[...] = x_sums
     mass_out[...] = jnp.broadcast_to(x_mass, mass_out.shape)
-    y_out[...] = sums[pl.ds(count, count), :] / mass[count:]
+    y_out[...] = sums[pl.ds(count, count), :] * (1.0 / mass[count:])
     send_out[:, :width] = x_sums.astype(BF16)
     high = x_mass.astype(BF16).astype(F32)
     middle = (x_mass - high).astype(BF16).astype(F32)
@@ -247,14 +261,18 @@
     send_out[:, width:] = block.astype(BF16)
 
 
-def norm_kernel(meta_ref, x_ref, recv_ref, mass_ref, y_ref, gain_ref, out_ref):
+def norm_kernel(
+    devices, place_ref, meta_ref, x_ref, recv_ref, mass_ref, y_ref, y_end_ref, gain_ref, out_ref
+):
     width = x_ref.shape[1]
     split = meta_ref[0] != 0
+    at_end = (place_ref[0] == 0) | (place_ref[0] == devices - 1)
     mass = mass_ref[:, :1] + total_mass(recv_ref[:, width:])
-    joined = (x_ref[...] + recv_ref[:, :width].astype(F32)) / mass
-    centroid = jnp.where(split, y_ref[...], joined)
+    joined = (x_ref[...] + recv_ref[:, :width].astype(F32)) * (1.0 / mass)
+    own = jnp.where(at_end, y_end_ref[...], y_ref[...])
+    centroid = jnp.where(split, own, joined)
     spread = jnp.sqrt(jnp.mean(centroid * centroid, axis=-1, keepdims=True) + 1e-06)
-    out_ref[...] = (centroid / spread * gain_ref[...]).astype(BF16)
+    out_ref[...] = (centroid * (1.0 / spread) * gain_ref[...]).astype(BF16)
 
 
 def on_device(tokens, shot_starts, seed_offsets, norm_gain, proj_weight):
@@ -265,6 +283,8 @@
     place = lax.axis_index(AXES).astype(jnp.int32).reshape(1)
     across = [(i, i + 1) for i in range(1, devices - 1, 2)]
     across += [(target, source) for source, target in across]
+    across += [(0, devices - 1), (devices - 1, 0)]
+    pair = [(0, 1), (1, 0)]
 
     def shape(*dims, dtype=BF16):
         return jax.ShapeDtypeStruct(dims, dtype)
@@ -298,9 +318,9 @@
         pltpu.with_memory_space_constraint(seed_offsets, pltpu.HBM),
         far_tokens,
     )
-    given = lax.ppermute(give, "feat", [(0, 1)])
+    given = lax.ppermute(give, "feat", pair)
     edge, given = lax.optimization_barrier((edge, given))
-    edge = lax.ppermute(edge, "feat", [(0, 1), (1, 0)])
+    edge = lax.ppermute(edge, "feat", pair)
     x = first + given[:count]
     y = own + given[count:]
     received = lax.ppermute(x, AXES, across)
@@ -314,16 +334,17 @@
         name="load",
     )(far_tokens, x)
     mass = jnp.zeros((count, LANES), F32)
-    for iteration in range(ITERS):
-        send, x, mass, y = pl.pallas_call(
-            functools.partial(pool_kernel, iteration == 0),
+
+    def pool(iteration, ends, *state):
+        return pl.pallas_call(
+            functools.partial(pool_kernel, iteration == 0, ends, devices),
             out_shape=(
                 shape(count, width + LANES),
                 shape(count, width, dtype=F32),
                 shape(count, LANES, dtype=F32),
                 shape(count, width, dtype=F32),
             ),
-            in_specs=[SMEM_SPEC] * 2 + [VMEM_SPEC] * 6,
+            in_specs=[SMEM_SPEC] * 2 + [VMEM_SPEC] * 7,
             out_specs=[VMEM_SPEC] * 4,
             scratch_shapes=[
                 pltpu.VMEM((2 * count, width), BF16),
@@ -331,17 +352,23 @@
                 pltpu.VMEM((2 * count, LANES), F32),
             ],
             compiler_params=pltpu.CompilerParams(vmem_limit_bytes=16 << 20),
-            name="pool",
-        )(place, meta, near_tokens, edge, x, received, mass, y)
+            name="ends" if ends else "pool",
+        )(place, meta, near_tokens, edge, *state)
+
+    y_end = y
+    for iteration in range(ITERS):
+        before = (x, received, mass)
+        send, x, mass, y = pool(iteration, False, *before, y, y_end)
         received = lax.ppermute(send, AXES, across)
+        y_end = pool(iteration, True, *before, y_end, mass)[3]
     normed = pl.pallas_call(
-        norm_kernel,
+        functools.partial(norm_kernel, devices),
         out_shape=shape(count, width),
-        in_specs=[SMEM_SPEC] + [VMEM_SPEC] * 5,
+        in_specs=[SMEM_SPEC] * 2 + [VMEM_SPEC] * 6,
         out_specs=VMEM_SPEC,
         compiler_params=pltpu.CompilerParams(vmem_limit_bytes=8 << 20),
         name="norm",
-    )(meta, x, received, mass, y, norm_gain[None, :])
+    )(place, meta, x, received, mass, y, y_end, norm_gain[None, :])
     projected = jnp.dot(
         lax.all_gather(normed, "feat", axis=0, tiled=True),
         proj_weight,

time: 74.1 us -> 62.8 us (0.85)
  starting transfers between devices: 14.3 us -> 3.77 us
  waiting for transfers between devices: 21.4 us -> 18 us
  Pallas kernels: 33 us -> 36.1 us
    ppermute x3, starting transfers between devices: 7.69 us -> 1.4 us  [on_device(): received = lax.ppermute(send, AXES, across)]
    pallas_call x4 -> x7, Pallas kernels: 23.1 us -> 27.5 us  [the longest x6 26.7 us: pool(): pl.pallas_call(functools.partial(pool_kernel, iteration == 0, ends, devic...]
    ppermute x1, starting transfers between devices: 5.23 us -> 1.3 us  [on_device(): received = lax.ppermute(x, AXES, across)]
    ppermute x3, waiting for transfers between devices: 18.5 us -> 15.3 us  [on_device(): received = lax.ppermute(send, AXES, across)]
    pallas_call x1, Pallas kernels: 5.81 us -> 4.48 us  [on_device(): pl.pallas_call(seed_kernel, out_shape=(shape(count, width), shape(count,...]
    ppermute x2, waiting for transfers between devices: 2.23 us -> 1.26 us  [the longest x1 1.26 us: on_device(): given = lax.ppermute(give, 'feat', pair)]
    ppermute x1, waiting for transfers between devices: 0.64 us -> 1.4 us  [on_device(): received = lax.ppermute(x, AXES, across)]
  transfers between devices with their start and end apart: 6 -> 6, of which waited for: 5 -> 5; matrix products, arithmetic and copies ran while one was open for 0% -> 0% of each run, Pallas kernels for 6% -> 13%
where the time goes in v2:
time: 62.8 us; the launch traced here: 62.6 us
  Pallas kernels  36.1 us (57%)
  waiting for transfers between devices  18 us (29%)
  starting transfers between devices  3.77 us (6%)
  matrix products  2.59 us (4%)
  blocking collectives  2.04 us (3%)
    pallas_call x6, Pallas kernels, pool(): pl.pallas_call(functools.partial(pool_kernel, iteration == 0, ends, devic...  26.7 us
    ppermute x3, waiting for transfers between devices, on_device(): received = lax.ppermute(send, AXES, across)  15.3 us
    pallas_call x1, Pallas kernels, on_device(): pl.pallas_call(seed_kernel, out_shape=(shape(count, width), shape(count,...  4.48 us
    pallas_call x1, Pallas kernels, on_device(): pl.pallas_call(load_kernel, out_shape=shape(rows, width), in_specs=[HBM_S...  4.1 us
    dot_general x1, matrix products, on_device(): jnp.dot(lax.all_gather(normed, 'feat', axis=0, tiled=True), proj_weight,...  2.59 us
    all_gather x1, blocking collectives, on_device(): lax.all_gather(normed, 'feat', axis=0, tiled=True)  2.04 us
    ppermute x3, starting transfers between devices, on_device(): received = lax.ppermute(send, AXES, across)  1.4 us
    ppermute x1, waiting for transfers between devices, on_device(): received = lax.ppermute(x, AXES, across)  1.4 us
  transfers between devices with their start and end apart: 6, of which 5 were waited for; matrix products, arithmetic and copies ran while one was open for 0% of the time, Pallas kernels for 13%

profile of v2, /device:TPU:29, one launch (start us, length us, event | category | flops | bytes accessed | tf_op | source)
XLA Modules:
  0.0 62.6 jit_solution(2510035204191811631)
XLA Ops:
  0.0 4.5 %seeds.1 = (bf16[64,1280]{1,0:T(8,128)(2,1)S(1)}, bf16[64,1280]{1,0:T(8,128)(2,1)S(1)}, bf16[128,1280]{1,0:T(8,128)(2,1)S(1)}, bf16[1536,1280]{1,0:T(8,128)(2,1)S(1)}, s32[8]{0:T(128)S(1)}) custom-call(s32[1]{0:T(128)} %bitcast.place_ref, s32[32]{0:T(128)} %starts_hbm.1, s32[32,64]{1,0:T(8,128)} %seeds_hbm.1, bf16[4096,1280]{1,0:T(8,128)(2,1)} %tokens_ref.3), custom_call_target="tpu_custom_call" | custom-call | tf_op jit(solution)/shard_map/seeds/pallas_call | solution.py:293
  4.5 0.7 %collective-permute-start = (bf16[128,1280]{1,0:T(8,128)(2,1)S(1)}, bf16[128,1280]{1,0:T(8,128)(2,1)S(1)}, u32[]{:S(2)}, u32[]{:S(2)}) collective-permute-start(bf16[128,1280]{1,0:T(8,128)(2,1)S(1)} %get-tuple-element.30), channel_id=1, source_target_pairs={{0,1},{1,0},{2,3},{3,2},{4,5},{5,4},{6,7},{7,6},{8,9},{9,8},{10,11... | collective-permute-start | bytes 983048 | tf_op jit(solution)/shard_map/ppermute | solution.py:321
  5.2 1.3 %collective-permute-done = bf16[128,1280]{1,0:T(8,128)(2,1)S(1)} collective-permute-done((bf16[128,1280]{1,0:T(8,128)(2,1)S(1)}, bf16[128,1280]{1,0:T(8,128)(2,1)S(1)}, u32[]{:S(2)}, u32[]{:S(2)}) %collective-permute-start) | collective-permute-done | bytes 327712 | tf_op jit(solution)/shard_map/ppermute | solution.py:321
  6.4 0.4 collective-permute-start.1
  6.9 1.3 %collective-permute-start.2 = (bf16[64,1280]{1,0:T(8,128)(2,1)S(1)}, bf16[64,1280]{1,0:T(8,128)(2,1)S(1)}, u32[]{:S(2)}, u32[]{:S(2)}) collective-permute-start(bf16[64,1280]{1,0:T(8,128)(2,1)S(1)} %get-tuple-element.50.after_ref.refs_2_), channel_id=1, source_target_pairs={{1,2},{3,4},{5,6},{7,8},{9,10},{11,12},{13,14},{15,16},{17,18},{19... | collective-permute-start | bytes 491528 | tf_op jit(solution)/shard_map/ppermute | solution.py:326
  8.2 4.1 %load.1.refs_0_ = bf16[4096,1280]{1,0:T(8,128)(2,1)S(1)} custom-call(bf16[4096,1280]{1,0:T(8,128)(2,1)} %tokens_ref.3, bf16[64,1280]{1,0:T(8,128)(2,1)S(1)} %get-tuple-element.50.after_ref.refs_2_), custom_call_target="tpu_custom_call" | custom-call | tf_op jit(solution)/shard_map/load/pallas_call | solution.py:327
  12.3 1.4 %collective-permute-done.2.refs_3_ = bf16[64,1280]{1,0:T(8,128)(2,1)S(1)} collective-permute-done((bf16[64,1280]{1,0:T(8,128)(2,1)S(1)}, bf16[64,1280]{1,0:T(8,128)(2,1)S(1)}, u32[]{:S(2)}, u32[]{:S(2)}) %collective-permute-start.2) | collective-permute-done | bytes 163872 | tf_op jit(solution)/shard_map/ppermute | solution.py:326
  13.7 0.0 collective-permute-done.1.refs_1_
  13.7 7.3 %pool.3 = (bf16[64,1408]{1,0:T(8,128)(2,1)S(1)}, f32[64,1280]{1,0:T(8,128)S(1)}, f32[64,128]{1,0:T(8,128)S(1)}, f32[64,1280]{1,0:T(8,128)S(1)}) custom-call(s32[1]{0:T(128)} %bitcast.place_ref, s32[8]{0:T(128)S(1)} %get-tuple-element.27.meta_ref, bf16[4096,1280]{1,0:T(8,128)(2,1)S(1)} %load.1.refs_0_, bf16[1536,1280]{1,0:T(8,128)(2,1)S(1)} %collective-permute-done.1.refs_1_, ...), custom_call_target="tpu_custom_call" | custom-call | tf_op jit(solution)/shard_map/pool/pallas_call | solution.py:339
  21.0 1.1 %collective-permute-start.3 = (bf16[64,1408]{1,0:T(8,128)(2,1)S(1)}, bf16[64,1408]{1,0:T(8,128)(2,1)S(1)}, u32[]{:S(2)}, u32[]{:S(2)}) collective-permute-start(bf16[64,1408]{1,0:T(8,128)(2,1)S(1)} %get-tuple-element.35), channel_id=1, source_target_pairs={{1,2},{3,4},{5,6},{7,8},{9,10},{11,12},{13,14},{15,16},{17,18},{19... | collective-permute-start | bytes 540680 | tf_op jit(solution)/shard_map/ppermute | solution.py:362
  22.1 1.3 %ends.3 = (bf16[64,1408]{1,0:T(8,128)(2,1)}, f32[64,1280]{1,0:T(8,128)}, f32[64,128]{1,0:T(8,128)}, f32[64,1280]{1,0:T(8,128)S(1)}) custom-call(s32[1]{0:T(128)} %bitcast.place_ref, s32[8]{0:T(128)S(1)} %get-tuple-element.27.meta_ref, bf16[4096,1280]{1,0:T(8,128)(2,1)S(1)} %load.1.refs_0_, bf16[1536,1280]{1,0:T(8,128)(2,1)S(1)} %collective-permute-done.1.refs_1_, ...), custom_call_target="tpu_custom_call" | custom-call | tf_op jit(solution)/shard_map/ends/pallas_call | solution.py:339
  23.4 4.5 %collective-permute-done.3.refs_3_ = bf16[64,1408]{1,0:T(8,128)(2,1)S(1)} collective-permute-done((bf16[64,1408]{1,0:T(8,128)(2,1)S(1)}, bf16[64,1408]{1,0:T(8,128)(2,1)S(1)}, u32[]{:S(2)}, u32[]{:S(2)}) %collective-permute-start.3) | collective-permute-done | bytes 180256 | tf_op jit(solution)/shard_map/ppermute | solution.py:362
  27.9 7.7 %pool.4 = (bf16[64,1408]{1,0:T(8,128)(2,1)S(1)}, f32[64,1280]{1,0:T(8,128)S(1)}, f32[64,128]{1,0:T(8,128)S(1)}, f32[64,1280]{1,0:T(8,128)S(1)}) custom-call(s32[1]{0:T(128)} %bitcast.place_ref, s32[8]{0:T(128)S(1)} %get-tuple-element.27.meta_ref, bf16[4096,1280]{1,0:T(8,128)(2,1)S(1)} %load.1.refs_0_, bf16[1536,1280]{1,0:T(8,128)(2,1)S(1)} %collective-permute-done.1.refs_1_, ...), custom_call_target="tpu_custom_call" | custom-call | tf_op jit(solution)/shard_map/pool/pallas_call | solution.py:339
  35.6 0.2 collective-permute-start.4
  35.8 1.3 %ends.4 = (bf16[64,1408]{1,0:T(8,128)(2,1)}, f32[64,1280]{1,0:T(8,128)}, f32[64,128]{1,0:T(8,128)}, f32[64,1280]{1,0:T(8,128)S(1)}) custom-call(s32[1]{0:T(128)} %bitcast.place_ref, s32[8]{0:T(128)S(1)} %get-tuple-element.27.meta_ref, bf16[4096,1280]{1,0:T(8,128)(2,1)S(1)} %load.1.refs_0_, bf16[1536,1280]{1,0:T(8,128)(2,1)S(1)} %collective-permute-done.1.refs_1_, ...), custom_call_target="tpu_custom_call" | custom-call | tf_op jit(solution)/shard_map/ends/pallas_call | solution.py:339
  37.1 0.0 copy-start
  37.1 5.4 %collective-permute-done.4.refs_3_ = bf16[64,1408]{1,0:T(8,128)(2,1)S(1)} collective-permute-done((bf16[64,1408]{1,0:T(8,128)(2,1)S(1)}, bf16[64,1408]{1,0:T(8,128)(2,1)S(1)}, u32[]{:S(2)}, u32[]{:S(2)}) %collective-permute-start.4) | collective-permute-done | bytes 180256 | tf_op jit(solution)/shard_map/ppermute | solution.py:362
  42.5 0.0 slice-start
  42.5 0.0 slice-start.1
  42.5 7.7 %pool.5 = (bf16[64,1408]{1,0:T(8,128)(2,1)S(1)}, f32[64,1280]{1,0:T(8,128)S(1)}, f32[64,128]{1,0:T(8,128)S(1)}, f32[64,1280]{1,0:T(8,128)S(1)}) custom-call(s32[1]{0:T(128)} %bitcast.place_ref, s32[8]{0:T(128)S(1)} %get-tuple-element.27.meta_ref, bf16[4096,1280]{1,0:T(8,128)(2,1)S(1)} %load.1.refs_0_, bf16[1536,1280]{1,0:T(8,128)(2,1)S(1)} %collective-permute-done.1.refs_1_, ...), custom_call_target="tpu_custom_call" | custom-call | tf_op jit(solution)/shard_map/pool/pallas_call | solution.py:339
  50.2 0.1 collective-permute-start.5
  50.3 0.0 copy-done
  50.3 0.0 slice-start.2
  50.3 1.3 %ends.5 = (bf16[64,1408]{1,0:T(8,128)(2,1)}, f32[64,1280]{1,0:T(8,128)}, f32[64,128]{1,0:T(8,128)}, f32[64,1280]{1,0:T(8,128)S(1)}) custom-call(s32[1]{0:T(128)} %bitcast.place_ref, s32[8]{0:T(128)S(1)} %get-tuple-element.27.meta_ref, bf16[4096,1280]{1,0:T(8,128)(2,1)S(1)} %load.1.refs_0_, bf16[1536,1280]{1,0:T(8,128)(2,1)S(1)} %collective-permute-done.1.refs_1_, ...), custom_call_target="tpu_custom_call" | custom-call | tf_op jit(solution)/shard_map/ends/pallas_call | solution.py:339
  51.7 5.5 %collective-permute-done.5.recv_ref = bf16[64,1408]{1,0:T(8,128)(2,1)S(1)} collective-permute-done((bf16[64,1408]{1,0:T(8,128)(2,1)S(1)}, bf16[64,1408]{1,0:T(8,128)(2,1)S(1)}, u32[]{:S(2)}, u32[]{:S(2)}) %collective-permute-start.5) | collective-permute-done | bytes 180256 | tf_op jit(solution)/shard_map/ppermute | solution.py:362
  57.1 0.9 %norm.1 = bf16[64,1280]{1,0:T(8,128)(2,1)S(1)} custom-call(s32[1]{0:T(128)} %bitcast.place_ref, s32[8]{0:T(128)S(1)} %get-tuple-element.27.meta_ref, f32[64,1280]{1,0:T(8,128)S(1)} %get-tuple-element.44.x_ref, bf16[64,1408]{1,0:T(8,128)(2,1)S(1)} %collective-permute-done.5.recv_ref, f32[64,128]{1,0:T(8,128)S(1)} %get-tuple-element.46.refs_6_.mass_ref, ...), custom_call_target="tpu_custom_call" | custom-call | tf_op jit(solution)/shard_map/norm/pallas_call | solution.py:364
  58.0 2.0 %all_gather.3 = bf16[128,1280]{1,0:T(8,128)(2,1)S(1)} all-gather(bf16[64,1280]{1,0:T(8,128)(2,1)S(1)} %norm.1), channel_id=1, replica_groups=mesh['seq'=16,'feat'=2] {'feat'}, dimensions={0}, use_global_device_ids=true | all-gather | bytes 491520 | tf_op jit(solution)/shard_map/all_gather | solution.py:373
  60.0 0.0 slice-done
  60.0 0.0 slice-done.1
  60.0 0.0 slice-done.2
  60.1 2.6 %convolution_convert_fusion = bf16[128,4096]{1,0:T(8,128)(2,1)} fusion(bf16[128,1280]{1,0:T(8,128)(2,1)S(1)} %all_gather.3, bf16[1280,4096]{1,0:T(8,128)(2,1)S(1)} %bitcast.4), kind=kOutput, calls=%fused_computation | convolution fusion | flops 1342701568 | bytes 11862016 | tf_op jit(solution)/shard_map/dot_general | solution.py:372
  (4 shorter events, 0.0 us)
Async XLA Ops:
  4.5 2.0 %collective-permute-start = (bf16[128,1280]{1,0:T(8,128)(2,1)S(1)}, bf16[128,1280]{1,0:T(8,128)(2,1)S(1)}, u32[]{:S(2)}, u32[]{:S(2)}) collective-permute-start(bf16[128,1280]{1,0:T(8,128)(2,1)S(1)} %get-tuple-element.30), channel_id=1, source_target_pairs={{0,1},{1,0},{2,3},{3,2},{4,5},{5,4},{6,7},{7,6},{8,9},{9,8},{10,11... | collective-permute-start | bytes 983048 | tf_op jit(solution)/shard_map/ppermute | solution.py:321
  6.4 7.2 %collective-permute-start.1 = (bf16[1536,1280]{1,0:T(8,128)(2,1)S(1)}, bf16[1536,1280]{1,0:T(8,128)(2,1)S(1)}, u32[]{:S(2)}, u32[]{:S(2)}) collective-permute-start(bf16[1536,1280]{1,0:T(8,128)(2,1)S(1)} %get-tuple-element.32), channel_id=1, source_target_pairs={{0,1},{1,0},{2,3},{3,2},{4,5},{5,4},{6,7},{7,6},{8,9},{9,8},{10,11... | collective-permute-start | bytes 11796488 | tf_op jit(solution)/shard_map/ppermute | solution.py:323
  6.9 6.8 %collective-permute-start.2 = (bf16[64,1280]{1,0:T(8,128)(2,1)S(1)}, bf16[64,1280]{1,0:T(8,128)(2,1)S(1)}, u32[]{:S(2)}, u32[]{:S(2)}) collective-permute-start(bf16[64,1280]{1,0:T(8,128)(2,1)S(1)} %get-tuple-element.50.after_ref.refs_2_), channel_id=1, source_target_pairs={{1,2},{3,4},{5,6},{7,8},{9,10},{11,12},{13,14},{15,16},{17,18},{19... | collective-permute-start | bytes 491528 | tf_op jit(solution)/shard_map/ppermute | solution.py:326
  21.0 6.9 %collective-permute-start.3 = (bf16[64,1408]{1,0:T(8,128)(2,1)S(1)}, bf16[64,1408]{1,0:T(8,128)(2,1)S(1)}, u32[]{:S(2)}, u32[]{:S(2)}) collective-permute-start(bf16[64,1408]{1,0:T(8,128)(2,1)S(1)} %get-tuple-element.35), channel_id=1, source_target_pairs={{1,2},{3,4},{5,6},{7,8},{9,10},{11,12},{13,14},{15,16},{17,18},{19... | collective-permute-start | bytes 540680 | tf_op jit(solution)/shard_map/ppermute | solution.py:362
  35.6 6.9 %collective-permute-start.4 = (bf16[64,1408]{1,0:T(8,128)(2,1)S(1)}, bf16[64,1408]{1,0:T(8,128)(2,1)S(1)}, u32[]{:S(2)}, u32[]{:S(2)}) collective-permute-start(bf16[64,1408]{1,0:T(8,128)(2,1)S(1)} %get-tuple-element.40), channel_id=1, source_target_pairs={{1,2},{3,4},{5,6},{7,8},{9,10},{11,12},{13,14},{15,16},{17,18},{19... | collective-permute-start | bytes 540680 | tf_op jit(solution)/shard_map/ppermute | solution.py:362
  37.1 13.2 %copy-start = (f32[1280]{0:T(1024)S(1)}, f32[1280]{0:T(1024)}, u32[]{:S(2)}) copy-start(f32[1280]{0:T(1024)} %param.8) | copy-start | bytes 15364
  42.5 17.6 %slice-start = ((s8[10485760]{0:T(1024)(128)(4,1)}), s8[4194304]{0:T(1024)(128)(4,1)S(1)}, s32[]{:S(2)}) async-start(s8[10485760]{0:T(1024)(128)(4,1)} %bitcast.3), calls=%async_computation | async-start | bytes 8388608
  42.5 17.6 %slice-start.1 = ((s8[10485760]{0:T(1024)(128)(4,1)}), s8[4194304]{0:T(1024)(128)(4,1)S(1)}, s32[]{:S(2)}) async-start(s8[10485760]{0:T(1024)(128)(4,1)} %bitcast.3), calls=%async_computation.1 | async-start | bytes 8388608
  50.2 6.9 %collective-permute-start.5 = (bf16[64,1408]{1,0:T(8,128)(2,1)S(1)}, bf16[64,1408]{1,0:T(8,128)(2,1)S(1)}, u32[]{:S(2)}, u32[]{:S(2)}) collective-permute-start(bf16[64,1408]{1,0:T(8,128)(2,1)S(1)} %get-tuple-element.45), channel_id=1, source_target_pairs={{1,2},{3,4},{5,6},{7,8},{9,10},{11,12},{13,14},{15,16},{17,18},{19... | collective-permute-start | bytes 540680 | tf_op jit(solution)/shard_map/ppermute | solution.py:362
  50.3 9.7 %slice-start.2 = ((s8[10485760]{0:T(1024)(128)(4,1)}), s8[2097152]{0:T(1024)(128)(4,1)S(1)}, s32[]{:S(2)}) async-start(s8[10485760]{0:T(1024)(128)(4,1)} %bitcast.3), calls=%async_computation.2 | async-start | bytes 4194304

commit v3 on v2

v3 whole, which is shorter than its diff:
```python
import functools
import math

import jax
import jax.numpy as jnp
from jax import lax
from jax.experimental import pallas as pl
from jax.experimental.pallas import tpu as pltpu
from jax.sharding import PartitionSpec as P

ITERS = 3
AXES = ("seq", "feat")
LANES = 128
TILE = 512
F32 = jnp.float32
BF16 = jnp.bfloat16
VMEM_SPEC = pl.BlockSpec(memory_space=pltpu.VMEM)
HBM_SPEC = pl.BlockSpec(memory_space=pltpu.HBM)
X_LOW, X_HIGH, Y_LOW, Y_HIGH, EDGE, SPLIT, OCCUPIED, UNUSED = range(8)


def start_of(starts_ref, shot, shots, total):
    first = starts_ref[jnp.minimum(shot, shots - 1)]
    return jnp.where(shot >= shots, total, first)


def column_of(row):
    n = row.shape[1]
    diagonal = lax.broadcasted_iota(jnp.int32, (n, n), 0) == lax.broadcasted_iota(
        jnp.int32, (n, n), 1
    )
    spread = jnp.where(diagonal, jnp.broadcast_to(row, (n, n)), 0)
    return jnp.sum(spread, axis=1, keepdims=True)


def seed_kernel(
    reach,
    starts_hbm,
    seeds_hbm,
    tokens_ref,
    first_ref,
    own_ref,
    tail_ref,
    share_ref,
    meta_ref,
    starts_ref,
    seeds_ref,
    seed_rows_ref,
    picked,
    index_sems,
    pick_sem,
):
    rows, width = tokens_ref.shape
    shots, count = seeds_ref.shape
    total = shots * rows
    index = lax.axis_index(AXES)
    second = index % 2 == 1
    base = index * rows
    indices = [
        pltpu.make_async_copy(starts_hbm, starts_ref, index_sems.at[0]),
        pltpu.make_async_copy(seeds_hbm, seeds_ref, index_sems.at[1]),
        pltpu.make_async_copy(seeds_hbm, seed_rows_ref, index_sems.at[2]),
    ]
    for copy in indices:
        copy.start()
    for copy in indices:
        copy.wait()
    following = jnp.minimum(index + 1, shots - 1)
    here = start_of(starts_ref, index, shots, total)
    after = start_of(starts_ref, index + 1, shots, total)

    def fetch(k, carry):
        for which, (shot, begin) in enumerate(((index, here), (following, after))):
            place = begin + seeds_ref[shot, k] - base
            slot = pl.multiple_of((which * count + k) * 8, 8)
            here_too = (place >= 0) & (place < rows)
            group = pl.multiple_of(jnp.where(here_too, (place // 8) * 8, slot), 8)
            pltpu.make_async_copy(
                tokens_ref.at[pl.ds(group, 8), :], picked.at[pl.ds(slot, 8), :], pick_sem
            ).start()
        return carry

    lax.fori_loop(0, count, fetch, 0, unroll=8)

    low = jnp.where(second, here - base, 0)
    high = jnp.where(second, rows, after - base)
    cut = jnp.where(second, after - base, here - base)
    split = jnp.where(second, after <= base + rows, here > base) | (index == 0)
    x_low = jnp.where(split & second, cut, low)
    x_high = jnp.where(split & ~second, cut, high)
    y_low = jnp.where(split, jnp.where(second, low, cut), high)
    y_high = jnp.where(split, jnp.where(second, cut, high), high)
    table = {
        X_LOW: x_low,
        X_HIGH: x_high,
        Y_LOW: y_low,
        Y_HIGH: y_high,
        EDGE: jnp.where(second, -reach, rows),
        SPLIT: split.astype(jnp.int32),
        OCCUPIED: (x_low < x_high).astype(jnp.int32),
        UNUSED: 0,
    }
    for row, value in table.items():
        meta_ref[pl.ds(row, 1), :] = jnp.full((1, width), value, jnp.int32)
    lends = jnp.where(second, 1.0, 0.0)
    row = lax.broadcasted_iota(jnp.int32, share_ref.shape, 0)
    share_ref[...] = jnp.where(row == 0, jnp.where(split, 0.0, lends), lends).astype(BF16)

    choices = []
    for shot, begin in ((index, here), (following, after)):
        place = column_of(seed_rows_ref[pl.ds(shot, 1), :]) + (begin - base)
        valid = (place >= 0) & (place < rows)
        target = lax.broadcasted_iota(jnp.int32, (count, 1), 0) * 8 + place % 8
        lane = lax.broadcasted_iota(jnp.int32, (count, 8 * count), 1)
        choices.append(jnp.where(valid & (lane == target), 1.0, 0.0).astype(BF16))
    pltpu.make_async_copy(tokens_ref.at[pl.ds(0, 16 * count), :], picked, pick_sem).wait()
    own, tail = (
        jnp.dot(
            choose,
            picked[pl.ds(which * 8 * count, 8 * count), :],
            preferred_element_type=F32,
        )
        for which, choose in enumerate(choices)
    )
    first_ref[...] = jnp.where(split, jnp.where(second, tail, 0.0), own).astype(BF16)
    own_ref[...] = own.astype(BF16)
    tail_ref[...] = tail.astype(BF16)


def copy_pieces(tokens_ref, low, out_ref, sems):
    pieces = sems.shape[0]
    piece = out_ref.shape[0] // pieces
    copies = [
        pltpu.make_async_copy(
            tokens_ref.at[pl.ds(pl.multiple_of(low + i * piece, 8), piece), :],
            out_ref.at[pl.ds(i * piece, piece), :],
            sems.at[i],
        )
        for i in range(pieces)
    ]
    for copy in copies:
        copy.start()
    for copy in copies:
        copy.wait()


def strip_kernel(tokens_ref, order_ref, out_ref, sems):
    second = lax.axis_index(AXES) % 2 == 1
    low = jnp.where(second, 0, tokens_ref.shape[0] - out_ref.shape[0])
    copy_pieces(tokens_ref, low, out_ref, sems)


def load_kernel(tokens_ref, order_ref, out_ref, sems):
    copy_pieces(tokens_ref, 0, out_ref, sems)


def at_end(devices):
    index = lax.axis_index(AXES)
    return (index == 0) | (index == devices - 1)


def lane_sum(block):
    return jnp.sum(block.astype(F32), axis=1, keepdims=True)


def pool_kernel(first, ends, devices, *refs):
    @pl.when(at_end(devices) == ends)
    def _():
        pool_body(first, ends, *refs)


def pool_body(first, ends, meta_ref, tokens_ref, edge_ref, *refs):
    if first:
        (x_ref, recv_ref, y_ref, _), refs = refs[:4], refs[4:]
        count, width = y_ref.shape
    else:
        (old_ref, old_mass_ref, recv_ref, _), refs = refs[:4], refs[4:]
        count, width = recv_ref.shape[0], old_ref.shape[1]
    sums, masses, *send_out, centroids = refs
    rows = tokens_ref.shape[0]
    reach = edge_ref.shape[0]
    scale = math.log2(math.e) / math.sqrt(width)
    x_rows, y_rows = pl.ds(0, count), pl.ds(count, count)

    occupied = meta_ref[pl.ds(OCCUPIED, 1), :] != 0
    if first:
        joined = x_ref[...] + recv_ref[...]
        centroids[x_rows, :] = jnp.where(occupied, joined, jnp.zeros_like(joined))
        centroids[y_rows, :] = y_ref[...]
    else:
        mass = lane_sum(old_mass_ref[x_rows, :]) + lane_sum(recv_ref[:, width:])
        joined = (old_ref[x_rows, :] + recv_ref[:, :width].astype(F32)) * (1.0 / mass)
        centroids[x_rows, :] = jnp.where(occupied, joined, 0.0).astype(BF16)
        mass = lane_sum(old_mass_ref[y_rows, :])
        centroids[y_rows, :] = (old_ref[y_rows, :] * (1.0 / mass)).astype(BF16)

    tiles = [(tokens_ref, i * TILE) for i in range(rows // TILE)]
    tiles += [(edge_ref, i * TILE) for i in range(reach // TILE)]

    def scores_of(tile):
        ref, row = tile
        return lax.dot_general(
            centroids[...],
            ref[pl.ds(row, TILE), :],
            (((1,), (1,)), ((), ())),
            preferred_element_type=F32,
        )

    def weights_of(tile, scores):
        ref, row = tile
        place = row + lax.broadcasted_iota(jnp.int32, (1, TILE), 1)
        if ref is edge_ref:
            place = place + meta_ref[pl.ds(EDGE, 1), :TILE]
        bound = [meta_ref[pl.ds(i, 1), :TILE] for i in (X_LOW, X_HIGH, Y_LOW, Y_HIGH)]
        in_x = (place >= bound[0]) & (place < bound[1])
        in_y = (place >= bound[2]) & (place < bound[3])
        mine = jnp.where(in_y, scores[count:], scores[:count])
        top = jnp.max(mine, axis=0, keepdims=True)
        powers = jnp.exp2((mine - top) * scale)
        inverse = 1.0 / jnp.sum(powers, axis=0, keepdims=True)
        return jnp.concatenate(
            [powers * jnp.where(in_x, inverse, 0.0), powers * jnp.where(in_y, inverse, 0.0)], axis=0
        )

    scores = scores_of(tiles[0])
    for at, tile in enumerate(tiles):
        upcoming = scores_of(tiles[at + 1]) if at + 1 < len(tiles) else None
        weights = weights_of(tile, scores)
        part = weights[:, :LANES]
        for i in range(1, TILE // LANES):
            part = part + weights[:, i * LANES : (i + 1) * LANES]
        added = jnp.dot(
            weights.astype(BF16), tile[0][pl.ds(tile[1], TILE), :], preferred_element_type=F32
        )
        if at == 0:
            masses[...] = part
            sums[...] = added
        else:
            masses[...] += part
            sums[...] += added
        scores = upcoming

    if ends:
        return
    (send_out,) = send_out
    mass = lane_sum(masses[x_rows, :])
    send_out[:, :width] = sums[x_rows, :].astype(BF16)
    high = mass.astype(BF16).astype(F32)
    middle = (mass - high).astype(BF16).astype(F32)
    low = mass - high - middle
    lane = lax.broadcasted_iota(jnp.int32, (count, LANES), 1)
    block = jnp.where(
        lane == 0, high, jnp.where(lane == 1, middle, jnp.where(lane == 2, low, 0.0))
    )
    send_out[:, width:] = block.astype(BF16)


def norm_kernel(devices, meta_ref, gain_ref, recv_ref, *refs):
    out_ref = refs[-1]
    count, width = out_ref.shape
    x_rows, y_rows = pl.ds(0, count), pl.ds(count, count)

    def finish(centroid):
        spread = jnp.sqrt(jnp.mean(centroid * centroid, axis=-1, keepdims=True) + 1e-06)
        out_ref[...] = (centroid * (1.0 / spread) * gain_ref[...]).astype(BF16)

    @pl.when(at_end(devices))
    def _():
        sums, masses = refs[2:4]
        finish(sums[y_rows, :] * (1.0 / lane_sum(masses[y_rows, :])))

    @pl.when(~at_end(devices))
    def _():
        sums, masses = refs[:2]
        mass = lane_sum(masses[x_rows, :]) + lane_sum(recv_ref[:, width:])
        joined = (sums[x_rows, :] + recv_ref[:, :width].astype(F32)) * (1.0 / mass)
        own = sums[y_rows, :] * (1.0 / lane_sum(masses[y_rows, :]))
        finish(jnp.where(meta_ref[pl.ds(SPLIT, 1), :] != 0, own, joined))


def on_device(tokens, shot_starts, seed_offsets, norm_gain, proj_weight):
    rows, width = tokens.shape
    count = seed_offsets.shape[1]
    reach = 3 * rows // 8
    devices = lax.axis_size(AXES)
    across = [(i, i + 1) for i in range(1, devices - 1, 2)]
    across += [(target, source) for source, target in across]
    across += [(0, devices - 1), (devices - 1, 0)]
    pair = [(0, 1), (1, 0)]

    def shape(*dims, dtype=BF16):
        return jax.ShapeDtypeStruct(dims, dtype)

    def in_hbm(array):
        return pltpu.with_memory_space_constraint(array, pltpu.HBM)

    far_tokens = in_hbm(tokens)
    first, own, tail, share, meta = pl.pallas_call(
        functools.partial(seed_kernel, reach),
        out_shape=(
            shape(count, width),
            shape(count, width),
            shape(count, width),
            shape(2, width),
            shape(8, width, dtype=jnp.int32),
        ),
        in_specs=[HBM_SPEC] * 3,
        out_specs=[VMEM_SPEC] * 5,
        scratch_shapes=[
            pltpu.SMEM(shot_starts.shape, jnp.int32),
            pltpu.SMEM(seed_offsets.shape, jnp.int32),
            pltpu.VMEM(seed_offsets.shape, jnp.int32),
            pltpu.VMEM((16 * count, width), BF16),
            pltpu.SemaphoreType.DMA((3,)),
            pltpu.SemaphoreType.DMA(()),
        ],
        compiler_params=pltpu.CompilerParams(vmem_limit_bytes=16 << 20),
        name="seeds",
    )(in_hbm(shot_starts), in_hbm(seed_offsets), far_tokens)
    given = lax.ppermute(tail, "feat", pair)

    def fetch(kernel, size, after, name):
        return pl.pallas_call(
            kernel,
            out_shape=shape(size, width),
            in_specs=[HBM_SPEC, VMEM_SPEC],
            out_specs=VMEM_SPEC,
            scratch_shapes=[pltpu.SemaphoreType.DMA((4,))],
            compiler_params=pltpu.CompilerParams(vmem_limit_bytes=16 << 20),
            name=name,
        )(far_tokens, after)

    edge = fetch(strip_kernel, reach, tail, "strip")
    edge, given = lax.optimization_barrier((edge, given))
    edge = lax.ppermute(edge, "feat", pair)
    x = first + given * share[:1]
    y = own + given * share[1:]
    received = lax.ppermute(x, AXES, across)
    near_tokens = fetch(load_kernel, rows, x, "load")

    def pool(first, ends, *state):
        outs = (shape(2 * count, width, dtype=F32), shape(2 * count, LANES, dtype=F32))
        outs += () if ends else (shape(count, width + LANES),)
        return pl.pallas_call(
            functools.partial(pool_kernel, first, ends, devices),
            out_shape=outs,
            in_specs=[VMEM_SPEC] * 7,
            out_specs=[VMEM_SPEC] * len(outs),
            scratch_shapes=[pltpu.VMEM((2 * count, width), BF16)],
            compiler_params=pltpu.CompilerParams(vmem_limit_bytes=16 << 20),
            name="ends" if ends else "pool",
        )(meta, near_tokens, edge, *state)

    sums, masses, send = pool(True, False, x, received, y, y)
    start = received
    received = lax.ppermute(send, AXES, across)
    end_sums, end_masses = pool(True, True, x, start, y, masses)
    for _ in range(ITERS - 1):
        before = received
        sums, masses, send = pool(False, False, sums, masses, before, end_masses)
        received = lax.ppermute(send, AXES, across)
        end_sums, end_masses = pool(False, True, end_sums, end_masses, before, masses)
    normed = pl.pallas_call(
        functools.partial(norm_kernel, devices),
        out_shape=shape(count, width),
        in_specs=[VMEM_SPEC] * 7,
        out_specs=VMEM_SPEC,
        compiler_params=pltpu.CompilerParams(vmem_limit_bytes=8 << 20),
        name="norm",
    )(meta, norm_gain[None, :], received, sums, masses, end_sums, end_masses)
    both = lax.all_gather(normed, "feat", axis=0, tiled=True)
    return jnp.dot(both, proj_weight, preferred_element_type=F32).astype(BF16)


def solution(mesh):
    in_specs = (P(AXES, None), P(), P(), P(), P(None, "feat"))
    out_specs = P("seq", "feat")
    return jax.shard_map(
        on_device, mesh=mesh, in_specs=in_specs, out_specs=out_specs, check_vma=False
    )
```

time: 62.8 us -> 60 us (0.955)
  Pallas kernels: 36.1 us -> 30.6 us
  waiting for transfers between devices: 18 us -> 20.4 us
    pallas_call x8 -> x9, Pallas kernels: 35.2 us -> 30.3 us  [the longest x6 20.4 us: pool(): pl.pallas_call(functools.partial(pool_kernel, first, ends, devices), out_...]
    ppermute x3, waiting for transfers between devices: 15.3 us -> 19.3 us  [on_device(): received = lax.ppermute(send, AXES, across)]
    ppermute x1, waiting for transfers between devices: 1.26 us -> 0.01 us  [on_device(): given = lax.ppermute(tail, 'feat', pair)]
  transfers between devices with their start and end apart: 6 -> 6, of which waited for: 5 -> 4; matrix products, arithmetic and copies ran while one was open for 0% -> 0% of each run, Pallas kernels for 13% -> 10%
where the time goes in v3:
time: 60 us; the launch traced here: 59.8 us
  Pallas kernels  30.6 us (51%)
  waiting for transfers between devices  20.4 us (34%)
  starting transfers between devices  3.87 us (6%)
  matrix products  2.6 us (4%)
  blocking collectives  2.04 us (3%)
    pallas_call x6, Pallas kernels, pool(): pl.pallas_call(functools.partial(pool_kernel, first, ends, devices), out_...  20.4 us
    ppermute x3, waiting for transfers between devices, on_device(): received = lax.ppermute(send, AXES, across)  19.3 us
    pallas_call x2, Pallas kernels, fetch(): pl.pallas_call(kernel, out_shape=shape(size, width), in_specs=[HBM_SPEC,...  6.22 us
    pallas_call x1, Pallas kernels, on_device(): pl.pallas_call(functools.partial(seed_kernel, reach), out_shape=(shape(co...  3.74 us
    dot_general x1, matrix products, on_device(): return jnp.dot(both, proj_weight, preferred_element_type=F32).astype(BF16)  2.6 us
    all_gather x1, blocking collectives, on_device(): both = lax.all_gather(normed, 'feat', axis=0, tiled=True)  2.04 us
    ppermute x1, starting transfers between devices, on_device(): received = lax.ppermute(x, AXES, across)  1.64 us
    ppermute x3, starting transfers between devices, on_device(): received = lax.ppermute(send, AXES, across)  1.39 us
  transfers between devices with their start and end apart: 6, of which 4 were waited for; matrix products, arithmetic and copies ran while one was open for 0% of the time, Pallas kernels for 10%

profile of v3, /device:TPU:29, one launch (start us, length us, event | category | flops | bytes accessed | tf_op | source)
XLA Modules:
  0.0 59.8 jit_solution(8758670759703475349)
XLA Ops:
  0.0 3.7 %seeds.1 = (bf16[64,1280]{1,0:T(8,128)(2,1)S(1)}, bf16[64,1280]{1,0:T(8,128)(2,1)S(1)}, bf16[64,1280]{1,0:T(8,128)(2,1)S(1)}, bf16[2,1280]{1,0:T(2,128)(2,1)S(1)}, s32[8,1280]{1,0:T(8,128)S(1)}) custom-call(s32[32]{0:T(128)} %starts_hbm.1, s32[32,64]{1,0:T(8,128)} %seeds_hbm.1, bf16[4096,1280]{1,0:T(8,128)(2,1)} %tokens_ref.5), custom_call_target="tpu_custom_call" | custom-call | tf_op jit(solution)/shard_map/seeds/pallas_call | solution.py:298
  3.8 0.7 %collective-permute-start = (bf16[64,1280]{1,0:T(8,128)(2,1)S(1)}, bf16[64,1280]{1,0:T(8,128)(2,1)S(1)}, u32[]{:S(2)}, u32[]{:S(2)}) collective-permute-start(bf16[64,1280]{1,0:T(8,128)(2,1)S(1)} %get-tuple-element.29.order_ref), channel_id=1, source_target_pairs={{0,1},{1,0},{2,3},{3,2},{4,5},{5,4},{6,7},{7,6},{8,9},{9,8},{10,11... | collective-permute-start | bytes 491528 | tf_op jit(solution)/shard_map/ppermute | solution.py:320
  4.5 2.1 %strip.1 = bf16[1536,1280]{1,0:T(8,128)(2,1)S(1)} custom-call(bf16[4096,1280]{1,0:T(8,128)(2,1)} %tokens_ref.5, bf16[64,1280]{1,0:T(8,128)(2,1)S(1)} %get-tuple-element.29.order_ref), custom_call_target="tpu_custom_call" | custom-call | tf_op jit(solution)/shard_map/strip/pallas_call | solution.py:323
  6.6 0.0 collective-permute-done
  6.6 0.1 collective-permute-start.1
  6.8 1.6 %collective-permute-start.2 = (bf16[64,1280]{1,0:T(8,128)(2,1)S(1)}, bf16[64,1280]{1,0:T(8,128)(2,1)S(1)}, u32[]{:S(2)}, u32[]{:S(2)}) collective-permute-start(bf16[64,1280]{1,0:T(8,128)(2,1)S(1)} %get-tuple-element.52.order_ref.refs_3_), channel_id=1, source_target_pairs={{1,2},{3,4},{5,6},{7,8},{9,10},{11,12},{13,14},{15,16},{17,18},{19... | collective-permute-start | bytes 491528 | tf_op jit(solution)/shard_map/ppermute | solution.py:338
  8.5 4.1 %load.1.refs_1_ = bf16[4096,1280]{1,0:T(8,128)(2,1)S(1)} custom-call(bf16[4096,1280]{1,0:T(8,128)(2,1)} %tokens_ref.5, bf16[64,1280]{1,0:T(8,128)(2,1)S(1)} %get-tuple-element.52.order_ref.refs_3_), custom_call_target="tpu_custom_call" | custom-call | tf_op jit(solution)/shard_map/load/pallas_call | solution.py:323
  12.6 1.1 %collective-permute-done.2.refs_4_ = bf16[64,1280]{1,0:T(8,128)(2,1)S(1)} collective-permute-done((bf16[64,1280]{1,0:T(8,128)(2,1)S(1)}, bf16[64,1280]{1,0:T(8,128)(2,1)S(1)}, u32[]{:S(2)}, u32[]{:S(2)}) %collective-permute-start.2) | collective-permute-done | bytes 163872 | tf_op jit(solution)/shard_map/ppermute | solution.py:338
  13.6 0.0 collective-permute-done.1.refs_2_
  13.6 6.7 %pool.3 = (f32[128,1280]{1,0:T(8,128)S(1)}, f32[128,128]{1,0:T(8,128)S(1)}, bf16[64,1408]{1,0:T(8,128)(2,1)S(1)}) custom-call(s32[8,1280]{1,0:T(8,128)S(1)} %get-tuple-element.27.refs_0_.meta_ref, bf16[4096,1280]{1,0:T(8,128)(2,1)S(1)} %load.1.refs_1_, bf16[1536,1280]{1,0:T(8,128)(2,1)S(1)} %collective-permute-done.1.refs_2_, ...), custom_call_target="tpu_custom_call" | custom-call | tf_op jit(solution)/shard_map/pool/pallas_call | solution.py:344
  20.4 1.2 %collective-permute-start.3 = (bf16[64,1408]{1,0:T(8,128)(2,1)S(1)}, bf16[64,1408]{1,0:T(8,128)(2,1)S(1)}, u32[]{:S(2)}, u32[]{:S(2)}) collective-permute-start(bf16[64,1408]{1,0:T(8,128)(2,1)S(1)} %get-tuple-element.36), channel_id=1, source_target_pairs={{1,2},{3,4},{5,6},{7,8},{9,10},{11,12},{13,14},{15,16},{17,18},{19... | collective-permute-start | bytes 540680 | tf_op jit(solution)/shard_map/ppermute | solution.py:356
  21.6 5.8 %collective-permute-done.3.refs_5_ = bf16[64,1408]{1,0:T(8,128)(2,1)S(1)} collective-permute-done((bf16[64,1408]{1,0:T(8,128)(2,1)S(1)}, bf16[64,1408]{1,0:T(8,128)(2,1)S(1)}, u32[]{:S(2)}, u32[]{:S(2)}) %collective-permute-start.3) | collective-permute-done | bytes 180256 | tf_op jit(solution)/shard_map/ppermute | solution.py:356
  27.4 6.8 %pool.4 = (f32[128,1280]{1,0:T(8,128)S(1)}, f32[128,128]{1,0:T(8,128)S(1)}, bf16[64,1408]{1,0:T(8,128)(2,1)S(1)}) custom-call(s32[8,1280]{1,0:T(8,128)S(1)} %get-tuple-element.27.refs_0_.meta_ref, bf16[4096,1280]{1,0:T(8,128)(2,1)S(1)} %load.1.refs_1_, bf16[1536,1280]{1,0:T(8,128)(2,1)S(1)} %collective-permute-done.1.refs_2_, ...), custom_call_target="tpu_custom_call" | custom-call | tf_op jit(solution)/shard_map/pool/pallas_call | solution.py:344
  34.2 0.1 collective-permute-start.4
  34.3 0.0 copy-start
  34.3 6.8 %collective-permute-done.4.refs_5_ = bf16[64,1408]{1,0:T(8,128)(2,1)S(1)} collective-permute-done((bf16[64,1408]{1,0:T(8,128)(2,1)S(1)}, bf16[64,1408]{1,0:T(8,128)(2,1)S(1)}, u32[]{:S(2)}, u32[]{:S(2)}) %collective-permute-start.4) | collective-permute-done | bytes 180256 | tf_op jit(solution)/shard_map/ppermute | solution.py:361
  41.1 0.0 slice-start
  41.1 0.0 slice-start.1
  41.1 6.8 %pool.5 = (f32[128,1280]{1,0:T(8,128)S(1)}, f32[128,128]{1,0:T(8,128)S(1)}, bf16[64,1408]{1,0:T(8,128)(2,1)S(1)}) custom-call(s32[8,1280]{1,0:T(8,128)S(1)} %get-tuple-element.27.refs_0_.meta_ref, bf16[4096,1280]{1,0:T(8,128)(2,1)S(1)} %load.1.refs_1_, bf16[1536,1280]{1,0:T(8,128)(2,1)S(1)} %collective-permute-done.1.refs_2_, ...), custom_call_target="tpu_custom_call" | custom-call | tf_op jit(solution)/shard_map/pool/pallas_call | solution.py:344
  47.9 0.1 collective-permute-start.5
  48.0 0.0 copy-done
  48.0 0.0 slice-start.2
  48.1 6.8 %collective-permute-done.5.recv_ref = bf16[64,1408]{1,0:T(8,128)(2,1)S(1)} collective-permute-done((bf16[64,1408]{1,0:T(8,128)(2,1)S(1)}, bf16[64,1408]{1,0:T(8,128)(2,1)S(1)}, u32[]{:S(2)}, u32[]{:S(2)}) %collective-permute-start.5) | collective-permute-done | bytes 180256 | tf_op jit(solution)/shard_map/ppermute | solution.py:361
  54.8 0.3 norm.1
  55.1 2.0 %all_gather.3 = bf16[128,1280]{1,0:T(8,128)(2,1)S(1)} all-gather(bf16[64,1280]{1,0:T(8,128)(2,1)S(1)} %norm.1), channel_id=1, replica_groups=mesh['seq'=16,'feat'=2] {'feat'}, dimensions={0}, use_global_device_ids=true | all-gather | bytes 491520 | tf_op jit(solution)/shard_map/all_gather | solution.py:371
  57.2 0.0 slice-done
  57.2 0.0 slice-done.1
  57.2 0.0 slice-done.2
  57.2 2.6 %convolution_convert_fusion = bf16[128,4096]{1,0:T(8,128)(2,1)} fusion(bf16[128,1280]{1,0:T(8,128)(2,1)S(1)} %all_gather.3, bf16[1280,4096]{1,0:T(8,128)(2,1)S(1)} %bitcast.3), kind=kOutput, calls=%fused_computation | convolution fusion | flops 1342701568 | bytes 11862016 | tf_op jit(solution)/shard_map/dot_general | solution.py:372
  (7 shorter events, 0.1 us)
Async XLA Ops:
  3.8 2.9 %collective-permute-start = (bf16[64,1280]{1,0:T(8,128)(2,1)S(1)}, bf16[64,1280]{1,0:T(8,128)(2,1)S(1)}, u32[]{:S(2)}, u32[]{:S(2)}) collective-permute-start(bf16[64,1280]{1,0:T(8,128)(2,1)S(1)} %get-tuple-element.29.order_ref), channel_id=1, source_target_pairs={{0,1},{1,0},{2,3},{3,2},{4,5},{5,4},{6,7},{7,6},{8,9},{9,8},{10,11... | collective-permute-start | bytes 491528 | tf_op jit(solution)/shard_map/ppermute | solution.py:320
  6.6 7.0 %collective-permute-start.1 = (bf16[1536,1280]{1,0:T(8,128)(2,1)S(1)}, bf16[1536,1280]{1,0:T(8,128)(2,1)S(1)}, u32[]{:S(2)}, u32[]{:S(2)}) collective-permute-start(bf16[1536,1280]{1,0:T(8,128)(2,1)S(1)} %strip.1), channel_id=1, source_target_pairs={{0,1},{1,0},{2,3},{3,2},{4,5},{5,4},{6,7},{7,6},{8,9},{9,8},{10,11... | collective-permute-start | bytes 11796488 | tf_op jit(solution)/shard_map/ppermute | solution.py:335
  6.8 6.8 %collective-permute-start.2 = (bf16[64,1280]{1,0:T(8,128)(2,1)S(1)}, bf16[64,1280]{1,0:T(8,128)(2,1)S(1)}, u32[]{:S(2)}, u32[]{:S(2)}) collective-permute-start(bf16[64,1280]{1,0:T(8,128)(2,1)S(1)} %get-tuple-element.52.order_ref.refs_3_), channel_id=1, source_target_pairs={{1,2},{3,4},{5,6},{7,8},{9,10},{11,12},{13,14},{15,16},{17,18},{19... | collective-permute-start | bytes 491528 | tf_op jit(solution)/shard_map/ppermute | solution.py:338
  20.4 7.0 %collective-permute-start.3 = (bf16[64,1408]{1,0:T(8,128)(2,1)S(1)}, bf16[64,1408]{1,0:T(8,128)(2,1)S(1)}, u32[]{:S(2)}, u32[]{:S(2)}) collective-permute-start(bf16[64,1408]{1,0:T(8,128)(2,1)S(1)} %get-tuple-element.36), channel_id=1, source_target_pairs={{1,2},{3,4},{5,6},{7,8},{9,10},{11,12},{13,14},{15,16},{17,18},{19... | collective-permute-start | bytes 540680 | tf_op jit(solution)/shard_map/ppermute | solution.py:356
  34.2 6.9 %collective-permute-start.4 = (bf16[64,1408]{1,0:T(8,128)(2,1)S(1)}, bf16[64,1408]{1,0:T(8,128)(2,1)S(1)}, u32[]{:S(2)}, u32[]{:S(2)}) collective-permute-start(bf16[64,1408]{1,0:T(8,128)(2,1)S(1)} %get-tuple-element.40), channel_id=1, source_target_pairs={{1,2},{3,4},{5,6},{7,8},{9,10},{11,12},{13,14},{15,16},{17,18},{19... | collective-permute-start | bytes 540680 | tf_op jit(solution)/shard_map/ppermute | solution.py:361
  34.3 13.7 %copy-start = (f32[1280]{0:T(1024)S(1)}, f32[1280]{0:T(1024)}, u32[]{:S(2)}) copy-start(f32[1280]{0:T(1024)} %param.8) | copy-start | bytes 15364
  41.1 16.1 %slice-start = ((s8[10485760]{0:T(1024)(128)(4,1)}), s8[4194304]{0:T(1024)(128)(4,1)S(1)}, s32[]{:S(2)}) async-start(s8[10485760]{0:T(1024)(128)(4,1)} %bitcast.2), calls=%async_computation | async-start | bytes 8388608
  41.1 16.1 %slice-start.1 = ((s8[10485760]{0:T(1024)(128)(4,1)}), s8[4194304]{0:T(1024)(128)(4,1)S(1)}, s32[]{:S(2)}) async-start(s8[10485760]{0:T(1024)(128)(4,1)} %bitcast.2), calls=%async_computation.1 | async-start | bytes 8388608
  47.9 6.9 %collective-permute-start.5 = (bf16[64,1408]{1,0:T(8,128)(2,1)S(1)}, bf16[64,1408]{1,0:T(8,128)(2,1)S(1)}, u32[]{:S(2)}, u32[]{:S(2)}) collective-permute-start(bf16[64,1408]{1,0:T(8,128)(2,1)S(1)} %get-tuple-element.43), channel_id=1, source_target_pairs={{1,2},{3,4},{5,6},{7,8},{9,10},{11,12},{13,14},{15,16},{17,18},{19... | collective-permute-start | bytes 540680 | tf_op jit(solution)/shard_map/ppermute | solution.py:361
  48.0 9.1 %slice-start.2 = ((s8[10485760]{0:T(1024)(128)(4,1)}), s8[2097152]{0:T(1024)(128)(4,1)S(1)}, s32[]{:S(2)}) async-start(s8[10485760]{0:T(1024)(128)(4,1)} %bitcast.2), calls=%async_computation.2 | async-start | bytes 4194304

commit v4 on v3

--- a/solution.py
+++ b/solution.py
@@ -278,6 +278,16 @@
         finish(jnp.where(meta_ref[pl.ds(SPLIT, 1), :] != 0, own, joined))
 
 
+def join_kernel(normed_ref, other_ref, out_ref):
+    count = normed_ref.shape[0]
+    for half in range(2):
+
+        @pl.when(lax.axis_index("feat") == half)
+        def _():
+            out_ref[pl.ds(half * count, count), :] = normed_ref[...]
+            out_ref[pl.ds((1 - half) * count, count), :] = other_ref[...]
+
+
 def on_device(tokens, shot_starts, seed_offsets, norm_gain, proj_weight):
     rows, width = tokens.shape
     count = seed_offsets.shape[1]
@@ -368,7 +378,14 @@
         compiler_params=pltpu.CompilerParams(vmem_limit_bytes=8 << 20),
         name="norm",
     )(meta, norm_gain[None, :], received, sums, masses, end_sums, end_masses)
-    both = lax.all_gather(normed, "feat", axis=0, tiled=True)
+    both = pl.pallas_call(
+        join_kernel,
+        out_shape=shape(2 * count, width),
+        in_specs=[VMEM_SPEC] * 2,
+        out_specs=VMEM_SPEC,
+        compiler_params=pltpu.CompilerParams(vmem_limit_bytes=8 << 20),
+        name="join",
+    )(normed, lax.ppermute(normed, "feat", pair))
     return jnp.dot(both, proj_weight, preferred_element_type=F32).astype(BF16)
 
 

time: 60 us -> 59.5 us (level)
  blocking collectives: 2.04 us -> 0 us
  waiting for transfers between devices: 20.4 us -> 21.8 us
    all_gather x1 -> x0, blocking collectives: 2.04 us -> none  [on_device(): both = lax.all_gather(normed, 'feat', axis=0, tiled=True)]
    ppermute x0 -> x1, waiting for transfers between devices: none -> 1.38 us  [on_device(): lax.ppermute(normed, 'feat', pair)]
  transfers between devices with their start and end apart: 6 -> 7, of which waited for: 4 -> 5; matrix products, arithmetic and copies ran while one was open for 0% -> 0% of each run, Pallas kernels for 10% -> 11%
where the time goes in v4:
time: 59.5 us; the launch traced here: 59.2 us
  Pallas kernels  30.6 us (51%)
  waiting for transfers between devices  21.8 us (37%)
  starting transfers between devices  3.91 us (7%)
  matrix products  2.59 us (4%)
    pallas_call x6, Pallas kernels, pool(): pl.pallas_call(functools.partial(pool_kernel, first, ends, devices), out_...  20.4 us
    ppermute x3, waiting for transfers between devices, on_device(): received = lax.ppermute(send, AXES, across)  19.4 us
    pallas_call x2, Pallas kernels, fetch(): pl.pallas_call(kernel, out_shape=shape(size, width), in_specs=[HBM_SPEC,...  6.22 us
    pallas_call x1, Pallas kernels, on_device(): pl.pallas_call(functools.partial(seed_kernel, reach), out_shape=(shape(co...  3.74 us
    dot_general x1, matrix products, on_device(): return jnp.dot(both, proj_weight, preferred_element_type=F32).astype(BF16)  2.59 us
    ppermute x1, starting transfers between devices, on_device(): received = lax.ppermute(x, AXES, across)  1.64 us
    ppermute x1, waiting for transfers between devices, on_device(): lax.ppermute(normed, 'feat', pair)  1.38 us
    ppermute x3, starting transfers between devices, on_device(): received = lax.ppermute(send, AXES, across)  1.36 us
  transfers between devices with their start and end apart: 7, of which 5 were waited for; matrix products, arithmetic and copies ran while one was open for 0% of the time, Pallas kernels for 11%

profile of v4, /device:TPU:29, one launch (start us, length us, event | category | flops | bytes accessed | tf_op | source)
XLA Modules:
  0.0 59.2 jit_solution(1673582254206704122)
XLA Ops:
  0.0 3.7 %seeds.1 = (bf16[64,1280]{1,0:T(8,128)(2,1)S(1)}, bf16[64,1280]{1,0:T(8,128)(2,1)S(1)}, bf16[64,1280]{1,0:T(8,128)(2,1)S(1)}, bf16[2,1280]{1,0:T(2,128)(2,1)S(1)}, s32[8,1280]{1,0:T(8,128)S(1)}) custom-call(s32[32]{0:T(128)} %starts_hbm.1, s32[32,64]{1,0:T(8,128)} %seeds_hbm.1, bf16[4096,1280]{1,0:T(8,128)(2,1)} %tokens_ref.5), custom_call_target="tpu_custom_call" | custom-call | tf_op jit(solution)/shard_map/seeds/pallas_call | solution.py:308
  3.8 0.7 %collective-permute-start = (bf16[64,1280]{1,0:T(8,128)(2,1)S(1)}, bf16[64,1280]{1,0:T(8,128)(2,1)S(1)}, u32[]{:S(2)}, u32[]{:S(2)}) collective-permute-start(bf16[64,1280]{1,0:T(8,128)(2,1)S(1)} %get-tuple-element.29.order_ref), channel_id=1, source_target_pairs={{0,1},{1,0},{2,3},{3,2},{4,5},{5,4},{6,7},{7,6},{8,9},{9,8},{10,11... | collective-permute-start | bytes 491528 | tf_op jit(solution)/shard_map/ppermute | solution.py:330
  4.5 2.1 %strip.1 = bf16[1536,1280]{1,0:T(8,128)(2,1)S(1)} custom-call(bf16[4096,1280]{1,0:T(8,128)(2,1)} %tokens_ref.5, bf16[64,1280]{1,0:T(8,128)(2,1)S(1)} %get-tuple-element.29.order_ref), custom_call_target="tpu_custom_call" | custom-call | tf_op jit(solution)/shard_map/strip/pallas_call | solution.py:333
  6.6 0.0 collective-permute-done
  6.6 0.1 collective-permute-start.1
  6.8 1.6 %collective-permute-start.2 = (bf16[64,1280]{1,0:T(8,128)(2,1)S(1)}, bf16[64,1280]{1,0:T(8,128)(2,1)S(1)}, u32[]{:S(2)}, u32[]{:S(2)}) collective-permute-start(bf16[64,1280]{1,0:T(8,128)(2,1)S(1)} %get-tuple-element.52.order_ref.refs_3_), channel_id=1, source_target_pairs={{1,2},{3,4},{5,6},{7,8},{9,10},{11,12},{13,14},{15,16},{17,18},{19... | collective-permute-start | bytes 491528 | tf_op jit(solution)/shard_map/ppermute | solution.py:348
  8.5 4.1 %load.1.refs_1_ = bf16[4096,1280]{1,0:T(8,128)(2,1)S(1)} custom-call(bf16[4096,1280]{1,0:T(8,128)(2,1)} %tokens_ref.5, bf16[64,1280]{1,0:T(8,128)(2,1)S(1)} %get-tuple-element.52.order_ref.refs_3_), custom_call_target="tpu_custom_call" | custom-call | tf_op jit(solution)/shard_map/load/pallas_call | solution.py:333
  12.6 1.1 %collective-permute-done.2.refs_4_ = bf16[64,1280]{1,0:T(8,128)(2,1)S(1)} collective-permute-done((bf16[64,1280]{1,0:T(8,128)(2,1)S(1)}, bf16[64,1280]{1,0:T(8,128)(2,1)S(1)}, u32[]{:S(2)}, u32[]{:S(2)}) %collective-permute-start.2) | collective-permute-done | bytes 163872 | tf_op jit(solution)/shard_map/ppermute | solution.py:348
  13.6 0.0 collective-permute-done.1.refs_2_
  13.6 6.7 %pool.3 = (f32[128,1280]{1,0:T(8,128)S(1)}, f32[128,128]{1,0:T(8,128)S(1)}, bf16[64,1408]{1,0:T(8,128)(2,1)S(1)}) custom-call(s32[8,1280]{1,0:T(8,128)S(1)} %get-tuple-element.27.refs_0_.meta_ref, bf16[4096,1280]{1,0:T(8,128)(2,1)S(1)} %load.1.refs_1_, bf16[1536,1280]{1,0:T(8,128)(2,1)S(1)} %collective-permute-done.1.refs_2_, ...), custom_call_target="tpu_custom_call" | custom-call | tf_op jit(solution)/shard_map/pool/pallas_call | solution.py:354
  20.4 1.2 %collective-permute-start.3 = (bf16[64,1408]{1,0:T(8,128)(2,1)S(1)}, bf16[64,1408]{1,0:T(8,128)(2,1)S(1)}, u32[]{:S(2)}, u32[]{:S(2)}) collective-permute-start(bf16[64,1408]{1,0:T(8,128)(2,1)S(1)} %get-tuple-element.36), channel_id=1, source_target_pairs={{1,2},{3,4},{5,6},{7,8},{9,10},{11,12},{13,14},{15,16},{17,18},{19... | collective-permute-start | bytes 540680 | tf_op jit(solution)/shard_map/ppermute | solution.py:366
  21.6 5.8 %collective-permute-done.3.refs_5_ = bf16[64,1408]{1,0:T(8,128)(2,1)S(1)} collective-permute-done((bf16[64,1408]{1,0:T(8,128)(2,1)S(1)}, bf16[64,1408]{1,0:T(8,128)(2,1)S(1)}, u32[]{:S(2)}, u32[]{:S(2)}) %collective-permute-start.3) | collective-permute-done | bytes 180256 | tf_op jit(solution)/shard_map/ppermute | solution.py:366
  27.4 6.8 %pool.4 = (f32[128,1280]{1,0:T(8,128)S(1)}, f32[128,128]{1,0:T(8,128)S(1)}, bf16[64,1408]{1,0:T(8,128)(2,1)S(1)}) custom-call(s32[8,1280]{1,0:T(8,128)S(1)} %get-tuple-element.27.refs_0_.meta_ref, bf16[4096,1280]{1,0:T(8,128)(2,1)S(1)} %load.1.refs_1_, bf16[1536,1280]{1,0:T(8,128)(2,1)S(1)} %collective-permute-done.1.refs_2_, ...), custom_call_target="tpu_custom_call" | custom-call | tf_op jit(solution)/shard_map/pool/pallas_call | solution.py:354
  34.2 0.1 collective-permute-start.4
  34.3 0.0 copy-start
  34.3 6.8 %collective-permute-done.4.refs_5_ = bf16[64,1408]{1,0:T(8,128)(2,1)S(1)} collective-permute-done((bf16[64,1408]{1,0:T(8,128)(2,1)S(1)}, bf16[64,1408]{1,0:T(8,128)(2,1)S(1)}, u32[]{:S(2)}, u32[]{:S(2)}) %collective-permute-start.4) | collective-permute-done | bytes 180256 | tf_op jit(solution)/shard_map/ppermute | solution.py:371
  41.1 0.0 slice-start
  41.1 0.0 slice-start.1
  41.1 6.8 %pool.5 = (f32[128,1280]{1,0:T(8,128)S(1)}, f32[128,128]{1,0:T(8,128)S(1)}, bf16[64,1408]{1,0:T(8,128)(2,1)S(1)}) custom-call(s32[8,1280]{1,0:T(8,128)S(1)} %get-tuple-element.27.refs_0_.meta_ref, bf16[4096,1280]{1,0:T(8,128)(2,1)S(1)} %load.1.refs_1_, bf16[1536,1280]{1,0:T(8,128)(2,1)S(1)} %collective-permute-done.1.refs_2_, ...), custom_call_target="tpu_custom_call" | custom-call | tf_op jit(solution)/shard_map/pool/pallas_call | solution.py:354
  47.9 0.1 collective-permute-start.5
  48.0 0.0 copy-done
  48.0 0.0 slice-start.2
  48.1 6.8 %collective-permute-done.5.recv_ref = bf16[64,1408]{1,0:T(8,128)(2,1)S(1)} collective-permute-done((bf16[64,1408]{1,0:T(8,128)(2,1)S(1)}, bf16[64,1408]{1,0:T(8,128)(2,1)S(1)}, u32[]{:S(2)}, u32[]{:S(2)}) %collective-permute-start.5) | collective-permute-done | bytes 180256 | tf_op jit(solution)/shard_map/ppermute | solution.py:371
  54.8 0.3 norm.1.normed_ref
  55.1 0.1 collective-permute-start.6
  55.2 1.4 %collective-permute-done.6.other_ref = bf16[64,1280]{1,0:T(8,128)(2,1)S(1)} collective-permute-done((bf16[64,1280]{1,0:T(8,128)(2,1)S(1)}, bf16[64,1280]{1,0:T(8,128)(2,1)S(1)}, u32[]{:S(2)}, u32[]{:S(2)}) %collective-permute-start.6) | collective-permute-done | bytes 163872 | tf_op jit(solution)/shard_map/ppermute | solution.py:388
  56.6 0.0 slice-done
  56.6 0.0 slice-done.1
  56.6 0.0 slice-done.2
  56.6 2.6 %convolution_convert_fusion = bf16[128,4096]{1,0:T(8,128)(2,1)} fusion(bf16[128,1280]{1,0:T(8,128)(2,1)S(1)} %join.1, bf16[1280,4096]{1,0:T(8,128)(2,1)S(1)} %bitcast.3), kind=kOutput, calls=%fused_computation | convolution fusion | flops 1342701568 | bytes 11862016 | tf_op jit(solution)/shard_map/dot_general | solution.py:389
  (8 shorter events, 0.1 us)
Async XLA Ops:
  3.8 2.9 %collective-permute-start = (bf16[64,1280]{1,0:T(8,128)(2,1)S(1)}, bf16[64,1280]{1,0:T(8,128)(2,1)S(1)}, u32[]{:S(2)}, u32[]{:S(2)}) collective-permute-start(bf16[64,1280]{1,0:T(8,128)(2,1)S(1)} %get-tuple-element.29.order_ref), channel_id=1, source_target_pairs={{0,1},{1,0},{2,3},{3,2},{4,5},{5,4},{6,7},{7,6},{8,9},{9,8},{10,11... | collective-permute-start | bytes 491528 | tf_op jit(solution)/shard_map/ppermute | solution.py:330
  6.6 7.0 %collective-permute-start.1 = (bf16[1536,1280]{1,0:T(8,128)(2,1)S(1)}, bf16[1536,1280]{1,0:T(8,128)(2,1)S(1)}, u32[]{:S(2)}, u32[]{:S(2)}) collective-permute-start(bf16[1536,1280]{1,0:T(8,128)(2,1)S(1)} %strip.1), channel_id=1, source_target_pairs={{0,1},{1,0},{2,3},{3,2},{4,5},{5,4},{6,7},{7,6},{8,9},{9,8},{10,11... | collective-permute-start | bytes 11796488 | tf_op jit(solution)/shard_map/ppermute | solution.py:345
  6.8 6.8 %collective-permute-start.2 = (bf16[64,1280]{1,0:T(8,128)(2,1)S(1)}, bf16[64,1280]{1,0:T(8,128)(2,1)S(1)}, u32[]{:S(2)}, u32[]{:S(2)}) collective-permute-start(bf16[64,1280]{1,0:T(8,128)(2,1)S(1)} %get-tuple-element.52.order_ref.refs_3_), channel_id=1, source_target_pairs={{1,2},{3,4},{5,6},{7,8},{9,10},{11,12},{13,14},{15,16},{17,18},{19... | collective-permute-start | bytes 491528 | tf_op jit(solution)/shard_map/ppermute | solution.py:348
  20.4 7.0 %collective-permute-start.3 = (bf16[64,1408]{1,0:T(8,128)(2,1)S(1)}, bf16[64,1408]{1,0:T(8,128)(2,1)S(1)}, u32[]{:S(2)}, u32[]{:S(2)}) collective-permute-start(bf16[64,1408]{1,0:T(8,128)(2,1)S(1)} %get-tuple-element.36), channel_id=1, source_target_pairs={{1,2},{3,4},{5,6},{7,8},{9,10},{11,12},{13,14},{15,16},{17,18},{19... | collective-permute-start | bytes 540680 | tf_op jit(solution)/shard_map/ppermute | solution.py:366
  34.2 6.9 %collective-permute-start.4 = (bf16[64,1408]{1,0:T(8,128)(2,1)S(1)}, bf16[64,1408]{1,0:T(8,128)(2,1)S(1)}, u32[]{:S(2)}, u32[]{:S(2)}) collective-permute-start(bf16[64,1408]{1,0:T(8,128)(2,1)S(1)} %get-tuple-element.40), channel_id=1, source_target_pairs={{1,2},{3,4},{5,6},{7,8},{9,10},{11,12},{13,14},{15,16},{17,18},{19... | collective-permute-start | bytes 540680 | tf_op jit(solution)/shard_map/ppermute | solution.py:371
  34.3 13.7 %copy-start = (f32[1280]{0:T(1024)S(1)}, f32[1280]{0:T(1024)}, u32[]{:S(2)}) copy-start(f32[1280]{0:T(1024)} %param.8) | copy-start | bytes 15364
  41.1 15.5 %slice-start = ((s8[10485760]{0:T(1024)(128)(4,1)}), s8[4194304]{0:T(1024)(128)(4,1)S(1)}, s32[]{:S(2)}) async-start(s8[10485760]{0:T(1024)(128)(4,1)} %bitcast.2), calls=%async_computation | async-start | bytes 8388608
  41.1 15.5 %slice-start.1 = ((s8[10485760]{0:T(1024)(128)(4,1)}), s8[4194304]{0:T(1024)(128)(4,1)S(1)}, s32[]{:S(2)}) async-start(s8[10485760]{0:T(1024)(128)(4,1)} %bitcast.2), calls=%async_computation.1 | async-start | bytes 8388608
  47.9 6.9 %collective-permute-start.5 = (bf16[64,1408]{1,0:T(8,128)(2,1)S(1)}, bf16[64,1408]{1,0:T(8,128)(2,1)S(1)}, u32[]{:S(2)}, u32[]{:S(2)}) collective-permute-start(bf16[64,1408]{1,0:T(8,128)(2,1)S(1)} %get-tuple-element.43), channel_id=1, source_target_pairs={{1,2},{3,4},{5,6},{7,8},{9,10},{11,12},{13,14},{15,16},{17,18},{19... | collective-permute-start | bytes 540680 | tf_op jit(solution)/shard_map/ppermute | solution.py:371
  48.0 8.6 %slice-start.2 = ((s8[10485760]{0:T(1024)(128)(4,1)}), s8[2097152]{0:T(1024)(128)(4,1)S(1)}, s32[]{:S(2)}) async-start(s8[10485760]{0:T(1024)(128)(4,1)} %bitcast.2), calls=%async_computation.2 | async-start | bytes 4194304
  55.1 1.5 %collective-permute-start.6 = (bf16[64,1280]{1,0:T(8,128)(2,1)S(1)}, bf16[64,1280]{1,0:T(8,128)(2,1)S(1)}, u32[]{:S(2)}, u32[]{:S(2)}) collective-permute-start(bf16[64,1280]{1,0:T(8,128)(2,1)S(1)} %norm.1.normed_ref), channel_id=1, source_target_pairs={{0,1},{1,0},{2,3},{3,2},{4,5},{5,4},{6,7},{7,6},{8,9},{9,8},{10,11... | collective-permute-start | bytes 491528 | tf_op jit(solution)/shard_map/ppermute | solution.py:388

commit v5 on v4

--- a/solution.py
+++ b/solution.py
@@ -34,7 +34,6 @@
 
 
 def seed_kernel(
-    reach,
     starts_hbm,
     seeds_hbm,
     tokens_ref,
@@ -43,14 +42,17 @@
     tail_ref,
     share_ref,
     meta_ref,
+    edge_ref,
     starts_ref,
     seeds_ref,
     seed_rows_ref,
     picked,
     index_sems,
     pick_sem,
+    edge_sems,
 ):
     rows, width = tokens_ref.shape
+    reach = edge_ref.shape[0]
     shots, count = seeds_ref.shape
     total = shots * rows
     index = lax.axis_index(AXES)
@@ -63,6 +65,16 @@
     ]
     for copy in indices:
         copy.start()
+    strip_low = jnp.where(second, 0, rows - reach)
+    strip = [
+        pltpu.make_async_copy(
+            tokens_ref.at[pl.ds(pl.multiple_of(strip_low + begin, 8), size), :],
+            edge_ref.at[pl.ds(begin, size), :],
+            edge_sems.at[at],
+        )
+        for at, (begin, size) in enumerate(((0, reach - TILE), (reach - TILE, TILE)))
+    ]
+    strip[0].start()
     for copy in indices:
         copy.wait()
     following = jnp.minimum(index + 1, shots - 1)
@@ -81,6 +93,7 @@
         return carry
 
     lax.fori_loop(0, count, fetch, 0, unroll=8)
+    strip[1].start()
 
     low = jnp.where(second, here - base, 0)
     high = jnp.where(second, rows, after - base)
@@ -125,6 +138,8 @@
     first_ref[...] = jnp.where(split, jnp.where(second, tail, 0.0), own).astype(BF16)
     own_ref[...] = own.astype(BF16)
     tail_ref[...] = tail.astype(BF16)
+    for copy in strip:
+        copy.wait()
 
 
 def copy_pieces(tokens_ref, low, out_ref, sems):
@@ -142,12 +157,6 @@
         copy.start()
     for copy in copies:
         copy.wait()
-
-
-def strip_kernel(tokens_ref, order_ref, out_ref, sems):
-    second = lax.axis_index(AXES) % 2 == 1
-    low = jnp.where(second, 0, tokens_ref.shape[0] - out_ref.shape[0])
-    copy_pieces(tokens_ref, low, out_ref, sems)
 
 
 def load_kernel(tokens_ref, order_ref, out_ref, sems):
@@ -305,17 +314,18 @@
         return pltpu.with_memory_space_constraint(array, pltpu.HBM)
 
     far_tokens = in_hbm(tokens)
-    first, own, tail, share, meta = pl.pallas_call(
-        functools.partial(seed_kernel, reach),
+    first, own, tail, share, meta, edge = pl.pallas_call(
+        seed_kernel,
         out_shape=(
             shape(count, width),
             shape(count, width),
             shape(count, width),
             shape(2, width),
             shape(8, width, dtype=jnp.int32),
+            shape(reach, width),
         ),
         in_specs=[HBM_SPEC] * 3,
-        out_specs=[VMEM_SPEC] * 5,
+        out_specs=[VMEM_SPEC] * 6,
         scratch_shapes=[
             pltpu.SMEM(shot_starts.shape, jnp.int32),
             pltpu.SMEM(seed_offsets.shape, jnp.int32),
@@ -323,6 +333,7 @@
             pltpu.VMEM((16 * count, width), BF16),
             pltpu.SemaphoreType.DMA((3,)),
             pltpu.SemaphoreType.DMA(()),
+            pltpu.SemaphoreType.DMA((2,)),
         ],
         compiler_params=pltpu.CompilerParams(vmem_limit_bytes=16 << 20),
         name="seeds",
@@ -340,7 +351,6 @@
             name=name,
         )(far_tokens, after)
 
-    edge = fetch(strip_kernel, reach, tail, "strip")
     edge, given = lax.optimization_barrier((edge, given))
     edge = lax.ppermute(edge, "feat", pair)
     x = first + given * share[:1]

time: 59.5 us -> 58.6 us (0.985)
  Pallas kernels: 30.6 us -> 28.6 us
  waiting for transfers between devices: 21.8 us -> 23.2 us
    pallas_call x2 -> x1, Pallas kernels: 6.22 us -> 4.1 us  [fetch(): pl.pallas_call(kernel, out_shape=shape(size, width), in_specs=[HBM_SPEC,...]
    ppermute x1, waiting for transfers between devices: 0.01 us -> 1.03 us  [on_device(): given = lax.ppermute(tail, 'feat', pair)]
  transfers between devices with their start and end apart: 7 -> 7, of which waited for: 5 -> 6; matrix products, arithmetic and copies ran while one was open for 0% -> 0% of each run, Pallas kernels for 11% -> 7%
where the time goes in v5:
time: 58.6 us; the launch traced here: 58.4 us
  Pallas kernels  28.6 us (49%)
  waiting for transfers between devices  23.2 us (40%)
  starting transfers between devices  3.76 us (6%)
  matrix products  2.6 us (4%)
    pallas_call x6, Pallas kernels, pool(): pl.pallas_call(functools.partial(pool_kernel, first, ends, devices), out_...  20.4 us
    ppermute x3, waiting for transfers between devices, on_device(): received = lax.ppermute(send, AXES, across)  19.4 us
    pallas_call x1, Pallas kernels, fetch(): pl.pallas_call(kernel, out_shape=shape(size, width), in_specs=[HBM_SPEC,...  4.1 us
    pallas_call x1, Pallas kernels, on_device(): pl.pallas_call(seed_kernel, out_shape=(shape(count, width), shape(count,...  3.83 us
    dot_general x1, matrix products, on_device(): return jnp.dot(both, proj_weight, preferred_element_type=F32).astype(BF16)  2.6 us
    ppermute x1, waiting for transfers between devices, on_device(): received = lax.ppermute(x, AXES, across)  1.39 us
    ppermute x1, waiting for transfers between devices, on_device(): lax.ppermute(normed, 'feat', pair)  1.38 us
    ppermute x1, starting transfers between devices, on_device(): received = lax.ppermute(x, AXES, across)  1.31 us
  transfers between devices with their start and end apart: 7, of which 6 were waited for; matrix products, arithmetic and copies ran while one was open for 0% of the time, Pallas kernels for 7%

profile of v5, /device:TPU:29, one launch (start us, length us, event | category | flops | bytes accessed | tf_op | source)
XLA Modules:
  0.0 58.4 jit_solution(8249244307522770298)
XLA Ops:
  0.0 3.8 %seeds.1 = (bf16[64,1280]{1,0:T(8,128)(2,1)S(1)}, bf16[64,1280]{1,0:T(8,128)(2,1)S(1)}, bf16[64,1280]{1,0:T(8,128)(2,1)S(1)}, bf16[2,1280]{1,0:T(2,128)(2,1)S(1)...) custom-call(s32[32]{0:T(128)} %starts_hbm.1, s32[32,64]{1,0:T(8,128)} %seeds_hbm.1, bf16[4096,1280]{1,0:T(8,128)(2,1)} %tokens_ref.3), custom_call_target="tpu_custom_call" | custom-call | tf_op jit(solution)/shard_map/seeds/pallas_call | solution.py:317
  3.8 0.7 %collective-permute-start = (bf16[64,1280]{1,0:T(8,128)(2,1)S(1)}, bf16[64,1280]{1,0:T(8,128)(2,1)S(1)}, u32[]{:S(2)}, u32[]{:S(2)}) collective-permute-start(bf16[64,1280]{1,0:T(8,128)(2,1)S(1)} %get-tuple-element.31), channel_id=1, source_target_pairs={{0,1},{1,0},{2,3},{3,2},{4,5},{5,4},{6,7},{7,6},{8,9},{9,8},{10,11... | collective-permute-start | bytes 491528 | tf_op jit(solution)/shard_map/ppermute | solution.py:341
  4.6 1.0 %collective-permute-done = bf16[64,1280]{1,0:T(8,128)(2,1)S(1)} collective-permute-done((bf16[64,1280]{1,0:T(8,128)(2,1)S(1)}, bf16[64,1280]{1,0:T(8,128)(2,1)S(1)}, u32[]{:S(2)}, u32[]{:S(2)}) %collective-permute-start) | collective-permute-done | bytes 163872 | tf_op jit(solution)/shard_map/ppermute | solution.py:341
  5.6 0.4 collective-permute-start.1
  6.1 1.3 %collective-permute-start.2 = (bf16[64,1280]{1,0:T(8,128)(2,1)S(1)}, bf16[64,1280]{1,0:T(8,128)(2,1)S(1)}, u32[]{:S(2)}, u32[]{:S(2)}) collective-permute-start(bf16[64,1280]{1,0:T(8,128)(2,1)S(1)} %get-tuple-element.54.order_ref.refs_3_), channel_id=1, source_target_pairs={{1,2},{3,4},{5,6},{7,8},{9,10},{11,12},{13,14},{15,16},{17,18},{19... | collective-permute-start | bytes 491528 | tf_op jit(solution)/shard_map/ppermute | solution.py:358
  7.4 4.1 %load.1.refs_1_ = bf16[4096,1280]{1,0:T(8,128)(2,1)S(1)} custom-call(bf16[4096,1280]{1,0:T(8,128)(2,1)} %tokens_ref.3, bf16[64,1280]{1,0:T(8,128)(2,1)S(1)} %get-tuple-element.54.order_ref.refs_3_), custom_call_target="tpu_custom_call" | custom-call | tf_op jit(solution)/shard_map/load/pallas_call | solution.py:344
  11.5 1.4 %collective-permute-done.2.refs_4_ = bf16[64,1280]{1,0:T(8,128)(2,1)S(1)} collective-permute-done((bf16[64,1280]{1,0:T(8,128)(2,1)S(1)}, bf16[64,1280]{1,0:T(8,128)(2,1)S(1)}, u32[]{:S(2)}, u32[]{:S(2)}) %collective-permute-start.2) | collective-permute-done | bytes 163872 | tf_op jit(solution)/shard_map/ppermute | solution.py:358
  12.9 0.0 collective-permute-done.1.refs_2_
  12.9 6.8 %pool.3 = (f32[128,1280]{1,0:T(8,128)S(1)}, f32[128,128]{1,0:T(8,128)S(1)}, bf16[64,1408]{1,0:T(8,128)(2,1)S(1)}) custom-call(s32[8,1280]{1,0:T(8,128)S(1)} %get-tuple-element.28.refs_0_.meta_ref, bf16[4096,1280]{1,0:T(8,128)(2,1)S(1)} %load.1.refs_1_, bf16[1536,1280]{1,0:T(8,128)(2,1)S(1)} %collective-permute-done.1.refs_2_, ...), custom_call_target="tpu_custom_call" | custom-call | tf_op jit(solution)/shard_map/pool/pallas_call | solution.py:364
  19.6 1.1 %collective-permute-start.3 = (bf16[64,1408]{1,0:T(8,128)(2,1)S(1)}, bf16[64,1408]{1,0:T(8,128)(2,1)S(1)}, u32[]{:S(2)}, u32[]{:S(2)}) collective-permute-start(bf16[64,1408]{1,0:T(8,128)(2,1)S(1)} %get-tuple-element.38), channel_id=1, source_target_pairs={{1,2},{3,4},{5,6},{7,8},{9,10},{11,12},{13,14},{15,16},{17,18},{19... | collective-permute-start | bytes 540680 | tf_op jit(solution)/shard_map/ppermute | solution.py:376
  20.7 5.9 %collective-permute-done.3.refs_5_ = bf16[64,1408]{1,0:T(8,128)(2,1)S(1)} collective-permute-done((bf16[64,1408]{1,0:T(8,128)(2,1)S(1)}, bf16[64,1408]{1,0:T(8,128)(2,1)S(1)}, u32[]{:S(2)}, u32[]{:S(2)}) %collective-permute-start.3) | collective-permute-done | bytes 180256 | tf_op jit(solution)/shard_map/ppermute | solution.py:376
  26.5 6.8 %pool.4 = (f32[128,1280]{1,0:T(8,128)S(1)}, f32[128,128]{1,0:T(8,128)S(1)}, bf16[64,1408]{1,0:T(8,128)(2,1)S(1)}) custom-call(s32[8,1280]{1,0:T(8,128)S(1)} %get-tuple-element.28.refs_0_.meta_ref, bf16[4096,1280]{1,0:T(8,128)(2,1)S(1)} %load.1.refs_1_, bf16[1536,1280]{1,0:T(8,128)(2,1)S(1)} %collective-permute-done.1.refs_2_, ...), custom_call_target="tpu_custom_call" | custom-call | tf_op jit(solution)/shard_map/pool/pallas_call | solution.py:364
  33.3 0.1 collective-permute-start.4
  33.5 0.0 copy-start
  33.5 6.8 %collective-permute-done.4.refs_5_ = bf16[64,1408]{1,0:T(8,128)(2,1)S(1)} collective-permute-done((bf16[64,1408]{1,0:T(8,128)(2,1)S(1)}, bf16[64,1408]{1,0:T(8,128)(2,1)S(1)}, u32[]{:S(2)}, u32[]{:S(2)}) %collective-permute-start.4) | collective-permute-done | bytes 180256 | tf_op jit(solution)/shard_map/ppermute | solution.py:381
  40.3 0.0 slice-start
  40.3 0.0 slice-start.1
  40.3 6.8 %pool.5 = (f32[128,1280]{1,0:T(8,128)S(1)}, f32[128,128]{1,0:T(8,128)S(1)}, bf16[64,1408]{1,0:T(8,128)(2,1)S(1)}) custom-call(s32[8,1280]{1,0:T(8,128)S(1)} %get-tuple-element.28.refs_0_.meta_ref, bf16[4096,1280]{1,0:T(8,128)(2,1)S(1)} %load.1.refs_1_, bf16[1536,1280]{1,0:T(8,128)(2,1)S(1)} %collective-permute-done.1.refs_2_, ...), custom_call_target="tpu_custom_call" | custom-call | tf_op jit(solution)/shard_map/pool/pallas_call | solution.py:364
  47.1 0.1 collective-permute-start.5
  47.2 0.0 copy-done
  47.2 0.0 slice-start.2
  47.2 6.8 %collective-permute-done.5.recv_ref = bf16[64,1408]{1,0:T(8,128)(2,1)S(1)} collective-permute-done((bf16[64,1408]{1,0:T(8,128)(2,1)S(1)}, bf16[64,1408]{1,0:T(8,128)(2,1)S(1)}, u32[]{:S(2)}, u32[]{:S(2)}) %collective-permute-start.5) | collective-permute-done | bytes 180256 | tf_op jit(solution)/shard_map/ppermute | solution.py:381
  54.0 0.3 norm.1.normed_ref
  54.3 0.1 collective-permute-start.6
  54.3 1.4 %collective-permute-done.6.other_ref = bf16[64,1280]{1,0:T(8,128)(2,1)S(1)} collective-permute-done((bf16[64,1280]{1,0:T(8,128)(2,1)S(1)}, bf16[64,1280]{1,0:T(8,128)(2,1)S(1)}, u32[]{:S(2)}, u32[]{:S(2)}) %collective-permute-start.6) | collective-permute-done | bytes 163872 | tf_op jit(solution)/shard_map/ppermute | solution.py:398
  55.8 0.0 slice-done
  55.8 0.0 slice-done.1
  55.8 0.0 slice-done.2
  55.8 2.6 %convolution_convert_fusion = bf16[128,4096]{1,0:T(8,128)(2,1)} fusion(bf16[128,1280]{1,0:T(8,128)(2,1)S(1)} %join.1, bf16[1280,4096]{1,0:T(8,128)(2,1)S(1)} %bitcast.3), kind=kOutput, calls=%fused_computation | convolution fusion | flops 1342701568 | bytes 11862016 | tf_op jit(solution)/shard_map/dot_general | solution.py:399
  (8 shorter events, 0.1 us)
Async XLA Ops:
  3.8 1.8 %collective-permute-start = (bf16[64,1280]{1,0:T(8,128)(2,1)S(1)}, bf16[64,1280]{1,0:T(8,128)(2,1)S(1)}, u32[]{:S(2)}, u32[]{:S(2)}) collective-permute-start(bf16[64,1280]{1,0:T(8,128)(2,1)S(1)} %get-tuple-element.31), channel_id=1, source_target_pairs={{0,1},{1,0},{2,3},{3,2},{4,5},{5,4},{6,7},{7,6},{8,9},{9,8},{10,11... | collective-permute-start | bytes 491528 | tf_op jit(solution)/shard_map/ppermute | solution.py:341
  5.6 7.3 %collective-permute-start.1 = (bf16[1536,1280]{1,0:T(8,128)(2,1)S(1)}, bf16[1536,1280]{1,0:T(8,128)(2,1)S(1)}, u32[]{:S(2)}, u32[]{:S(2)}) collective-permute-start(bf16[1536,1280]{1,0:T(8,128)(2,1)S(1)} %get-tuple-element.34), channel_id=1, source_target_pairs={{0,1},{1,0},{2,3},{3,2},{4,5},{5,4},{6,7},{7,6},{8,9},{9,8},{10,11... | collective-permute-start | bytes 11796488 | tf_op jit(solution)/shard_map/ppermute | solution.py:355
  6.1 6.8 %collective-permute-start.2 = (bf16[64,1280]{1,0:T(8,128)(2,1)S(1)}, bf16[64,1280]{1,0:T(8,128)(2,1)S(1)}, u32[]{:S(2)}, u32[]{:S(2)}) collective-permute-start(bf16[64,1280]{1,0:T(8,128)(2,1)S(1)} %get-tuple-element.54.order_ref.refs_3_), channel_id=1, source_target_pairs={{1,2},{3,4},{5,6},{7,8},{9,10},{11,12},{13,14},{15,16},{17,18},{19... | collective-permute-start | bytes 491528 | tf_op jit(solution)/shard_map/ppermute | solution.py:358
  19.6 6.9 %collective-permute-start.3 = (bf16[64,1408]{1,0:T(8,128)(2,1)S(1)}, bf16[64,1408]{1,0:T(8,128)(2,1)S(1)}, u32[]{:S(2)}, u32[]{:S(2)}) collective-permute-start(bf16[64,1408]{1,0:T(8,128)(2,1)S(1)} %get-tuple-element.38), channel_id=1, source_target_pairs={{1,2},{3,4},{5,6},{7,8},{9,10},{11,12},{13,14},{15,16},{17,18},{19... | collective-permute-start | bytes 540680 | tf_op jit(solution)/shard_map/ppermute | solution.py:376
  33.3 6.9 %collective-permute-start.4 = (bf16[64,1408]{1,0:T(8,128)(2,1)S(1)}, bf16[64,1408]{1,0:T(8,128)(2,1)S(1)}, u32[]{:S(2)}, u32[]{:S(2)}) collective-permute-start(bf16[64,1408]{1,0:T(8,128)(2,1)S(1)} %get-tuple-element.42), channel_id=1, source_target_pairs={{1,2},{3,4},{5,6},{7,8},{9,10},{11,12},{13,14},{15,16},{17,18},{19... | collective-permute-start | bytes 540680 | tf_op jit(solution)/shard_map/ppermute | solution.py:381
  33.5 13.7 %copy-start = (f32[1280]{0:T(1024)S(1)}, f32[1280]{0:T(1024)}, u32[]{:S(2)}) copy-start(f32[1280]{0:T(1024)} %param.8) | copy-start | bytes 15364
  40.3 15.5 %slice-start = ((s8[10485760]{0:T(1024)(128)(4,1)}), s8[4194304]{0:T(1024)(128)(4,1)S(1)}, s32[]{:S(2)}) async-start(s8[10485760]{0:T(1024)(128)(4,1)} %bitcast.2), calls=%async_computation | async-start | bytes 8388608
  40.3 15.5 %slice-start.1 = ((s8[10485760]{0:T(1024)(128)(4,1)}), s8[4194304]{0:T(1024)(128)(4,1)S(1)}, s32[]{:S(2)}) async-start(s8[10485760]{0:T(1024)(128)(4,1)} %bitcast.2), calls=%async_computation.1 | async-start | bytes 8388608
  47.1 6.9 %collective-permute-start.5 = (bf16[64,1408]{1,0:T(8,128)(2,1)S(1)}, bf16[64,1408]{1,0:T(8,128)(2,1)S(1)}, u32[]{:S(2)}, u32[]{:S(2)}) collective-permute-start(bf16[64,1408]{1,0:T(8,128)(2,1)S(1)} %get-tuple-element.45), channel_id=1, source_target_pairs={{1,2},{3,4},{5,6},{7,8},{9,10},{11,12},{13,14},{15,16},{17,18},{19... | collective-permute-start | bytes 540680 | tf_op jit(solution)/shard_map/ppermute | solution.py:381
  47.2 8.6 %slice-start.2 = ((s8[10485760]{0:T(1024)(128)(4,1)}), s8[2097152]{0:T(1024)(128)(4,1)S(1)}, s32[]{:S(2)}) async-start(s8[10485760]{0:T(1024)(128)(4,1)} %bitcast.2), calls=%async_computation.2 | async-start | bytes 4194304
  54.3 1.5 %collective-permute-start.6 = (bf16[64,1280]{1,0:T(8,128)(2,1)S(1)}, bf16[64,1280]{1,0:T(8,128)(2,1)S(1)}, u32[]{:S(2)}, u32[]{:S(2)}) collective-permute-start(bf16[64,1280]{1,0:T(8,128)(2,1)S(1)} %norm.1.normed_ref), channel_id=1, source_target_pairs={{0,1},{1,0},{2,3},{3,2},{4,5},{5,4},{6,7},{7,6},{8,9},{9,8},{10,11... | collective-permute-start | bytes 491528 | tf_op jit(solution)/shard_map/ppermute | solution.py:398

commit v6 on v5

--- a/solution.py
+++ b/solution.py
@@ -172,6 +172,36 @@
     return jnp.sum(block.astype(F32), axis=1, keepdims=True)
 
 
+def on_diagonal(count):
+    shape = (count, LANES)
+    return lax.broadcasted_iota(jnp.int32, shape, 0) == lax.broadcasted_iota(jnp.int32, shape, 1)
+
+
+def pack(sums, mass, out_ref):
+    count, width = sums.shape
+    blocks = width // LANES
+    for at in range(blocks):
+        block = sums[:, at * LANES : (at + 1) * LANES]
+        out_ref[pl.ds(at * count, count), :] = block.astype(BF16)
+    spread = jnp.sum(jnp.where(on_diagonal(count), mass, 0.0), axis=0, keepdims=True)
+    high = spread.astype(BF16).astype(F32)
+    middle = (spread - high).astype(BF16).astype(F32)
+    low = spread - high - middle
+    row = lax.broadcasted_iota(jnp.int32, (8, LANES), 0)
+    terms = jnp.where(row == 0, high, jnp.where(row == 1, middle, jnp.where(row == 2, low, 0.0)))
+    out_ref[pl.ds(blocks * count, 8), :] = terms.astype(BF16)
+
+
+def unpack(packed_ref, count, width):
+    blocks = width // LANES
+    sums = jnp.concatenate(
+        [packed_ref[pl.ds(at * count, count), :].astype(F32) for at in range(blocks)], axis=1
+    )
+    terms = packed_ref[pl.ds(blocks * count, 8), :].astype(F32)
+    total = jnp.sum(terms, axis=0, keepdims=True)
+    return sums, jnp.sum(jnp.where(on_diagonal(count), total, 0.0), axis=1, keepdims=True)
+
+
 def pool_kernel(first, ends, devices, *refs):
     @pl.when(at_end(devices) == ends)
     def _():
@@ -184,7 +214,7 @@
         count, width = y_ref.shape
     else:
         (old_ref, old_mass_ref, recv_ref, _), refs = refs[:4], refs[4:]
-        count, width = recv_ref.shape[0], old_ref.shape[1]
+        count, width = old_ref.shape[0] // 2, old_ref.shape[1]
     sums, masses, *send_out, centroids = refs
     rows = tokens_ref.shape[0]
     reach = edge_ref.shape[0]
@@ -197,8 +227,9 @@
         centroids[x_rows, :] = jnp.where(occupied, joined, jnp.zeros_like(joined))
         centroids[y_rows, :] = y_ref[...]
     else:
-        mass = lane_sum(old_mass_ref[x_rows, :]) + lane_sum(recv_ref[:, width:])
-        joined = (old_ref[x_rows, :] + recv_ref[:, :width].astype(F32)) * (1.0 / mass)
+        other, other_mass = unpack(recv_ref, count, width)
+        mass = lane_sum(old_mass_ref[x_rows, :]) + other_mass
+        joined = (old_ref[x_rows, :] + other) * (1.0 / mass)
         centroids[x_rows, :] = jnp.where(occupied, joined, 0.0).astype(BF16)
         mass = lane_sum(old_mass_ref[y_rows, :])
         centroids[y_rows, :] = (old_ref[y_rows, :] * (1.0 / mass)).astype(BF16)
@@ -252,16 +283,7 @@
     if ends:
         return
     (send_out,) = send_out
-    mass = lane_sum(masses[x_rows, :])
-    send_out[:, :width] = sums[x_rows, :].astype(BF16)
-    high = mass.astype(BF16).astype(F32)
-    middle = (mass - high).astype(BF16).astype(F32)
-    low = mass - high - middle
-    lane = lax.broadcasted_iota(jnp.int32, (count, LANES), 1)
-    block = jnp.where(
-        lane == 0, high, jnp.where(lane == 1, middle, jnp.where(lane == 2, low, 0.0))
-    )
-    send_out[:, width:] = block.astype(BF16)
+    pack(sums[x_rows, :], lane_sum(masses[x_rows, :]), send_out)
 
 
 def norm_kernel(devices, meta_ref, gain_ref, recv_ref, *refs):
@@ -281,8 +303,9 @@
     @pl.when(~at_end(devices))
     def _():
         sums, masses = refs[:2]
-        mass = lane_sum(masses[x_rows, :]) + lane_sum(recv_ref[:, width:])
-        joined = (sums[x_rows, :] + recv_ref[:, :width].astype(F32)) * (1.0 / mass)
+        other, other_mass = unpack(recv_ref, count, width)
+        mass = lane_sum(masses[x_rows, :]) + other_mass
+        joined = (sums[x_rows, :] + other) * (1.0 / mass)
         own = sums[y_rows, :] * (1.0 / lane_sum(masses[y_rows, :]))
         finish(jnp.where(meta_ref[pl.ds(SPLIT, 1), :] != 0, own, joined))
 
@@ -360,7 +383,7 @@
 
     def pool(first, ends, *state):
         outs = (shape(2 * count, width, dtype=F32), shape(2 * count, LANES, dtype=F32))
-        outs += () if ends else (shape(count, width + LANES),)
+        outs += () if ends else (shape(count * width // LANES + 8, LANES),)
         return pl.pallas_call(
             functools.partial(pool_kernel, first, ends, devices),
             out_shape=outs,

time: 58.6 us -> 57.4 us (0.980)
  waiting for transfers between devices: 23.2 us -> 22.3 us
    ppermute x3, waiting for transfers between devices: 19.4 us -> 18.5 us  [on_device(): received = lax.ppermute(send, AXES, across)]
where the time goes in v6:
time: 57.4 us; the launch traced here: 57.2 us
  Pallas kernels  28.4 us (49%)
  waiting for transfers between devices  22.3 us (39%)
  starting transfers between devices  3.74 us (7%)
  matrix products  2.51 us (4%)
    pallas_call x6, Pallas kernels, pool(): pl.pallas_call(functools.partial(pool_kernel, first, ends, devices), out_...  20.2 us
    ppermute x3, waiting for transfers between devices, on_device(): received = lax.ppermute(send, AXES, across)  18.5 us
    pallas_call x1, Pallas kernels, fetch(): pl.pallas_call(kernel, out_shape=shape(size, width), in_specs=[HBM_SPEC,...  4.1 us
    pallas_call x1, Pallas kernels, on_device(): pl.pallas_call(seed_kernel, out_shape=(shape(count, width), shape(count,...  3.83 us
    dot_general x1, matrix products, on_device(): return jnp.dot(both, proj_weight, preferred_element_type=F32).astype(BF16)  2.51 us
    ppermute x1, waiting for transfers between devices, on_device(): received = lax.ppermute(x, AXES, across)  1.4 us
    ppermute x1, waiting for transfers between devices, on_device(): lax.ppermute(normed, 'feat', pair)  1.38 us
    ppermute x1, starting transfers between devices, on_device(): received = lax.ppermute(x, AXES, across)  1.28 us
  transfers between devices with their start and end apart: 7, of which 6 were waited for; matrix products, arithmetic and copies ran while one was open for 0% of the time, Pallas kernels for 7%

profile of v6, /device:TPU:29, one launch (start us, length us, event | category | flops | bytes accessed | tf_op | source)
XLA Modules:
  0.0 57.2 jit_solution(14492632431208396430)
XLA Ops:
  0.0 3.8 %seeds.1 = (bf16[64,1280]{1,0:T(8,128)(2,1)S(1)}, bf16[64,1280]{1,0:T(8,128)(2,1)S(1)}, bf16[64,1280]{1,0:T(8,128)(2,1)S(1)}, bf16[2,1280]{1,0:T(2,128)(2,1)S(1)...) custom-call(s32[32]{0:T(128)} %starts_hbm.1, s32[32,64]{1,0:T(8,128)} %seeds_hbm.1, bf16[4096,1280]{1,0:T(8,128)(2,1)} %tokens_ref.3), custom_call_target="tpu_custom_call" | custom-call | tf_op jit(solution)/shard_map/seeds/pallas_call | solution.py:340
  3.8 0.8 %collective-permute-start = (bf16[64,1280]{1,0:T(8,128)(2,1)S(1)}, bf16[64,1280]{1,0:T(8,128)(2,1)S(1)}, u32[]{:S(2)}, u32[]{:S(2)}) collective-permute-start(bf16[64,1280]{1,0:T(8,128)(2,1)S(1)} %get-tuple-element.31), channel_id=1, source_target_pairs={{0,1},{1,0},{2,3},{3,2},{4,5},{5,4},{6,7},{7,6},{8,9},{9,8},{10,11... | collective-permute-start | bytes 491528 | tf_op jit(solution)/shard_map/ppermute | solution.py:364
  4.6 1.0 %collective-permute-done = bf16[64,1280]{1,0:T(8,128)(2,1)S(1)} collective-permute-done((bf16[64,1280]{1,0:T(8,128)(2,1)S(1)}, bf16[64,1280]{1,0:T(8,128)(2,1)S(1)}, u32[]{:S(2)}, u32[]{:S(2)}) %collective-permute-start) | collective-permute-done | bytes 163872 | tf_op jit(solution)/shard_map/ppermute | solution.py:364
  5.6 0.4 collective-permute-start.1
  6.1 1.3 %collective-permute-start.2 = (bf16[64,1280]{1,0:T(8,128)(2,1)S(1)}, bf16[64,1280]{1,0:T(8,128)(2,1)S(1)}, u32[]{:S(2)}, u32[]{:S(2)}) collective-permute-start(bf16[64,1280]{1,0:T(8,128)(2,1)S(1)} %get-tuple-element.54.order_ref.refs_3_), channel_id=1, source_target_pairs={{1,2},{3,4},{5,6},{7,8},{9,10},{11,12},{13,14},{15,16},{17,18},{19... | collective-permute-start | bytes 491528 | tf_op jit(solution)/shard_map/ppermute | solution.py:381
  7.4 4.1 %load.1.refs_1_ = bf16[4096,1280]{1,0:T(8,128)(2,1)S(1)} custom-call(bf16[4096,1280]{1,0:T(8,128)(2,1)} %tokens_ref.3, bf16[64,1280]{1,0:T(8,128)(2,1)S(1)} %get-tuple-element.54.order_ref.refs_3_), custom_call_target="tpu_custom_call" | custom-call | tf_op jit(solution)/shard_map/load/pallas_call | solution.py:367
  11.5 1.4 %collective-permute-done.2.refs_4_ = bf16[64,1280]{1,0:T(8,128)(2,1)S(1)} collective-permute-done((bf16[64,1280]{1,0:T(8,128)(2,1)S(1)}, bf16[64,1280]{1,0:T(8,128)(2,1)S(1)}, u32[]{:S(2)}, u32[]{:S(2)}) %collective-permute-start.2) | collective-permute-done | bytes 163872 | tf_op jit(solution)/shard_map/ppermute | solution.py:381
  12.9 0.0 collective-permute-done.1.refs_2_
  12.9 6.7 %pool.3 = (f32[128,1280]{1,0:T(8,128)S(1)}, f32[128,128]{1,0:T(8,128)S(1)}, bf16[648,128]{1,0:T(8,128)(2,1)S(1)}) custom-call(s32[8,1280]{1,0:T(8,128)S(1)} %get-tuple-element.28.refs_0_.meta_ref, bf16[4096,1280]{1,0:T(8,128)(2,1)S(1)} %load.1.refs_1_, bf16[1536,1280]{1,0:T(8,128)(2,1)S(1)} %collective-permute-done.1.refs_2_, ...), custom_call_target="tpu_custom_call" | custom-call | tf_op jit(solution)/shard_map/pool/pallas_call | solution.py:387
  19.6 1.1 %collective-permute-start.3 = (bf16[648,128]{1,0:T(8,128)(2,1)S(1)}, bf16[648,128]{1,0:T(8,128)(2,1)S(1)}, u32[]{:S(2)}, u32[]{:S(2)}) collective-permute-start(bf16[648,128]{1,0:T(8,128)(2,1)S(1)} %get-tuple-element.38), channel_id=1, source_target_pairs={{1,2},{3,4},{5,6},{7,8},{9,10},{11,12},{13,14},{15,16},{17,18},{19... | collective-permute-start | bytes 497672 | tf_op jit(solution)/shard_map/ppermute | solution.py:399
  20.6 5.6 %collective-permute-done.3.refs_5_ = bf16[648,128]{1,0:T(8,128)(2,1)S(1)} collective-permute-done((bf16[648,128]{1,0:T(8,128)(2,1)S(1)}, bf16[648,128]{1,0:T(8,128)(2,1)S(1)}, u32[]{:S(2)}, u32[]{:S(2)}) %collective-permute-start.3) | collective-permute-done | bytes 165920 | tf_op jit(solution)/shard_map/ppermute | solution.py:399
  26.2 6.7 %pool.4 = (f32[128,1280]{1,0:T(8,128)S(1)}, f32[128,128]{1,0:T(8,128)S(1)}, bf16[648,128]{1,0:T(8,128)(2,1)S(1)}) custom-call(s32[8,1280]{1,0:T(8,128)S(1)} %get-tuple-element.28.refs_0_.meta_ref, bf16[4096,1280]{1,0:T(8,128)(2,1)S(1)} %load.1.refs_1_, bf16[1536,1280]{1,0:T(8,128)(2,1)S(1)} %collective-permute-done.1.refs_2_, ...), custom_call_target="tpu_custom_call" | custom-call | tf_op jit(solution)/shard_map/pool/pallas_call | solution.py:387
  32.9 0.1 collective-permute-start.4
  33.1 0.0 copy-start
  33.1 6.5 %collective-permute-done.4.refs_5_ = bf16[648,128]{1,0:T(8,128)(2,1)S(1)} collective-permute-done((bf16[648,128]{1,0:T(8,128)(2,1)S(1)}, bf16[648,128]{1,0:T(8,128)(2,1)S(1)}, u32[]{:S(2)}, u32[]{:S(2)}) %collective-permute-start.4) | collective-permute-done | bytes 165920 | tf_op jit(solution)/shard_map/ppermute | solution.py:404
  39.5 0.0 slice-start
  39.5 0.0 slice-start.1
  39.5 6.7 %pool.5 = (f32[128,1280]{1,0:T(8,128)S(1)}, f32[128,128]{1,0:T(8,128)S(1)}, bf16[648,128]{1,0:T(8,128)(2,1)S(1)}) custom-call(s32[8,1280]{1,0:T(8,128)S(1)} %get-tuple-element.28.refs_0_.meta_ref, bf16[4096,1280]{1,0:T(8,128)(2,1)S(1)} %load.1.refs_1_, bf16[1536,1280]{1,0:T(8,128)(2,1)S(1)} %collective-permute-done.1.refs_2_, ...), custom_call_target="tpu_custom_call" | custom-call | tf_op jit(solution)/shard_map/pool/pallas_call | solution.py:387
  46.3 0.1 collective-permute-start.5
  46.4 0.0 copy-done
  46.4 0.0 slice-start.2
  46.4 6.5 %collective-permute-done.5.recv_ref = bf16[648,128]{1,0:T(8,128)(2,1)S(1)} collective-permute-done((bf16[648,128]{1,0:T(8,128)(2,1)S(1)}, bf16[648,128]{1,0:T(8,128)(2,1)S(1)}, u32[]{:S(2)}, u32[]{:S(2)}) %collective-permute-start.5) | collective-permute-done | bytes 165920 | tf_op jit(solution)/shard_map/ppermute | solution.py:404
  52.9 0.3 norm.1.normed_ref
  53.2 0.1 collective-permute-start.6
  53.2 1.4 %collective-permute-done.6.other_ref = bf16[64,1280]{1,0:T(8,128)(2,1)S(1)} collective-permute-done((bf16[64,1280]{1,0:T(8,128)(2,1)S(1)}, bf16[64,1280]{1,0:T(8,128)(2,1)S(1)}, u32[]{:S(2)}, u32[]{:S(2)}) %collective-permute-start.6) | collective-permute-done | bytes 163872 | tf_op jit(solution)/shard_map/ppermute | solution.py:421
  54.7 0.0 slice-done
  54.7 0.0 slice-done.1
  54.7 0.0 slice-done.2
  54.7 2.5 %convolution_convert_fusion = bf16[128,4096]{1,0:T(8,128)(2,1)} fusion(bf16[128,1280]{1,0:T(8,128)(2,1)S(1)} %join.1, bf16[1280,4096]{1,0:T(8,128)(2,1)S(1)} %bitcast.3), kind=kOutput, calls=%fused_computation | convolution fusion | flops 1342701568 | bytes 11862016 | tf_op jit(solution)/shard_map/dot_general | solution.py:422
  (8 shorter events, 0.1 us)
Async XLA Ops:
  3.8 1.8 %collective-permute-start = (bf16[64,1280]{1,0:T(8,128)(2,1)S(1)}, bf16[64,1280]{1,0:T(8,128)(2,1)S(1)}, u32[]{:S(2)}, u32[]{:S(2)}) collective-permute-start(bf16[64,1280]{1,0:T(8,128)(2,1)S(1)} %get-tuple-element.31), channel_id=1, source_target_pairs={{0,1},{1,0},{2,3},{3,2},{4,5},{5,4},{6,7},{7,6},{8,9},{9,8},{10,11... | collective-permute-start | bytes 491528 | tf_op jit(solution)/shard_map/ppermute | solution.py:364
  5.6 7.2 %collective-permute-start.1 = (bf16[1536,1280]{1,0:T(8,128)(2,1)S(1)}, bf16[1536,1280]{1,0:T(8,128)(2,1)S(1)}, u32[]{:S(2)}, u32[]{:S(2)}) collective-permute-start(bf16[1536,1280]{1,0:T(8,128)(2,1)S(1)} %get-tuple-element.34), channel_id=1, source_target_pairs={{0,1},{1,0},{2,3},{3,2},{4,5},{5,4},{6,7},{7,6},{8,9},{9,8},{10,11... | collective-permute-start | bytes 11796488 | tf_op jit(solution)/shard_map/ppermute | solution.py:378
  6.1 6.8 %collective-permute-start.2 = (bf16[64,1280]{1,0:T(8,128)(2,1)S(1)}, bf16[64,1280]{1,0:T(8,128)(2,1)S(1)}, u32[]{:S(2)}, u32[]{:S(2)}) collective-permute-start(bf16[64,1280]{1,0:T(8,128)(2,1)S(1)} %get-tuple-element.54.order_ref.refs_3_), channel_id=1, source_target_pairs={{1,2},{3,4},{5,6},{7,8},{9,10},{11,12},{13,14},{15,16},{17,18},{19... | collective-permute-start | bytes 491528 | tf_op jit(solution)/shard_map/ppermute | solution.py:381
  19.6 6.6 %collective-permute-start.3 = (bf16[648,128]{1,0:T(8,128)(2,1)S(1)}, bf16[648,128]{1,0:T(8,128)(2,1)S(1)}, u32[]{:S(2)}, u32[]{:S(2)}) collective-permute-start(bf16[648,128]{1,0:T(8,128)(2,1)S(1)} %get-tuple-element.38), channel_id=1, source_target_pairs={{1,2},{3,4},{5,6},{7,8},{9,10},{11,12},{13,14},{15,16},{17,18},{19... | collective-permute-start | bytes 497672 | tf_op jit(solution)/shard_map/ppermute | solution.py:399
  32.9 6.6 %collective-permute-start.4 = (bf16[648,128]{1,0:T(8,128)(2,1)S(1)}, bf16[648,128]{1,0:T(8,128)(2,1)S(1)}, u32[]{:S(2)}, u32[]{:S(2)}) collective-permute-start(bf16[648,128]{1,0:T(8,128)(2,1)S(1)} %get-tuple-element.42), channel_id=1, source_target_pairs={{1,2},{3,4},{5,6},{7,8},{9,10},{11,12},{13,14},{15,16},{17,18},{19... | collective-permute-start | bytes 497672 | tf_op jit(solution)/shard_map/ppermute | solution.py:404
  33.1 13.3 %copy-start = (f32[1280]{0:T(1024)S(1)}, f32[1280]{0:T(1024)}, u32[]{:S(2)}) copy-start(f32[1280]{0:T(1024)} %param.8) | copy-start | bytes 15364
  39.5 15.1 %slice-start = ((s8[10485760]{0:T(1024)(128)(4,1)}), s8[4194304]{0:T(1024)(128)(4,1)S(1)}, s32[]{:S(2)}) async-start(s8[10485760]{0:T(1024)(128)(4,1)} %bitcast.2), calls=%async_computation | async-start | bytes 8388608
  39.5 15.1 %slice-start.1 = ((s8[10485760]{0:T(1024)(128)(4,1)}), s8[4194304]{0:T(1024)(128)(4,1)S(1)}, s32[]{:S(2)}) async-start(s8[10485760]{0:T(1024)(128)(4,1)} %bitcast.2), calls=%async_computation.1 | async-start | bytes 8388608
  46.3 6.6 %collective-permute-start.5 = (bf16[648,128]{1,0:T(8,128)(2,1)S(1)}, bf16[648,128]{1,0:T(8,128)(2,1)S(1)}, u32[]{:S(2)}, u32[]{:S(2)}) collective-permute-start(bf16[648,128]{1,0:T(8,128)(2,1)S(1)} %get-tuple-element.45), channel_id=1, source_target_pairs={{1,2},{3,4},{5,6},{7,8},{9,10},{11,12},{13,14},{15,16},{17,18},{19... | collective-permute-start | bytes 497672 | tf_op jit(solution)/shard_map/ppermute | solution.py:404
  46.4 8.3 %slice-start.2 = ((s8[10485760]{0:T(1024)(128)(4,1)}), s8[2097152]{0:T(1024)(128)(4,1)S(1)}, s32[]{:S(2)}) async-start(s8[10485760]{0:T(1024)(128)(4,1)} %bitcast.2), calls=%async_computation.2 | async-start | bytes 4194304
  53.2 1.5 %collective-permute-start.6 = (bf16[64,1280]{1,0:T(8,128)(2,1)S(1)}, bf16[64,1280]{1,0:T(8,128)(2,1)S(1)}, u32[]{:S(2)}, u32[]{:S(2)}) collective-permute-start(bf16[64,1280]{1,0:T(8,128)(2,1)S(1)} %norm.1.normed_ref), channel_id=1, source_target_pairs={{0,1},{1,0},{2,3},{3,2},{4,5},{5,4},{6,7},{7,6},{8,9},{9,8},{10,11... | collective-permute-start | bytes 491528 | tf_op jit(solution)/shard_map/ppermute | solution.py:421

commit v7 on v6

--- a/solution.py
+++ b/solution.py
@@ -37,9 +37,9 @@
     starts_hbm,
     seeds_hbm,
     tokens_ref,
-    first_ref,
-    own_ref,
     tail_ref,
+    near_ref,
+    choose_ref,
     share_ref,
     meta_ref,
     edge_ref,
@@ -48,7 +48,7 @@
     seed_rows_ref,
     picked,
     index_sems,
-    pick_sem,
+    pick_sems,
     edge_sems,
 ):
     rows, width = tokens_ref.shape
@@ -81,18 +81,20 @@
     here = start_of(starts_ref, index, shots, total)
     after = start_of(starts_ref, index + 1, shots, total)
 
-    def fetch(k, carry):
-        for which, (shot, begin) in enumerate(((index, here), (following, after))):
+    sides = ((following, after, picked, pick_sems.at[0]), (index, here, near_ref, pick_sems.at[1]))
+    for shot, begin, rows_ref, sem in sides:
+
+        def fetch(k, carry, shot=shot, begin=begin, rows_ref=rows_ref, sem=sem):
             place = begin + seeds_ref[shot, k] - base
-            slot = pl.multiple_of((which * count + k) * 8, 8)
+            slot = pl.multiple_of(k * 8, 8)
             here_too = (place >= 0) & (place < rows)
             group = pl.multiple_of(jnp.where(here_too, (place // 8) * 8, slot), 8)
             pltpu.make_async_copy(
-                tokens_ref.at[pl.ds(group, 8), :], picked.at[pl.ds(slot, 8), :], pick_sem
+                tokens_ref.at[pl.ds(group, 8), :], rows_ref.at[pl.ds(slot, 8), :], sem
             ).start()
-        return carry
-
-    lax.fori_loop(0, count, fetch, 0, unroll=8)
+            return carry
+
+        lax.fori_loop(0, count, fetch, 0, unroll=8)
     strip[1].start()
 
     low = jnp.where(second, here - base, 0)
@@ -120,26 +122,31 @@
     share_ref[...] = jnp.where(row == 0, jnp.where(split, 0.0, lends), lends).astype(BF16)
 
     choices = []
-    for shot, begin in ((index, here), (following, after)):
+    for shot, begin, _, _ in sides:
         place = column_of(seed_rows_ref[pl.ds(shot, 1), :]) + (begin - base)
         valid = (place >= 0) & (place < rows)
         target = lax.broadcasted_iota(jnp.int32, (count, 1), 0) * 8 + place % 8
         lane = lax.broadcasted_iota(jnp.int32, (count, 8 * count), 1)
         choices.append(jnp.where(valid & (lane == target), 1.0, 0.0).astype(BF16))
-    pltpu.make_async_copy(tokens_ref.at[pl.ds(0, 16 * count), :], picked, pick_sem).wait()
-    own, tail = (
-        jnp.dot(
-            choose,
-            picked[pl.ds(which * 8 * count, 8 * count), :],
-            preferred_element_type=F32,
-        )
-        for which, choose in enumerate(choices)
-    )
+    choose_ref[...] = choices[1]
+    waits = [
+        pltpu.make_async_copy(tokens_ref.at[pl.ds(0, 8 * count), :], rows_ref, sem)
+        for _, _, rows_ref, sem in sides
+    ]
+    waits[0].wait()
+    tail_ref[...] = jnp.dot(choices[0], picked[...], preferred_element_type=F32).astype(BF16)
+    waits[1].wait()
+    for copy in strip:
+        copy.wait()
+
+
+def own_kernel(near_ref, choose_ref, tail_ref, meta_ref, first_ref, own_ref):
+    own = jnp.dot(choose_ref[...], near_ref[...], preferred_element_type=F32)
+    tail = tail_ref[...].astype(F32)
+    second = lax.axis_index(AXES) % 2 == 1
+    split = meta_ref[pl.ds(SPLIT, 1), :] != 0
     first_ref[...] = jnp.where(split, jnp.where(second, tail, 0.0), own).astype(BF16)
     own_ref[...] = own.astype(BF16)
-    tail_ref[...] = tail.astype(BF16)
-    for copy in strip:
-        copy.wait()
 
 
 def copy_pieces(tokens_ref, low, out_ref, sems):
@@ -337,12 +344,12 @@
         return pltpu.with_memory_space_constraint(array, pltpu.HBM)
 
     far_tokens = in_hbm(tokens)
-    first, own, tail, share, meta, edge = pl.pallas_call(
+    tail, near, choose, share, meta, edge = pl.pallas_call(
         seed_kernel,
         out_shape=(
             shape(count, width),
-            shape(count, width),
-            shape(count, width),
+            shape(8 * count, width),
+            shape(count, 8 * count),
             shape(2, width),
             shape(8, width, dtype=jnp.int32),
             shape(reach, width),
@@ -353,15 +360,26 @@
             pltpu.SMEM(shot_starts.shape, jnp.int32),
             pltpu.SMEM(seed_offsets.shape, jnp.int32),
             pltpu.VMEM(seed_offsets.shape, jnp.int32),
-            pltpu.VMEM((16 * count, width), BF16),
+            pltpu.VMEM((8 * count, width), BF16),
             pltpu.SemaphoreType.DMA((3,)),
-            pltpu.SemaphoreType.DMA(()),
+            pltpu.SemaphoreType.DMA((2,)),
             pltpu.SemaphoreType.DMA((2,)),
         ],
         compiler_params=pltpu.CompilerParams(vmem_limit_bytes=16 << 20),
         name="seeds",
     )(in_hbm(shot_starts), in_hbm(seed_offsets), far_tokens)
     given = lax.ppermute(tail, "feat", pair)
+    first, own = pl.pallas_call(
+        own_kernel,
+        out_shape=(shape(count, width), shape(count, width)),
+        in_specs=[VMEM_SPEC] * 4,
+        out_specs=[VMEM_SPEC] * 2,
+        compiler_params=pltpu.CompilerParams(vmem_limit_bytes=8 << 20),
+        cost_estimate=pl.CostEstimate(
+            flops=16 * count * count * width, bytes_accessed=24 * count * width, transcendentals=0
+        ),
+        name="own",
+    )(near, choose, tail, meta)
 
     def fetch(kernel, size, after, name):
         return pl.pallas_call(
@@ -374,7 +392,7 @@
             name=name,
         )(far_tokens, after)
 
-    edge, given = lax.optimization_barrier((edge, given))
+    edge, given, first = lax.optimization_barrier((edge, given, first))
     edge = lax.ppermute(edge, "feat", pair)
     x = first + given * share[:1]
     y = own + given * share[1:]

time: 57.4 us -> 57.5 us (level)
    pallas_call x1 -> x2, Pallas kernels: 3.83 us -> 4.22 us  [the longest x1 3.87 us: on_device(): pl.pallas_call(seed_kernel, out_shape=(shape(count, width), shape(8 * cou...]
  transfers between devices with their start and end apart: 7 -> 7, of which waited for: 6 -> 6; matrix products, arithmetic and copies ran while one was open for 0% -> 0% of each run, Pallas kernels for 7% -> 8%
where the time goes in v7:
time: 57.5 us; the launch traced here: 57.2 us
  Pallas kernels  28.8 us (50%)
  waiting for transfers between devices  21.9 us (38%)
  starting transfers between devices  3.75 us (7%)
  matrix products  2.51 us (4%)
    pallas_call x6, Pallas kernels, pool(): pl.pallas_call(functools.partial(pool_kernel, first, ends, devices), out_...  20.2 us
    ppermute x3, waiting for transfers between devices, on_device(): received = lax.ppermute(send, AXES, across)  18.5 us
    pallas_call x1, Pallas kernels, fetch(): pl.pallas_call(kernel, out_shape=shape(size, width), in_specs=[HBM_SPEC,...  4.1 us
    pallas_call x1, Pallas kernels, on_device(): pl.pallas_call(seed_kernel, out_shape=(shape(count, width), shape(8 * cou...  3.87 us
    dot_general x1, matrix products, on_device(): return jnp.dot(both, proj_weight, preferred_element_type=F32).astype(BF16)  2.51 us
    ppermute x1, waiting for transfers between devices, on_device(): received = lax.ppermute(x, AXES, across)  1.39 us
    ppermute x1, waiting for transfers between devices, on_device(): lax.ppermute(normed, 'feat', pair)  1.38 us
    ppermute x1, starting transfers between devices, on_device(): received = lax.ppermute(x, AXES, across)  1.31 us
  transfers between devices with their start and end apart: 7, of which 6 were waited for; matrix products, arithmetic and copies ran while one was open for 0% of the time, Pallas kernels for 8%

profile of v7, /device:TPU:29, one launch (start us, length us, event | category | flops | bytes accessed | tf_op | source)
XLA Modules:
  0.0 57.2 jit_solution(1223320584860692252)
XLA Ops:
  0.0 3.9 %seeds.1 = (bf16[64,1280]{1,0:T(8,128)(2,1)S(1)}, bf16[512,1280]{1,0:T(8,128)(2,1)S(1)}, bf16[64,512]{1,0:T(8,128)(2,1)S(1)}, bf16[2,1280]{1,0:T(2,128)(2,1)S(1)...) custom-call(s32[32]{0:T(128)} %starts_hbm.1, s32[32,64]{1,0:T(8,128)} %seeds_hbm.1, bf16[4096,1280]{1,0:T(8,128)(2,1)} %tokens_ref.3), custom_call_target="tpu_custom_call" | custom-call | tf_op jit(solution)/shard_map/seeds/pallas_call | solution.py:347
  3.9 0.7 %collective-permute-start = (bf16[64,1280]{1,0:T(8,128)(2,1)S(1)}, bf16[64,1280]{1,0:T(8,128)(2,1)S(1)}, u32[]{:S(2)}, u32[]{:S(2)}) collective-permute-start(bf16[64,1280]{1,0:T(8,128)(2,1)S(1)} %get-tuple-element.33.tail_ref), channel_id=1, source_target_pairs={{0,1},{1,0},{2,3},{3,2},{4,5},{5,4},{6,7},{7,6},{8,9},{9,8},{10,11... | collective-permute-start | bytes 491528 | tf_op jit(solution)/shard_map/ppermute | solution.py:371
  4.6 0.4 own.1
  5.0 0.7 %collective-permute-done = bf16[64,1280]{1,0:T(8,128)(2,1)S(1)} collective-permute-done((bf16[64,1280]{1,0:T(8,128)(2,1)S(1)}, bf16[64,1280]{1,0:T(8,128)(2,1)S(1)}, u32[]{:S(2)}, u32[]{:S(2)}) %collective-permute-start) | collective-permute-done | bytes 163872 | tf_op jit(solution)/shard_map/ppermute | solution.py:371
  5.7 0.4 collective-permute-start.1
  6.1 1.3 %collective-permute-start.2 = (bf16[64,1280]{1,0:T(8,128)(2,1)S(1)}, bf16[64,1280]{1,0:T(8,128)(2,1)S(1)}, u32[]{:S(2)}, u32[]{:S(2)}) collective-permute-start(bf16[64,1280]{1,0:T(8,128)(2,1)S(1)} %get-tuple-element.60.order_ref.refs_3_), channel_id=1, source_target_pairs={{1,2},{3,4},{5,6},{7,8},{9,10},{11,12},{13,14},{15,16},{17,18},{19... | collective-permute-start | bytes 491528 | tf_op jit(solution)/shard_map/ppermute | solution.py:399
  7.4 4.1 %load.1.refs_1_ = bf16[4096,1280]{1,0:T(8,128)(2,1)S(1)} custom-call(bf16[4096,1280]{1,0:T(8,128)(2,1)} %tokens_ref.3, bf16[64,1280]{1,0:T(8,128)(2,1)S(1)} %get-tuple-element.60.order_ref.refs_3_), custom_call_target="tpu_custom_call" | custom-call | tf_op jit(solution)/shard_map/load/pallas_call | solution.py:385
  11.5 1.4 %collective-permute-done.2.refs_4_ = bf16[64,1280]{1,0:T(8,128)(2,1)S(1)} collective-permute-done((bf16[64,1280]{1,0:T(8,128)(2,1)S(1)}, bf16[64,1280]{1,0:T(8,128)(2,1)S(1)}, u32[]{:S(2)}, u32[]{:S(2)}) %collective-permute-start.2) | collective-permute-done | bytes 163872 | tf_op jit(solution)/shard_map/ppermute | solution.py:399
  12.9 0.0 collective-permute-done.1.refs_2_
  12.9 6.7 %pool.3 = (f32[128,1280]{1,0:T(8,128)S(1)}, f32[128,128]{1,0:T(8,128)S(1)}, bf16[648,128]{1,0:T(8,128)(2,1)S(1)}) custom-call(s32[8,1280]{1,0:T(8,128)S(1)} %get-tuple-element.31.meta_ref.refs_0_, bf16[4096,1280]{1,0:T(8,128)(2,1)S(1)} %load.1.refs_1_, bf16[1536,1280]{1,0:T(8,128)(2,1)S(1)} %collective-permute-done.1.refs_2_, ...), custom_call_target="tpu_custom_call" | custom-call | tf_op jit(solution)/shard_map/pool/pallas_call | solution.py:405
  19.6 1.1 %collective-permute-start.3 = (bf16[648,128]{1,0:T(8,128)(2,1)S(1)}, bf16[648,128]{1,0:T(8,128)(2,1)S(1)}, u32[]{:S(2)}, u32[]{:S(2)}) collective-permute-start(bf16[648,128]{1,0:T(8,128)(2,1)S(1)} %get-tuple-element.44), channel_id=1, source_target_pairs={{1,2},{3,4},{5,6},{7,8},{9,10},{11,12},{13,14},{15,16},{17,18},{19... | collective-permute-start | bytes 497672 | tf_op jit(solution)/shard_map/ppermute | solution.py:417
  20.7 5.5 %collective-permute-done.3.refs_5_ = bf16[648,128]{1,0:T(8,128)(2,1)S(1)} collective-permute-done((bf16[648,128]{1,0:T(8,128)(2,1)S(1)}, bf16[648,128]{1,0:T(8,128)(2,1)S(1)}, u32[]{:S(2)}, u32[]{:S(2)}) %collective-permute-start.3) | collective-permute-done | bytes 165920 | tf_op jit(solution)/shard_map/ppermute | solution.py:417
  26.2 6.7 %pool.4 = (f32[128,1280]{1,0:T(8,128)S(1)}, f32[128,128]{1,0:T(8,128)S(1)}, bf16[648,128]{1,0:T(8,128)(2,1)S(1)}) custom-call(s32[8,1280]{1,0:T(8,128)S(1)} %get-tuple-element.31.meta_ref.refs_0_, bf16[4096,1280]{1,0:T(8,128)(2,1)S(1)} %load.1.refs_1_, bf16[1536,1280]{1,0:T(8,128)(2,1)S(1)} %collective-permute-done.1.refs_2_, ...), custom_call_target="tpu_custom_call" | custom-call | tf_op jit(solution)/shard_map/pool/pallas_call | solution.py:405
  33.0 0.1 collective-permute-start.4
  33.1 0.0 copy-start
  33.1 6.5 %collective-permute-done.4.refs_5_ = bf16[648,128]{1,0:T(8,128)(2,1)S(1)} collective-permute-done((bf16[648,128]{1,0:T(8,128)(2,1)S(1)}, bf16[648,128]{1,0:T(8,128)(2,1)S(1)}, u32[]{:S(2)}, u32[]{:S(2)}) %collective-permute-start.4) | collective-permute-done | bytes 165920 | tf_op jit(solution)/shard_map/ppermute | solution.py:422
  39.6 0.0 slice-start
  39.6 0.0 slice-start.1
  39.6 6.7 %pool.5 = (f32[128,1280]{1,0:T(8,128)S(1)}, f32[128,128]{1,0:T(8,128)S(1)}, bf16[648,128]{1,0:T(8,128)(2,1)S(1)}) custom-call(s32[8,1280]{1,0:T(8,128)S(1)} %get-tuple-element.31.meta_ref.refs_0_, bf16[4096,1280]{1,0:T(8,128)(2,1)S(1)} %load.1.refs_1_, bf16[1536,1280]{1,0:T(8,128)(2,1)S(1)} %collective-permute-done.1.refs_2_, ...), custom_call_target="tpu_custom_call" | custom-call | tf_op jit(solution)/shard_map/pool/pallas_call | solution.py:405
  46.3 0.1 collective-permute-start.5
  46.4 0.0 copy-done
  46.4 0.0 slice-start.2
  46.5 6.5 %collective-permute-done.5.recv_ref = bf16[648,128]{1,0:T(8,128)(2,1)S(1)} collective-permute-done((bf16[648,128]{1,0:T(8,128)(2,1)S(1)}, bf16[648,128]{1,0:T(8,128)(2,1)S(1)}, u32[]{:S(2)}, u32[]{:S(2)}) %collective-permute-start.5) | collective-permute-done | bytes 165920 | tf_op jit(solution)/shard_map/ppermute | solution.py:422
  52.9 0.3 norm.1.normed_ref
  53.2 0.1 collective-permute-start.6
  53.3 1.4 %collective-permute-done.6.other_ref = bf16[64,1280]{1,0:T(8,128)(2,1)S(1)} collective-permute-done((bf16[64,1280]{1,0:T(8,128)(2,1)S(1)}, bf16[64,1280]{1,0:T(8,128)(2,1)S(1)}, u32[]{:S(2)}, u32[]{:S(2)}) %collective-permute-start.6) | collective-permute-done | bytes 163872 | tf_op jit(solution)/shard_map/ppermute | solution.py:439
  54.7 0.0 slice-done
  54.7 0.0 slice-done.1
  54.7 0.0 slice-done.2
  54.7 2.5 %convolution_convert_fusion = bf16[128,4096]{1,0:T(8,128)(2,1)} fusion(bf16[128,1280]{1,0:T(8,128)(2,1)S(1)} %join.1, bf16[1280,4096]{1,0:T(8,128)(2,1)S(1)} %bitcast.3), kind=kOutput, calls=%fused_computation | convolution fusion | flops 1342701568 | bytes 11862016 | tf_op jit(solution)/shard_map/dot_general | solution.py:440
  (8 shorter events, 0.1 us)
Async XLA Ops:
  3.9 1.8 %collective-permute-start = (bf16[64,1280]{1,0:T(8,128)(2,1)S(1)}, bf16[64,1280]{1,0:T(8,128)(2,1)S(1)}, u32[]{:S(2)}, u32[]{:S(2)}) collective-permute-start(bf16[64,1280]{1,0:T(8,128)(2,1)S(1)} %get-tuple-element.33.tail_ref), channel_id=1, source_target_pairs={{0,1},{1,0},{2,3},{3,2},{4,5},{5,4},{6,7},{7,6},{8,9},{9,8},{10,11... | collective-permute-start | bytes 491528 | tf_op jit(solution)/shard_map/ppermute | solution.py:371
  5.7 7.3 %collective-permute-start.1 = (bf16[1536,1280]{1,0:T(8,128)(2,1)S(1)}, bf16[1536,1280]{1,0:T(8,128)(2,1)S(1)}, u32[]{:S(2)}, u32[]{:S(2)}) collective-permute-start(bf16[1536,1280]{1,0:T(8,128)(2,1)S(1)} %get-tuple-element.40), channel_id=1, source_target_pairs={{0,1},{1,0},{2,3},{3,2},{4,5},{5,4},{6,7},{7,6},{8,9},{9,8},{10,11... | collective-permute-start | bytes 11796488 | tf_op jit(solution)/shard_map/ppermute | solution.py:396
  6.1 6.8 %collective-permute-start.2 = (bf16[64,1280]{1,0:T(8,128)(2,1)S(1)}, bf16[64,1280]{1,0:T(8,128)(2,1)S(1)}, u32[]{:S(2)}, u32[]{:S(2)}) collective-permute-start(bf16[64,1280]{1,0:T(8,128)(2,1)S(1)} %get-tuple-element.60.order_ref.refs_3_), channel_id=1, source_target_pairs={{1,2},{3,4},{5,6},{7,8},{9,10},{11,12},{13,14},{15,16},{17,18},{19... | collective-permute-start | bytes 491528 | tf_op jit(solution)/shard_map/ppermute | solution.py:399
  19.6 6.6 %collective-permute-start.3 = (bf16[648,128]{1,0:T(8,128)(2,1)S(1)}, bf16[648,128]{1,0:T(8,128)(2,1)S(1)}, u32[]{:S(2)}, u32[]{:S(2)}) collective-permute-start(bf16[648,128]{1,0:T(8,128)(2,1)S(1)} %get-tuple-element.44), channel_id=1, source_target_pairs={{1,2},{3,4},{5,6},{7,8},{9,10},{11,12},{13,14},{15,16},{17,18},{19... | collective-permute-start | bytes 497672 | tf_op jit(solution)/shard_map/ppermute | solution.py:417
  33.0 6.6 %collective-permute-start.4 = (bf16[648,128]{1,0:T(8,128)(2,1)S(1)}, bf16[648,128]{1,0:T(8,128)(2,1)S(1)}, u32[]{:S(2)}, u32[]{:S(2)}) collective-permute-start(bf16[648,128]{1,0:T(8,128)(2,1)S(1)} %get-tuple-element.48), channel_id=1, source_target_pairs={{1,2},{3,4},{5,6},{7,8},{9,10},{11,12},{13,14},{15,16},{17,18},{19... | collective-permute-start | bytes 497672 | tf_op jit(solution)/shard_map/ppermute | solution.py:422
  33.1 13.3 %copy-start = (f32[1280]{0:T(1024)S(1)}, f32[1280]{0:T(1024)}, u32[]{:S(2)}) copy-start(f32[1280]{0:T(1024)} %param.8) | copy-start | bytes 15364
  39.6 15.1 %slice-start = ((s8[10485760]{0:T(1024)(128)(4,1)}), s8[4194304]{0:T(1024)(128)(4,1)S(1)}, s32[]{:S(2)}) async-start(s8[10485760]{0:T(1024)(128)(4,1)} %bitcast.2), calls=%async_computation | async-start | bytes 8388608
  39.6 15.1 %slice-start.1 = ((s8[10485760]{0:T(1024)(128)(4,1)}), s8[4194304]{0:T(1024)(128)(4,1)S(1)}, s32[]{:S(2)}) async-start(s8[10485760]{0:T(1024)(128)(4,1)} %bitcast.2), calls=%async_computation.1 | async-start | bytes 8388608
  46.3 6.6 %collective-permute-start.5 = (bf16[648,128]{1,0:T(8,128)(2,1)S(1)}, bf16[648,128]{1,0:T(8,128)(2,1)S(1)}, u32[]{:S(2)}, u32[]{:S(2)}) collective-permute-start(bf16[648,128]{1,0:T(8,128)(2,1)S(1)} %get-tuple-element.51), channel_id=1, source_target_pairs={{1,2},{3,4},{5,6},{7,8},{9,10},{11,12},{13,14},{15,16},{17,18},{19... | collective-permute-start | bytes 497672 | tf_op jit(solution)/shard_map/ppermute | solution.py:422
  46.4 8.3 %slice-start.2 = ((s8[10485760]{0:T(1024)(128)(4,1)}), s8[2097152]{0:T(1024)(128)(4,1)S(1)}, s32[]{:S(2)}) async-start(s8[10485760]{0:T(1024)(128)(4,1)} %bitcast.2), calls=%async_computation.2 | async-start | bytes 4194304
  53.2 1.5 %collective-permute-start.6 = (bf16[64,1280]{1,0:T(8,128)(2,1)S(1)}, bf16[64,1280]{1,0:T(8,128)(2,1)S(1)}, u32[]{:S(2)}, u32[]{:S(2)}) collective-permute-start(bf16[64,1280]{1,0:T(8,128)(2,1)S(1)} %norm.1.normed_ref), channel_id=1, source_target_pairs={{0,1},{1,0},{2,3},{3,2},{4,5},{5,4},{6,7},{7,6},{8,9},{9,8},{10,11... | collective-permute-start | bytes 491528 | tf_op jit(solution)/shard_map/ppermute | solution.py:439

commit v8 on v7

--- a/solution.py
+++ b/solution.py
@@ -49,7 +49,7 @@
     picked,
     index_sems,
     pick_sems,
-    edge_sems,
+    edge_sem,
 ):
     rows, width = tokens_ref.shape
     reach = edge_ref.shape[0]
@@ -65,16 +65,12 @@
     ]
     for copy in indices:
         copy.start()
-    strip_low = jnp.where(second, 0, rows - reach)
-    strip = [
-        pltpu.make_async_copy(
-            tokens_ref.at[pl.ds(pl.multiple_of(strip_low + begin, 8), size), :],
-            edge_ref.at[pl.ds(begin, size), :],
-            edge_sems.at[at],
-        )
-        for at, (begin, size) in enumerate(((0, reach - TILE), (reach - TILE, TILE)))
-    ]
-    strip[0].start()
+    size = reach - TILE
+    strip_low = pl.multiple_of(jnp.where(second, 0, rows - reach), 8)
+    strip = pltpu.make_async_copy(
+        tokens_ref.at[pl.ds(strip_low, size), :], edge_ref.at[pl.ds(0, size), :], edge_sem
+    )
+    strip.start()
     for copy in indices:
         copy.wait()
     following = jnp.minimum(index + 1, shots - 1)
@@ -95,7 +91,6 @@
             return carry
 
         lax.fori_loop(0, count, fetch, 0, unroll=8)
-    strip[1].start()
 
     low = jnp.where(second, here - base, 0)
     high = jnp.where(second, rows, after - base)
@@ -136,17 +131,36 @@
     waits[0].wait()
     tail_ref[...] = jnp.dot(choices[0], picked[...], preferred_element_type=F32).astype(BF16)
     waits[1].wait()
-    for copy in strip:
-        copy.wait()
-
-
-def own_kernel(near_ref, choose_ref, tail_ref, meta_ref, first_ref, own_ref):
+    strip.wait()
+
+
+def own_kernel(
+    tokens_ref,
+    edge_in_ref,
+    near_ref,
+    choose_ref,
+    tail_ref,
+    meta_ref,
+    first_ref,
+    own_ref,
+    edge_ref,
+    edge_sem,
+):
+    rows, reach = tokens_ref.shape[0], edge_ref.shape[0]
+    begin = jnp.where(lax.axis_index(AXES) % 2 == 1, reach, rows) - TILE
+    strip = pltpu.make_async_copy(
+        tokens_ref.at[pl.ds(pl.multiple_of(begin, 8), TILE), :],
+        edge_ref.at[pl.ds(reach - TILE, TILE), :],
+        edge_sem,
+    )
+    strip.start()
     own = jnp.dot(choose_ref[...], near_ref[...], preferred_element_type=F32)
     tail = tail_ref[...].astype(F32)
     second = lax.axis_index(AXES) % 2 == 1
     split = meta_ref[pl.ds(SPLIT, 1), :] != 0
     first_ref[...] = jnp.where(split, jnp.where(second, tail, 0.0), own).astype(BF16)
     own_ref[...] = own.astype(BF16)
+    strip.wait()
 
 
 def copy_pieces(tokens_ref, low, out_ref, sems):
@@ -363,23 +377,25 @@
             pltpu.VMEM((8 * count, width), BF16),
             pltpu.SemaphoreType.DMA((3,)),
             pltpu.SemaphoreType.DMA((2,)),
-            pltpu.SemaphoreType.DMA((2,)),
+            pltpu.SemaphoreType.DMA(()),
         ],
         compiler_params=pltpu.CompilerParams(vmem_limit_bytes=16 << 20),
         name="seeds",
     )(in_hbm(shot_starts), in_hbm(seed_offsets), far_tokens)
     given = lax.ppermute(tail, "feat", pair)
-    first, own = pl.pallas_call(
+    first, own, edge = pl.pallas_call(
         own_kernel,
-        out_shape=(shape(count, width), shape(count, width)),
-        in_specs=[VMEM_SPEC] * 4,
-        out_specs=[VMEM_SPEC] * 2,
+        out_shape=(shape(count, width), shape(count, width), shape(reach, width)),
+        in_specs=[HBM_SPEC] + [VMEM_SPEC] * 5,
+        out_specs=[VMEM_SPEC] * 3,
+        scratch_shapes=[pltpu.SemaphoreType.DMA(())],
+        input_output_aliases={1: 2},
         compiler_params=pltpu.CompilerParams(vmem_limit_bytes=8 << 20),
         cost_estimate=pl.CostEstimate(
             flops=16 * count * count * width, bytes_accessed=24 * count * width, transcendentals=0
         ),
         name="own",
-    )(near, choose, tail, meta)
+    )(far_tokens, edge, near, choose, tail, meta)
 
     def fetch(kernel, size, after, name):
         return pl.pallas_call(

time: 57.5 us -> 57.5 us (level)
  waiting for transfers between devices: 21.9 us -> 20.8 us
  Pallas kernels: 28.8 us -> 29.4 us
    pallas_call x1, Pallas kernels: 0.35 us -> 1.53 us  [on_device(): pl.pallas_call(own_kernel, out_shape=(shape(count, width), shape(count, w...]
    ppermute x1, waiting for transfers between devices: 0.68 us -> 0.01 us  [on_device(): given = lax.ppermute(tail, 'feat', pair)]
    pallas_call x1, Pallas kernels: 3.87 us -> 3.24 us  [on_device(): pl.pallas_call(seed_kernel, out_shape=(shape(count, width), shape(8 * cou...]
  transfers between devices with their start and end apart: 7 -> 7, of which waited for: 6 -> 5; matrix products, arithmetic and copies ran while one was open for 0% -> 0% of each run, Pallas kernels for 8% -> 10%
where the time goes in v8:
time: 57.5 us; the launch traced here: 57 us
  Pallas kernels  29.4 us (51%)
  waiting for transfers between devices  20.8 us (36%)
  starting transfers between devices  4.01 us (7%)
  matrix products  2.51 us (4%)
    pallas_call x6, Pallas kernels, pool(): pl.pallas_call(functools.partial(pool_kernel, first, ends, devices), out_...  20.2 us
    ppermute x3, waiting for transfers between devices, on_device(): received = lax.ppermute(send, AXES, across)  18.4 us
    pallas_call x1, Pallas kernels, fetch(): pl.pallas_call(kernel, out_shape=shape(size, width), in_specs=[HBM_SPEC,...  4.1 us
    pallas_call x1, Pallas kernels, on_device(): pl.pallas_call(seed_kernel, out_shape=(shape(count, width), shape(8 * cou...  3.24 us
    dot_general x1, matrix products, on_device(): return jnp.dot(both, proj_weight, preferred_element_type=F32).astype(BF16)  2.51 us
    ppermute x1, starting transfers between devices, on_device(): received = lax.ppermute(x, AXES, across)  1.66 us
    pallas_call x1, Pallas kernels, on_device(): pl.pallas_call(own_kernel, out_shape=(shape(count, width), shape(count, w...  1.53 us
    ppermute x3, starting transfers between devices, on_device(): received = lax.ppermute(send, AXES, across)  1.46 us
  transfers between devices with their start and end apart: 7, of which 5 were waited for; matrix products, arithmetic and copies ran while one was open for 0% of the time, Pallas kernels for 10%

profile of v8, /device:TPU:29, one launch (start us, length us, event | category | flops | bytes accessed | tf_op | source)
XLA Modules:
  0.0 57.0 jit_solution(5325441170579163117)
XLA Ops:
  0.0 3.2 %seeds.1 = (bf16[64,1280]{1,0:T(8,128)(2,1)S(1)}, bf16[512,1280]{1,0:T(8,128)(2,1)S(1)}, bf16[64,512]{1,0:T(8,128)(2,1)S(1)}, bf16[2,1280]{1,0:T(2,128)(2,1)S(1)...) custom-call(s32[32]{0:T(128)} %starts_hbm.1, s32[32,64]{1,0:T(8,128)} %seeds_hbm.1, bf16[4096,1280]{1,0:T(8,128)(2,1)} %tokens_ref.5), custom_call_target="tpu_custom_call" | custom-call | tf_op jit(solution)/shard_map/seeds/pallas_call | solution.py:361
  3.3 0.7 %collective-permute-start = (bf16[64,1280]{1,0:T(8,128)(2,1)S(1)}, bf16[64,1280]{1,0:T(8,128)(2,1)S(1)}, u32[]{:S(2)}, u32[]{:S(2)}) collective-permute-start(bf16[64,1280]{1,0:T(8,128)(2,1)S(1)} %get-tuple-element.36.tail_ref), channel_id=1, source_target_pairs={{0,1},{1,0},{2,3},{3,2},{4,5},{5,4},{6,7},{7,6},{8,9},{9,8},{10,11... | collective-permute-start | bytes 491528 | tf_op jit(solution)/shard_map/ppermute | solution.py:385
  4.0 1.5 %own.1 = (bf16[64,1280]{1,0:T(8,128)(2,1)S(1)}, bf16[64,1280]{1,0:T(8,128)(2,1)S(1)}, bf16[1536,1280]{1,0:T(8,128)(2,1)S(1)}) custom-call(bf16[4096,1280]{1,0:T(8,128)(2,1)} %tokens_ref.5, bf16[1536,1280]{1,0:T(8,128)(2,1)S(1)} %get-tuple-element.33.edge_in_ref, bf16[512,1280]{1,0:T(8,128)(2,1)S(1)} %get-tuple-element.34.near_ref, ...), custom_call_target="tpu_custom_call", output_to_operand_aliasing={{2}: (1, {})} | custom-call | flops 83886080 | bytes 1966080 | tf_op jit(solution)/shard_map/own/pallas_call | solution.py:386
  5.5 0.0 collective-permute-done
  5.5 0.1 collective-permute-start.1
  5.7 1.7 %collective-permute-start.2 = (bf16[64,1280]{1,0:T(8,128)(2,1)S(1)}, bf16[64,1280]{1,0:T(8,128)(2,1)S(1)}, u32[]{:S(2)}, u32[]{:S(2)}) collective-permute-start(bf16[64,1280]{1,0:T(8,128)(2,1)S(1)} %get-tuple-element.62.order_ref.refs_3_), channel_id=1, source_target_pairs={{1,2},{3,4},{5,6},{7,8},{9,10},{11,12},{13,14},{15,16},{17,18},{19... | collective-permute-start | bytes 491528 | tf_op jit(solution)/shard_map/ppermute | solution.py:415
  7.4 4.1 %load.1.refs_1_ = bf16[4096,1280]{1,0:T(8,128)(2,1)S(1)} custom-call(bf16[4096,1280]{1,0:T(8,128)(2,1)} %tokens_ref.5, bf16[64,1280]{1,0:T(8,128)(2,1)S(1)} %get-tuple-element.62.order_ref.refs_3_), custom_call_target="tpu_custom_call" | custom-call | tf_op jit(solution)/shard_map/load/pallas_call | solution.py:401
  11.5 1.0 %collective-permute-done.2.refs_4_ = bf16[64,1280]{1,0:T(8,128)(2,1)S(1)} collective-permute-done((bf16[64,1280]{1,0:T(8,128)(2,1)S(1)}, bf16[64,1280]{1,0:T(8,128)(2,1)S(1)}, u32[]{:S(2)}, u32[]{:S(2)}) %collective-permute-start.2) | collective-permute-done | bytes 163872 | tf_op jit(solution)/shard_map/ppermute | solution.py:415
  12.5 0.0 collective-permute-done.1.refs_2_
  12.5 6.7 %pool.3 = (f32[128,1280]{1,0:T(8,128)S(1)}, f32[128,128]{1,0:T(8,128)S(1)}, bf16[648,128]{1,0:T(8,128)(2,1)S(1)}) custom-call(s32[8,1280]{1,0:T(8,128)S(1)} %get-tuple-element.32.meta_ref.refs_0_, bf16[4096,1280]{1,0:T(8,128)(2,1)S(1)} %load.1.refs_1_, bf16[1536,1280]{1,0:T(8,128)(2,1)S(1)} %collective-permute-done.1.refs_2_, ...), custom_call_target="tpu_custom_call" | custom-call | tf_op jit(solution)/shard_map/pool/pallas_call | solution.py:421
  19.2 1.3 %collective-permute-start.3 = (bf16[648,128]{1,0:T(8,128)(2,1)S(1)}, bf16[648,128]{1,0:T(8,128)(2,1)S(1)}, u32[]{:S(2)}, u32[]{:S(2)}) collective-permute-start(bf16[648,128]{1,0:T(8,128)(2,1)S(1)} %get-tuple-element.46), channel_id=1, source_target_pairs={{1,2},{3,4},{5,6},{7,8},{9,10},{11,12},{13,14},{15,16},{17,18},{19... | collective-permute-start | bytes 497672 | tf_op jit(solution)/shard_map/ppermute | solution.py:433
  20.5 5.4 %collective-permute-done.3.refs_5_ = bf16[648,128]{1,0:T(8,128)(2,1)S(1)} collective-permute-done((bf16[648,128]{1,0:T(8,128)(2,1)S(1)}, bf16[648,128]{1,0:T(8,128)(2,1)S(1)}, u32[]{:S(2)}, u32[]{:S(2)}) %collective-permute-start.3) | collective-permute-done | bytes 165920 | tf_op jit(solution)/shard_map/ppermute | solution.py:433
  25.9 6.8 %pool.4 = (f32[128,1280]{1,0:T(8,128)S(1)}, f32[128,128]{1,0:T(8,128)S(1)}, bf16[648,128]{1,0:T(8,128)(2,1)S(1)}) custom-call(s32[8,1280]{1,0:T(8,128)S(1)} %get-tuple-element.32.meta_ref.refs_0_, bf16[4096,1280]{1,0:T(8,128)(2,1)S(1)} %load.1.refs_1_, bf16[1536,1280]{1,0:T(8,128)(2,1)S(1)} %collective-permute-done.1.refs_2_, ...), custom_call_target="tpu_custom_call" | custom-call | tf_op jit(solution)/shard_map/pool/pallas_call | solution.py:421
  32.7 0.1 collective-permute-start.4
  32.8 0.0 copy-start
  32.8 6.5 %collective-permute-done.4.refs_5_ = bf16[648,128]{1,0:T(8,128)(2,1)S(1)} collective-permute-done((bf16[648,128]{1,0:T(8,128)(2,1)S(1)}, bf16[648,128]{1,0:T(8,128)(2,1)S(1)}, u32[]{:S(2)}, u32[]{:S(2)}) %collective-permute-start.4) | collective-permute-done | bytes 165920 | tf_op jit(solution)/shard_map/ppermute | solution.py:438
  39.3 0.0 slice-start
  39.3 0.0 slice-start.1
  39.3 6.7 %pool.5 = (f32[128,1280]{1,0:T(8,128)S(1)}, f32[128,128]{1,0:T(8,128)S(1)}, bf16[648,128]{1,0:T(8,128)(2,1)S(1)}) custom-call(s32[8,1280]{1,0:T(8,128)S(1)} %get-tuple-element.32.meta_ref.refs_0_, bf16[4096,1280]{1,0:T(8,128)(2,1)S(1)} %load.1.refs_1_, bf16[1536,1280]{1,0:T(8,128)(2,1)S(1)} %collective-permute-done.1.refs_2_, ...), custom_call_target="tpu_custom_call" | custom-call | tf_op jit(solution)/shard_map/pool/pallas_call | solution.py:421
  46.1 0.1 collective-permute-start.5
  46.1 0.0 copy-done
  46.2 0.0 slice-start.2
  46.2 6.5 %collective-permute-done.5.recv_ref = bf16[648,128]{1,0:T(8,128)(2,1)S(1)} collective-permute-done((bf16[648,128]{1,0:T(8,128)(2,1)S(1)}, bf16[648,128]{1,0:T(8,128)(2,1)S(1)}, u32[]{:S(2)}, u32[]{:S(2)}) %collective-permute-start.5) | collective-permute-done | bytes 165920 | tf_op jit(solution)/shard_map/ppermute | solution.py:438
  52.7 0.3 norm.1.normed_ref
  52.9 0.1 collective-permute-start.6
  53.0 1.4 %collective-permute-done.6.other_ref = bf16[64,1280]{1,0:T(8,128)(2,1)S(1)} collective-permute-done((bf16[64,1280]{1,0:T(8,128)(2,1)S(1)}, bf16[64,1280]{1,0:T(8,128)(2,1)S(1)}, u32[]{:S(2)}, u32[]{:S(2)}) %collective-permute-start.6) | collective-permute-done | bytes 163872 | tf_op jit(solution)/shard_map/ppermute | solution.py:455
  54.4 0.0 slice-done
  54.4 0.0 slice-done.1
  54.5 0.0 slice-done.2
  54.5 2.5 %convolution_convert_fusion = bf16[128,4096]{1,0:T(8,128)(2,1)} fusion(bf16[128,1280]{1,0:T(8,128)(2,1)S(1)} %join.1, bf16[1280,4096]{1,0:T(8,128)(2,1)S(1)} %bitcast.3), kind=kOutput, calls=%fused_computation | convolution fusion | flops 1342701568 | bytes 11862016 | tf_op jit(solution)/shard_map/dot_general | solution.py:456
  (8 shorter events, 0.1 us)
Async XLA Ops:
  3.3 2.3 %collective-permute-start = (bf16[64,1280]{1,0:T(8,128)(2,1)S(1)}, bf16[64,1280]{1,0:T(8,128)(2,1)S(1)}, u32[]{:S(2)}, u32[]{:S(2)}) collective-permute-start(bf16[64,1280]{1,0:T(8,128)(2,1)S(1)} %get-tuple-element.36.tail_ref), channel_id=1, source_target_pairs={{0,1},{1,0},{2,3},{3,2},{4,5},{5,4},{6,7},{7,6},{8,9},{9,8},{10,11... | collective-permute-start | bytes 491528 | tf_op jit(solution)/shard_map/ppermute | solution.py:385
  5.5 7.0 %collective-permute-start.1 = (bf16[1536,1280]{1,0:T(8,128)(2,1)S(1)}, bf16[1536,1280]{1,0:T(8,128)(2,1)S(1)}, u32[]{:S(2)}, u32[]{:S(2)}) collective-permute-start(bf16[1536,1280]{1,0:T(8,128)(2,1)S(1)} %get-tuple-element.42), channel_id=1, source_target_pairs={{0,1},{1,0},{2,3},{3,2},{4,5},{5,4},{6,7},{7,6},{8,9},{9,8},{10,11... | collective-permute-start | bytes 11796488 | tf_op jit(solution)/shard_map/ppermute | solution.py:412
  5.7 6.8 %collective-permute-start.2 = (bf16[64,1280]{1,0:T(8,128)(2,1)S(1)}, bf16[64,1280]{1,0:T(8,128)(2,1)S(1)}, u32[]{:S(2)}, u32[]{:S(2)}) collective-permute-start(bf16[64,1280]{1,0:T(8,128)(2,1)S(1)} %get-tuple-element.62.order_ref.refs_3_), channel_id=1, source_target_pairs={{1,2},{3,4},{5,6},{7,8},{9,10},{11,12},{13,14},{15,16},{17,18},{19... | collective-permute-start | bytes 491528 | tf_op jit(solution)/shard_map/ppermute | solution.py:415
  19.2 6.7 %collective-permute-start.3 = (bf16[648,128]{1,0:T(8,128)(2,1)S(1)}, bf16[648,128]{1,0:T(8,128)(2,1)S(1)}, u32[]{:S(2)}, u32[]{:S(2)}) collective-permute-start(bf16[648,128]{1,0:T(8,128)(2,1)S(1)} %get-tuple-element.46), channel_id=1, source_target_pairs={{1,2},{3,4},{5,6},{7,8},{9,10},{11,12},{13,14},{15,16},{17,18},{19... | collective-permute-start | bytes 497672 | tf_op jit(solution)/shard_map/ppermute | solution.py:433
  32.7 6.6 %collective-permute-start.4 = (bf16[648,128]{1,0:T(8,128)(2,1)S(1)}, bf16[648,128]{1,0:T(8,128)(2,1)S(1)}, u32[]{:S(2)}, u32[]{:S(2)}) collective-permute-start(bf16[648,128]{1,0:T(8,128)(2,1)S(1)} %get-tuple-element.50), channel_id=1, source_target_pairs={{1,2},{3,4},{5,6},{7,8},{9,10},{11,12},{13,14},{15,16},{17,18},{19... | collective-permute-start | bytes 497672 | tf_op jit(solution)/shard_map/ppermute | solution.py:438
  32.8 13.3 %copy-start = (f32[1280]{0:T(1024)S(1)}, f32[1280]{0:T(1024)}, u32[]{:S(2)}) copy-start(f32[1280]{0:T(1024)} %param.8) | copy-start | bytes 15364
  39.3 15.1 %slice-start = ((s8[10485760]{0:T(1024)(128)(4,1)}), s8[4194304]{0:T(1024)(128)(4,1)S(1)}, s32[]{:S(2)}) async-start(s8[10485760]{0:T(1024)(128)(4,1)} %bitcast.2), calls=%async_computation | async-start | bytes 8388608
  39.3 15.1 %slice-start.1 = ((s8[10485760]{0:T(1024)(128)(4,1)}), s8[4194304]{0:T(1024)(128)(4,1)S(1)}, s32[]{:S(2)}) async-start(s8[10485760]{0:T(1024)(128)(4,1)} %bitcast.2), calls=%async_computation.1 | async-start | bytes 8388608
  46.1 6.6 %collective-permute-start.5 = (bf16[648,128]{1,0:T(8,128)(2,1)S(1)}, bf16[648,128]{1,0:T(8,128)(2,1)S(1)}, u32[]{:S(2)}, u32[]{:S(2)}) collective-permute-start(bf16[648,128]{1,0:T(8,128)(2,1)S(1)} %get-tuple-element.53), channel_id=1, source_target_pairs={{1,2},{3,4},{5,6},{7,8},{9,10},{11,12},{13,14},{15,16},{17,18},{19... | collective-permute-start | bytes 497672 | tf_op jit(solution)/shard_map/ppermute | solution.py:438
  46.2 8.3 %slice-start.2 = ((s8[10485760]{0:T(1024)(128)(4,1)}), s8[2097152]{0:T(1024)(128)(4,1)S(1)}, s32[]{:S(2)}) async-start(s8[10485760]{0:T(1024)(128)(4,1)} %bitcast.2), calls=%async_computation.2 | async-start | bytes 4194304
  52.9 1.5 %collective-permute-start.6 = (bf16[64,1280]{1,0:T(8,128)(2,1)S(1)}, bf16[64,1280]{1,0:T(8,128)(2,1)S(1)}, u32[]{:S(2)}, u32[]{:S(2)}) collective-permute-start(bf16[64,1280]{1,0:T(8,128)(2,1)S(1)} %norm.1.normed_ref), channel_id=1, source_target_pairs={{0,1},{1,0},{2,3},{3,2},{4,5},{5,4},{6,7},{7,6},{8,9},{9,8},{10,11... | collective-permute-start | bytes 491528 | tf_op jit(solution)/shard_map/ppermute | solution.py:455

commit v9 on v8

--- a/solution.py
+++ b/solution.py
@@ -12,6 +12,7 @@
 AXES = ("seq", "feat")
 LANES = 128
 TILE = 512
+LATE = TILE // 2
 F32 = jnp.float32
 BF16 = jnp.bfloat16
 VMEM_SPEC = pl.BlockSpec(memory_space=pltpu.VMEM)
@@ -65,7 +66,7 @@
     ]
     for copy in indices:
         copy.start()
-    size = reach - TILE
+    size = reach - LATE
     strip_low = pl.multiple_of(jnp.where(second, 0, rows - reach), 8)
     strip = pltpu.make_async_copy(
         tokens_ref.at[pl.ds(strip_low, size), :], edge_ref.at[pl.ds(0, size), :], edge_sem
@@ -147,10 +148,10 @@
     edge_sem,
 ):
     rows, reach = tokens_ref.shape[0], edge_ref.shape[0]
-    begin = jnp.where(lax.axis_index(AXES) % 2 == 1, reach, rows) - TILE
+    begin = jnp.where(lax.axis_index(AXES) % 2 == 1, reach, rows) - LATE
     strip = pltpu.make_async_copy(
-        tokens_ref.at[pl.ds(pl.multiple_of(begin, 8), TILE), :],
-        edge_ref.at[pl.ds(reach - TILE, TILE), :],
+        tokens_ref.at[pl.ds(pl.multiple_of(begin, 8), LATE), :],
+        edge_ref.at[pl.ds(reach - LATE, LATE), :],
         edge_sem,
     )
     strip.start()

time: 57.5 us -> 57.4 us (level)
  no operation moved by 1% of the time
where the time goes in v9:
time: 57.4 us; the launch traced here: 56.8 us
  Pallas kernels  29.2 us (51%)
  waiting for transfers between devices  20.8 us (36%)
  starting transfers between devices  3.99 us (7%)
  matrix products  2.51 us (4%)
    pallas_call x6, Pallas kernels, pool(): pl.pallas_call(functools.partial(pool_kernel, first, ends, devices), out_...  20.2 us
    ppermute x3, waiting for transfers between devices, on_device(): received = lax.ppermute(send, AXES, across)  18.4 us
    pallas_call x1, Pallas kernels, fetch(): pl.pallas_call(kernel, out_shape=shape(size, width), in_specs=[HBM_SPEC,...  4.1 us
    pallas_call x1, Pallas kernels, on_device(): pl.pallas_call(seed_kernel, out_shape=(shape(count, width), shape(8 * cou...  3.31 us
    dot_general x1, matrix products, on_device(): return jnp.dot(both, proj_weight, preferred_element_type=F32).astype(BF16)  2.51 us
    ppermute x1, starting transfers between devices, on_device(): received = lax.ppermute(x, AXES, across)  1.65 us
    ppermute x3, starting transfers between devices, on_device(): received = lax.ppermute(send, AXES, across)  1.45 us
    ppermute x1, waiting for transfers between devices, on_device(): lax.ppermute(normed, 'feat', pair)  1.38 us
  transfers between devices with their start and end apart: 7, of which 5 were waited for; matrix products, arithmetic and copies ran while one was open for 0% of the time, Pallas kernels for 10%

profile of v9, /device:TPU:29, one launch (start us, length us, event | category | flops | bytes accessed | tf_op | source)
XLA Modules:
  0.0 56.8 jit_solution(8448905190468137232)
XLA Ops:
  0.0 3.3 %seeds.1 = (bf16[64,1280]{1,0:T(8,128)(2,1)S(1)}, bf16[512,1280]{1,0:T(8,128)(2,1)S(1)}, bf16[64,512]{1,0:T(8,128)(2,1)S(1)}, bf16[2,1280]{1,0:T(2,128)(2,1)S(1)...) custom-call(s32[32]{0:T(128)} %starts_hbm.1, s32[32,64]{1,0:T(8,128)} %seeds_hbm.1, bf16[4096,1280]{1,0:T(8,128)(2,1)} %tokens_ref.5), custom_call_target="tpu_custom_call" | custom-call | tf_op jit(solution)/shard_map/seeds/pallas_call | solution.py:362
  3.3 0.7 %collective-permute-start = (bf16[64,1280]{1,0:T(8,128)(2,1)S(1)}, bf16[64,1280]{1,0:T(8,128)(2,1)S(1)}, u32[]{:S(2)}, u32[]{:S(2)}) collective-permute-start(bf16[64,1280]{1,0:T(8,128)(2,1)S(1)} %get-tuple-element.36.tail_ref), channel_id=1, source_target_pairs={{0,1},{1,0},{2,3},{3,2},{4,5},{5,4},{6,7},{7,6},{8,9},{9,8},{10,11... | collective-permute-start | bytes 491528 | tf_op jit(solution)/shard_map/ppermute | solution.py:386
  4.1 1.3 %own.1 = (bf16[64,1280]{1,0:T(8,128)(2,1)S(1)}, bf16[64,1280]{1,0:T(8,128)(2,1)S(1)}, bf16[1536,1280]{1,0:T(8,128)(2,1)S(1)}) custom-call(bf16[4096,1280]{1,0:T(8,128)(2,1)} %tokens_ref.5, bf16[1536,1280]{1,0:T(8,128)(2,1)S(1)} %get-tuple-element.33.edge_in_ref, bf16[512,1280]{1,0:T(8,128)(2,1)S(1)} %get-tuple-element.34.near_ref, ...), custom_call_target="tpu_custom_call", output_to_operand_aliasing={{2}: (1, {})} | custom-call | flops 83886080 | bytes 1966080 | tf_op jit(solution)/shard_map/own/pallas_call | solution.py:387
  5.4 0.0 collective-permute-done
  5.4 0.1 collective-permute-start.1
  5.5 1.7 %collective-permute-start.2 = (bf16[64,1280]{1,0:T(8,128)(2,1)S(1)}, bf16[64,1280]{1,0:T(8,128)(2,1)S(1)}, u32[]{:S(2)}, u32[]{:S(2)}) collective-permute-start(bf16[64,1280]{1,0:T(8,128)(2,1)S(1)} %get-tuple-element.62.order_ref.refs_3_), channel_id=1, source_target_pairs={{1,2},{3,4},{5,6},{7,8},{9,10},{11,12},{13,14},{15,16},{17,18},{19... | collective-permute-start | bytes 491528 | tf_op jit(solution)/shard_map/ppermute | solution.py:416
  7.2 4.1 %load.1.refs_1_ = bf16[4096,1280]{1,0:T(8,128)(2,1)S(1)} custom-call(bf16[4096,1280]{1,0:T(8,128)(2,1)} %tokens_ref.5, bf16[64,1280]{1,0:T(8,128)(2,1)S(1)} %get-tuple-element.62.order_ref.refs_3_), custom_call_target="tpu_custom_call" | custom-call | tf_op jit(solution)/shard_map/load/pallas_call | solution.py:402
  11.3 1.0 %collective-permute-done.2.refs_4_ = bf16[64,1280]{1,0:T(8,128)(2,1)S(1)} collective-permute-done((bf16[64,1280]{1,0:T(8,128)(2,1)S(1)}, bf16[64,1280]{1,0:T(8,128)(2,1)S(1)}, u32[]{:S(2)}, u32[]{:S(2)}) %collective-permute-start.2) | collective-permute-done | bytes 163872 | tf_op jit(solution)/shard_map/ppermute | solution.py:416
  12.4 0.0 collective-permute-done.1.refs_2_
  12.4 6.7 %pool.3 = (f32[128,1280]{1,0:T(8,128)S(1)}, f32[128,128]{1,0:T(8,128)S(1)}, bf16[648,128]{1,0:T(8,128)(2,1)S(1)}) custom-call(s32[8,1280]{1,0:T(8,128)S(1)} %get-tuple-element.32.meta_ref.refs_0_, bf16[4096,1280]{1,0:T(8,128)(2,1)S(1)} %load.1.refs_1_, bf16[1536,1280]{1,0:T(8,128)(2,1)S(1)} %collective-permute-done.1.refs_2_, ...), custom_call_target="tpu_custom_call" | custom-call | tf_op jit(solution)/shard_map/pool/pallas_call | solution.py:422
  19.1 1.3 %collective-permute-start.3 = (bf16[648,128]{1,0:T(8,128)(2,1)S(1)}, bf16[648,128]{1,0:T(8,128)(2,1)S(1)}, u32[]{:S(2)}, u32[]{:S(2)}) collective-permute-start(bf16[648,128]{1,0:T(8,128)(2,1)S(1)} %get-tuple-element.46), channel_id=1, source_target_pairs={{1,2},{3,4},{5,6},{7,8},{9,10},{11,12},{13,14},{15,16},{17,18},{19... | collective-permute-start | bytes 497672 | tf_op jit(solution)/shard_map/ppermute | solution.py:434
  20.3 5.5 %collective-permute-done.3.refs_5_ = bf16[648,128]{1,0:T(8,128)(2,1)S(1)} collective-permute-done((bf16[648,128]{1,0:T(8,128)(2,1)S(1)}, bf16[648,128]{1,0:T(8,128)(2,1)S(1)}, u32[]{:S(2)}, u32[]{:S(2)}) %collective-permute-start.3) | collective-permute-done | bytes 165920 | tf_op jit(solution)/shard_map/ppermute | solution.py:434
  25.8 6.8 %pool.4 = (f32[128,1280]{1,0:T(8,128)S(1)}, f32[128,128]{1,0:T(8,128)S(1)}, bf16[648,128]{1,0:T(8,128)(2,1)S(1)}) custom-call(s32[8,1280]{1,0:T(8,128)S(1)} %get-tuple-element.32.meta_ref.refs_0_, bf16[4096,1280]{1,0:T(8,128)(2,1)S(1)} %load.1.refs_1_, bf16[1536,1280]{1,0:T(8,128)(2,1)S(1)} %collective-permute-done.1.refs_2_, ...), custom_call_target="tpu_custom_call" | custom-call | tf_op jit(solution)/shard_map/pool/pallas_call | solution.py:422
  32.5 0.1 collective-permute-start.4
  32.6 0.0 copy-start
  32.7 6.5 %collective-permute-done.4.refs_5_ = bf16[648,128]{1,0:T(8,128)(2,1)S(1)} collective-permute-done((bf16[648,128]{1,0:T(8,128)(2,1)S(1)}, bf16[648,128]{1,0:T(8,128)(2,1)S(1)}, u32[]{:S(2)}, u32[]{:S(2)}) %collective-permute-start.4) | collective-permute-done | bytes 165920 | tf_op jit(solution)/shard_map/ppermute | solution.py:439
  39.1 0.0 slice-start
  39.1 0.0 slice-start.1
  39.1 6.7 %pool.5 = (f32[128,1280]{1,0:T(8,128)S(1)}, f32[128,128]{1,0:T(8,128)S(1)}, bf16[648,128]{1,0:T(8,128)(2,1)S(1)}) custom-call(s32[8,1280]{1,0:T(8,128)S(1)} %get-tuple-element.32.meta_ref.refs_0_, bf16[4096,1280]{1,0:T(8,128)(2,1)S(1)} %load.1.refs_1_, bf16[1536,1280]{1,0:T(8,128)(2,1)S(1)} %collective-permute-done.1.refs_2_, ...), custom_call_target="tpu_custom_call" | custom-call | tf_op jit(solution)/shard_map/pool/pallas_call | solution.py:422
  45.9 0.1 collective-permute-start.5
  46.0 0.0 copy-done
  46.0 0.0 slice-start.2
  46.0 6.5 %collective-permute-done.5.recv_ref = bf16[648,128]{1,0:T(8,128)(2,1)S(1)} collective-permute-done((bf16[648,128]{1,0:T(8,128)(2,1)S(1)}, bf16[648,128]{1,0:T(8,128)(2,1)S(1)}, u32[]{:S(2)}, u32[]{:S(2)}) %collective-permute-start.5) | collective-permute-done | bytes 165920 | tf_op jit(solution)/shard_map/ppermute | solution.py:439
  52.5 0.3 norm.1.normed_ref
  52.8 0.1 collective-permute-start.6
  52.9 1.4 %collective-permute-done.6.other_ref = bf16[64,1280]{1,0:T(8,128)(2,1)S(1)} collective-permute-done((bf16[64,1280]{1,0:T(8,128)(2,1)S(1)}, bf16[64,1280]{1,0:T(8,128)(2,1)S(1)}, u32[]{:S(2)}, u32[]{:S(2)}) %collective-permute-start.6) | collective-permute-done | bytes 163872 | tf_op jit(solution)/shard_map/ppermute | solution.py:456
  54.3 0.0 slice-done
  54.3 0.0 slice-done.1
  54.3 0.0 slice-done.2
  54.3 2.5 %convolution_convert_fusion = bf16[128,4096]{1,0:T(8,128)(2,1)} fusion(bf16[128,1280]{1,0:T(8,128)(2,1)S(1)} %join.1, bf16[1280,4096]{1,0:T(8,128)(2,1)S(1)} %bitcast.3), kind=kOutput, calls=%fused_computation | convolution fusion | flops 1342701568 | bytes 11862016 | tf_op jit(solution)/shard_map/dot_general | solution.py:457
  (8 shorter events, 0.1 us)
Async XLA Ops:
  3.3 2.1 %collective-permute-start = (bf16[64,1280]{1,0:T(8,128)(2,1)S(1)}, bf16[64,1280]{1,0:T(8,128)(2,1)S(1)}, u32[]{:S(2)}, u32[]{:S(2)}) collective-permute-start(bf16[64,1280]{1,0:T(8,128)(2,1)S(1)} %get-tuple-element.36.tail_ref), channel_id=1, source_target_pairs={{0,1},{1,0},{2,3},{3,2},{4,5},{5,4},{6,7},{7,6},{8,9},{9,8},{10,11... | collective-permute-start | bytes 491528 | tf_op jit(solution)/shard_map/ppermute | solution.py:386
  5.4 7.0 %collective-permute-start.1 = (bf16[1536,1280]{1,0:T(8,128)(2,1)S(1)}, bf16[1536,1280]{1,0:T(8,128)(2,1)S(1)}, u32[]{:S(2)}, u32[]{:S(2)}) collective-permute-start(bf16[1536,1280]{1,0:T(8,128)(2,1)S(1)} %get-tuple-element.42), channel_id=1, source_target_pairs={{0,1},{1,0},{2,3},{3,2},{4,5},{5,4},{6,7},{7,6},{8,9},{9,8},{10,11... | collective-permute-start | bytes 11796488 | tf_op jit(solution)/shard_map/ppermute | solution.py:413
  5.5 6.8 %collective-permute-start.2 = (bf16[64,1280]{1,0:T(8,128)(2,1)S(1)}, bf16[64,1280]{1,0:T(8,128)(2,1)S(1)}, u32[]{:S(2)}, u32[]{:S(2)}) collective-permute-start(bf16[64,1280]{1,0:T(8,128)(2,1)S(1)} %get-tuple-element.62.order_ref.refs_3_), channel_id=1, source_target_pairs={{1,2},{3,4},{5,6},{7,8},{9,10},{11,12},{13,14},{15,16},{17,18},{19... | collective-permute-start | bytes 491528 | tf_op jit(solution)/shard_map/ppermute | solution.py:416
  19.1 6.7 %collective-permute-start.3 = (bf16[648,128]{1,0:T(8,128)(2,1)S(1)}, bf16[648,128]{1,0:T(8,128)(2,1)S(1)}, u32[]{:S(2)}, u32[]{:S(2)}) collective-permute-start(bf16[648,128]{1,0:T(8,128)(2,1)S(1)} %get-tuple-element.46), channel_id=1, source_target_pairs={{1,2},{3,4},{5,6},{7,8},{9,10},{11,12},{13,14},{15,16},{17,18},{19... | collective-permute-start | bytes 497672 | tf_op jit(solution)/shard_map/ppermute | solution.py:434
  32.5 6.6 %collective-permute-start.4 = (bf16[648,128]{1,0:T(8,128)(2,1)S(1)}, bf16[648,128]{1,0:T(8,128)(2,1)S(1)}, u32[]{:S(2)}, u32[]{:S(2)}) collective-permute-start(bf16[648,128]{1,0:T(8,128)(2,1)S(1)} %get-tuple-element.50), channel_id=1, source_target_pairs={{1,2},{3,4},{5,6},{7,8},{9,10},{11,12},{13,14},{15,16},{17,18},{19... | collective-permute-start | bytes 497672 | tf_op jit(solution)/shard_map/ppermute | solution.py:439
  32.6 13.3 %copy-start = (f32[1280]{0:T(1024)S(1)}, f32[1280]{0:T(1024)}, u32[]{:S(2)}) copy-start(f32[1280]{0:T(1024)} %param.8) | copy-start | bytes 15364
  39.1 15.1 %slice-start = ((s8[10485760]{0:T(1024)(128)(4,1)}), s8[4194304]{0:T(1024)(128)(4,1)S(1)}, s32[]{:S(2)}) async-start(s8[10485760]{0:T(1024)(128)(4,1)} %bitcast.2), calls=%async_computation | async-start | bytes 8388608
  39.1 15.1 %slice-start.1 = ((s8[10485760]{0:T(1024)(128)(4,1)}), s8[4194304]{0:T(1024)(128)(4,1)S(1)}, s32[]{:S(2)}) async-start(s8[10485760]{0:T(1024)(128)(4,1)} %bitcast.2), calls=%async_computation.1 | async-start | bytes 8388608
  45.9 6.6 %collective-permute-start.5 = (bf16[648,128]{1,0:T(8,128)(2,1)S(1)}, bf16[648,128]{1,0:T(8,128)(2,1)S(1)}, u32[]{:S(2)}, u32[]{:S(2)}) collective-permute-start(bf16[648,128]{1,0:T(8,128)(2,1)S(1)} %get-tuple-element.53), channel_id=1, source_target_pairs={{1,2},{3,4},{5,6},{7,8},{9,10},{11,12},{13,14},{15,16},{17,18},{19... | collective-permute-start | bytes 497672 | tf_op jit(solution)/shard_map/ppermute | solution.py:439
  46.0 8.3 %slice-start.2 = ((s8[10485760]{0:T(1024)(128)(4,1)}), s8[2097152]{0:T(1024)(128)(4,1)S(1)}, s32[]{:S(2)}) async-start(s8[10485760]{0:T(1024)(128)(4,1)} %bitcast.2), calls=%async_computation.2 | async-start | bytes 4194304
  52.8 1.5 %collective-permute-start.6 = (bf16[64,1280]{1,0:T(8,128)(2,1)S(1)}, bf16[64,1280]{1,0:T(8,128)(2,1)S(1)}, u32[]{:S(2)}, u32[]{:S(2)}) collective-permute-start(bf16[64,1280]{1,0:T(8,128)(2,1)S(1)} %norm.1.normed_ref), channel_id=1, source_target_pairs={{0,1},{1,0},{2,3},{3,2},{4,5},{5,4},{6,7},{7,6},{8,9},{9,8},{10,11... | collective-permute-start | bytes 491528 | tf_op jit(solution)/shard_map/ppermute | solution.py:456

commit v10 on v9

--- a/solution.py
+++ b/solution.py
@@ -91,7 +91,7 @@
             ).start()
             return carry
 
-        lax.fori_loop(0, count, fetch, 0, unroll=8)
+        lax.fori_loop(0, count, fetch, 0, unroll=32)
 
     low = jnp.where(second, here - base, 0)
     high = jnp.where(second, rows, after - base)

time: 57.4 us -> 57.3 us (level)
  no operation moved by 1% of the time
where the time goes in v10:
time: 57.3 us; the launch traced here: 56.8 us
  Pallas kernels  29.2 us (51%)
  waiting for transfers between devices  20.8 us (36%)
  starting transfers between devices  3.99 us (7%)
  matrix products  2.51 us (4%)
    pallas_call x6, Pallas kernels, pool(): pl.pallas_call(functools.partial(pool_kernel, first, ends, devices), out_...  20.2 us
    ppermute x3, waiting for transfers between devices, on_device(): received = lax.ppermute(send, AXES, across)  18.4 us
    pallas_call x1, Pallas kernels, fetch(): pl.pallas_call(kernel, out_shape=shape(size, width), in_specs=[HBM_SPEC,...  4.1 us
    pallas_call x1, Pallas kernels, on_device(): pl.pallas_call(seed_kernel, out_shape=(shape(count, width), shape(8 * cou...  3.28 us
    dot_general x1, matrix products, on_device(): return jnp.dot(both, proj_weight, preferred_element_type=F32).astype(BF16)  2.51 us
    ppermute x1, starting transfers between devices, on_device(): received = lax.ppermute(x, AXES, across)  1.65 us
    ppermute x3, starting transfers between devices, on_device(): received = lax.ppermute(send, AXES, across)  1.45 us
    ppermute x1, waiting for transfers between devices, on_device(): lax.ppermute(normed, 'feat', pair)  1.38 us
  transfers between devices with their start and end apart: 7, of which 5 were waited for; matrix products, arithmetic and copies ran while one was open for 0% of the time, Pallas kernels for 10%

profile of v10, /device:TPU:29, one launch (start us, length us, event | category | flops | bytes accessed | tf_op | source)
XLA Modules:
  0.0 56.8 jit_solution(8246440280368544435)
XLA Ops:
  0.0 3.3 %seeds.1 = (bf16[64,1280]{1,0:T(8,128)(2,1)S(1)}, bf16[512,1280]{1,0:T(8,128)(2,1)S(1)}, bf16[64,512]{1,0:T(8,128)(2,1)S(1)}, bf16[2,1280]{1,0:T(2,128)(2,1)S(1)...) custom-call(s32[32]{0:T(128)} %starts_hbm.1, s32[32,64]{1,0:T(8,128)} %seeds_hbm.1, bf16[4096,1280]{1,0:T(8,128)(2,1)} %tokens_ref.5), custom_call_target="tpu_custom_call" | custom-call | tf_op jit(solution)/shard_map/seeds/pallas_call | solution.py:362
  3.3 0.7 %collective-permute-start = (bf16[64,1280]{1,0:T(8,128)(2,1)S(1)}, bf16[64,1280]{1,0:T(8,128)(2,1)S(1)}, u32[]{:S(2)}, u32[]{:S(2)}) collective-permute-start(bf16[64,1280]{1,0:T(8,128)(2,1)S(1)} %get-tuple-element.36.tail_ref), channel_id=1, source_target_pairs={{0,1},{1,0},{2,3},{3,2},{4,5},{5,4},{6,7},{7,6},{8,9},{9,8},{10,11... | collective-permute-start | bytes 491528 | tf_op jit(solution)/shard_map/ppermute | solution.py:386
  4.0 1.3 %own.1 = (bf16[64,1280]{1,0:T(8,128)(2,1)S(1)}, bf16[64,1280]{1,0:T(8,128)(2,1)S(1)}, bf16[1536,1280]{1,0:T(8,128)(2,1)S(1)}) custom-call(bf16[4096,1280]{1,0:T(8,128)(2,1)} %tokens_ref.5, bf16[1536,1280]{1,0:T(8,128)(2,1)S(1)} %get-tuple-element.33.edge_in_ref, bf16[512,1280]{1,0:T(8,128)(2,1)S(1)} %get-tuple-element.34.near_ref, ...), custom_call_target="tpu_custom_call", output_to_operand_aliasing={{2}: (1, {})} | custom-call | flops 83886080 | bytes 1966080 | tf_op jit(solution)/shard_map/own/pallas_call | solution.py:387
  5.3 0.0 collective-permute-done
  5.3 0.1 collective-permute-start.1
  5.5 1.7 %collective-permute-start.2 = (bf16[64,1280]{1,0:T(8,128)(2,1)S(1)}, bf16[64,1280]{1,0:T(8,128)(2,1)S(1)}, u32[]{:S(2)}, u32[]{:S(2)}) collective-permute-start(bf16[64,1280]{1,0:T(8,128)(2,1)S(1)} %get-tuple-element.62.order_ref.refs_3_), channel_id=1, source_target_pairs={{1,2},{3,4},{5,6},{7,8},{9,10},{11,12},{13,14},{15,16},{17,18},{19... | collective-permute-start | bytes 491528 | tf_op jit(solution)/shard_map/ppermute | solution.py:416
  7.2 4.1 %load.1.refs_1_ = bf16[4096,1280]{1,0:T(8,128)(2,1)S(1)} custom-call(bf16[4096,1280]{1,0:T(8,128)(2,1)} %tokens_ref.5, bf16[64,1280]{1,0:T(8,128)(2,1)S(1)} %get-tuple-element.62.order_ref.refs_3_), custom_call_target="tpu_custom_call" | custom-call | tf_op jit(solution)/shard_map/load/pallas_call | solution.py:402
  11.3 1.0 %collective-permute-done.2.refs_4_ = bf16[64,1280]{1,0:T(8,128)(2,1)S(1)} collective-permute-done((bf16[64,1280]{1,0:T(8,128)(2,1)S(1)}, bf16[64,1280]{1,0:T(8,128)(2,1)S(1)}, u32[]{:S(2)}, u32[]{:S(2)}) %collective-permute-start.2) | collective-permute-done | bytes 163872 | tf_op jit(solution)/shard_map/ppermute | solution.py:416
  12.3 0.0 collective-permute-done.1.refs_2_
  12.3 6.7 %pool.3 = (f32[128,1280]{1,0:T(8,128)S(1)}, f32[128,128]{1,0:T(8,128)S(1)}, bf16[648,128]{1,0:T(8,128)(2,1)S(1)}) custom-call(s32[8,1280]{1,0:T(8,128)S(1)} %get-tuple-element.32.meta_ref.refs_0_, bf16[4096,1280]{1,0:T(8,128)(2,1)S(1)} %load.1.refs_1_, bf16[1536,1280]{1,0:T(8,128)(2,1)S(1)} %collective-permute-done.1.refs_2_, ...), custom_call_target="tpu_custom_call" | custom-call | tf_op jit(solution)/shard_map/pool/pallas_call | solution.py:422
  19.0 1.3 %collective-permute-start.3 = (bf16[648,128]{1,0:T(8,128)(2,1)S(1)}, bf16[648,128]{1,0:T(8,128)(2,1)S(1)}, u32[]{:S(2)}, u32[]{:S(2)}) collective-permute-start(bf16[648,128]{1,0:T(8,128)(2,1)S(1)} %get-tuple-element.46), channel_id=1, source_target_pairs={{1,2},{3,4},{5,6},{7,8},{9,10},{11,12},{13,14},{15,16},{17,18},{19... | collective-permute-start | bytes 497672 | tf_op jit(solution)/shard_map/ppermute | solution.py:434
  20.3 5.5 %collective-permute-done.3.refs_5_ = bf16[648,128]{1,0:T(8,128)(2,1)S(1)} collective-permute-done((bf16[648,128]{1,0:T(8,128)(2,1)S(1)}, bf16[648,128]{1,0:T(8,128)(2,1)S(1)}, u32[]{:S(2)}, u32[]{:S(2)}) %collective-permute-start.3) | collective-permute-done | bytes 165920 | tf_op jit(solution)/shard_map/ppermute | solution.py:434
  25.7 6.8 %pool.4 = (f32[128,1280]{1,0:T(8,128)S(1)}, f32[128,128]{1,0:T(8,128)S(1)}, bf16[648,128]{1,0:T(8,128)(2,1)S(1)}) custom-call(s32[8,1280]{1,0:T(8,128)S(1)} %get-tuple-element.32.meta_ref.refs_0_, bf16[4096,1280]{1,0:T(8,128)(2,1)S(1)} %load.1.refs_1_, bf16[1536,1280]{1,0:T(8,128)(2,1)S(1)} %collective-permute-done.1.refs_2_, ...), custom_call_target="tpu_custom_call" | custom-call | tf_op jit(solution)/shard_map/pool/pallas_call | solution.py:422
  32.5 0.1 collective-permute-start.4
  32.6 0.0 copy-start
  32.6 6.5 %collective-permute-done.4.refs_5_ = bf16[648,128]{1,0:T(8,128)(2,1)S(1)} collective-permute-done((bf16[648,128]{1,0:T(8,128)(2,1)S(1)}, bf16[648,128]{1,0:T(8,128)(2,1)S(1)}, u32[]{:S(2)}, u32[]{:S(2)}) %collective-permute-start.4) | collective-permute-done | bytes 165920 | tf_op jit(solution)/shard_map/ppermute | solution.py:439
  39.1 0.0 slice-start
  39.1 0.0 slice-start.1
  39.1 6.7 %pool.5 = (f32[128,1280]{1,0:T(8,128)S(1)}, f32[128,128]{1,0:T(8,128)S(1)}, bf16[648,128]{1,0:T(8,128)(2,1)S(1)}) custom-call(s32[8,1280]{1,0:T(8,128)S(1)} %get-tuple-element.32.meta_ref.refs_0_, bf16[4096,1280]{1,0:T(8,128)(2,1)S(1)} %load.1.refs_1_, bf16[1536,1280]{1,0:T(8,128)(2,1)S(1)} %collective-permute-done.1.refs_2_, ...), custom_call_target="tpu_custom_call" | custom-call | tf_op jit(solution)/shard_map/pool/pallas_call | solution.py:422
  45.9 0.1 collective-permute-start.5
  45.9 0.0 copy-done
  46.0 0.0 slice-start.2
  46.0 6.5 %collective-permute-done.5.recv_ref = bf16[648,128]{1,0:T(8,128)(2,1)S(1)} collective-permute-done((bf16[648,128]{1,0:T(8,128)(2,1)S(1)}, bf16[648,128]{1,0:T(8,128)(2,1)S(1)}, u32[]{:S(2)}, u32[]{:S(2)}) %collective-permute-start.5) | collective-permute-done | bytes 165920 | tf_op jit(solution)/shard_map/ppermute | solution.py:439
  52.5 0.3 norm.1.normed_ref
  52.8 0.1 collective-permute-start.6
  52.8 1.4 %collective-permute-done.6.other_ref = bf16[64,1280]{1,0:T(8,128)(2,1)S(1)} collective-permute-done((bf16[64,1280]{1,0:T(8,128)(2,1)S(1)}, bf16[64,1280]{1,0:T(8,128)(2,1)S(1)}, u32[]{:S(2)}, u32[]{:S(2)}) %collective-permute-start.6) | collective-permute-done | bytes 163872 | tf_op jit(solution)/shard_map/ppermute | solution.py:456
  54.2 0.0 slice-done
  54.2 0.0 slice-done.1
  54.3 0.0 slice-done.2
  54.3 2.5 %convolution_convert_fusion = bf16[128,4096]{1,0:T(8,128)(2,1)} fusion(bf16[128,1280]{1,0:T(8,128)(2,1)S(1)} %join.1, bf16[1280,4096]{1,0:T(8,128)(2,1)S(1)} %bitcast.3), kind=kOutput, calls=%fused_computation | convolution fusion | flops 1342701568 | bytes 11862016 | tf_op jit(solution)/shard_map/dot_general | solution.py:457
  (8 shorter events, 0.1 us)
Async XLA Ops:
  3.3 2.1 %collective-permute-start = (bf16[64,1280]{1,0:T(8,128)(2,1)S(1)}, bf16[64,1280]{1,0:T(8,128)(2,1)S(1)}, u32[]{:S(2)}, u32[]{:S(2)}) collective-permute-start(bf16[64,1280]{1,0:T(8,128)(2,1)S(1)} %get-tuple-element.36.tail_ref), channel_id=1, source_target_pairs={{0,1},{1,0},{2,3},{3,2},{4,5},{5,4},{6,7},{7,6},{8,9},{9,8},{10,11... | collective-permute-start | bytes 491528 | tf_op jit(solution)/shard_map/ppermute | solution.py:386
  5.3 7.0 %collective-permute-start.1 = (bf16[1536,1280]{1,0:T(8,128)(2,1)S(1)}, bf16[1536,1280]{1,0:T(8,128)(2,1)S(1)}, u32[]{:S(2)}, u32[]{:S(2)}) collective-permute-start(bf16[1536,1280]{1,0:T(8,128)(2,1)S(1)} %get-tuple-element.42), channel_id=1, source_target_pairs={{0,1},{1,0},{2,3},{3,2},{4,5},{5,4},{6,7},{7,6},{8,9},{9,8},{10,11... | collective-permute-start | bytes 11796488 | tf_op jit(solution)/shard_map/ppermute | solution.py:413
  5.5 6.8 %collective-permute-start.2 = (bf16[64,1280]{1,0:T(8,128)(2,1)S(1)}, bf16[64,1280]{1,0:T(8,128)(2,1)S(1)}, u32[]{:S(2)}, u32[]{:S(2)}) collective-permute-start(bf16[64,1280]{1,0:T(8,128)(2,1)S(1)} %get-tuple-element.62.order_ref.refs_3_), channel_id=1, source_target_pairs={{1,2},{3,4},{5,6},{7,8},{9,10},{11,12},{13,14},{15,16},{17,18},{19... | collective-permute-start | bytes 491528 | tf_op jit(solution)/shard_map/ppermute | solution.py:416
  19.0 6.7 %collective-permute-start.3 = (bf16[648,128]{1,0:T(8,128)(2,1)S(1)}, bf16[648,128]{1,0:T(8,128)(2,1)S(1)}, u32[]{:S(2)}, u32[]{:S(2)}) collective-permute-start(bf16[648,128]{1,0:T(8,128)(2,1)S(1)} %get-tuple-element.46), channel_id=1, source_target_pairs={{1,2},{3,4},{5,6},{7,8},{9,10},{11,12},{13,14},{15,16},{17,18},{19... | collective-permute-start | bytes 497672 | tf_op jit(solution)/shard_map/ppermute | solution.py:434
  32.5 6.6 %collective-permute-start.4 = (bf16[648,128]{1,0:T(8,128)(2,1)S(1)}, bf16[648,128]{1,0:T(8,128)(2,1)S(1)}, u32[]{:S(2)}, u32[]{:S(2)}) collective-permute-start(bf16[648,128]{1,0:T(8,128)(2,1)S(1)} %get-tuple-element.50), channel_id=1, source_target_pairs={{1,2},{3,4},{5,6},{7,8},{9,10},{11,12},{13,14},{15,16},{17,18},{19... | collective-permute-start | bytes 497672 | tf_op jit(solution)/shard_map/ppermute | solution.py:439
  32.6 13.3 %copy-start = (f32[1280]{0:T(1024)S(1)}, f32[1280]{0:T(1024)}, u32[]{:S(2)}) copy-start(f32[1280]{0:T(1024)} %param.8) | copy-start | bytes 15364
  39.1 15.1 %slice-start = ((s8[10485760]{0:T(1024)(128)(4,1)}), s8[4194304]{0:T(1024)(128)(4,1)S(1)}, s32[]{:S(2)}) async-start(s8[10485760]{0:T(1024)(128)(4,1)} %bitcast.2), calls=%async_computation | async-start | bytes 8388608
  39.1 15.1 %slice-start.1 = ((s8[10485760]{0:T(1024)(128)(4,1)}), s8[4194304]{0:T(1024)(128)(4,1)S(1)}, s32[]{:S(2)}) async-start(s8[10485760]{0:T(1024)(128)(4,1)} %bitcast.2), calls=%async_computation.1 | async-start | bytes 8388608
  45.9 6.6 %collective-permute-start.5 = (bf16[648,128]{1,0:T(8,128)(2,1)S(1)}, bf16[648,128]{1,0:T(8,128)(2,1)S(1)}, u32[]{:S(2)}, u32[]{:S(2)}) collective-permute-start(bf16[648,128]{1,0:T(8,128)(2,1)S(1)} %get-tuple-element.53), channel_id=1, source_target_pairs={{1,2},{3,4},{5,6},{7,8},{9,10},{11,12},{13,14},{15,16},{17,18},{19... | collective-permute-start | bytes 497672 | tf_op jit(solution)/shard_map/ppermute | solution.py:439
  46.0 8.3 %slice-start.2 = ((s8[10485760]{0:T(1024)(128)(4,1)}), s8[2097152]{0:T(1024)(128)(4,1)S(1)}, s32[]{:S(2)}) async-start(s8[10485760]{0:T(1024)(128)(4,1)} %bitcast.2), calls=%async_computation.2 | async-start | bytes 4194304
  52.8 1.5 %collective-permute-start.6 = (bf16[64,1280]{1,0:T(8,128)(2,1)S(1)}, bf16[64,1280]{1,0:T(8,128)(2,1)S(1)}, u32[]{:S(2)}, u32[]{:S(2)}) collective-permute-start(bf16[64,1280]{1,0:T(8,128)(2,1)S(1)} %norm.1.normed_ref), channel_id=1, source_target_pairs={{0,1},{1,0},{2,3},{3,2},{4,5},{5,4},{6,7},{7,6},{8,9},{9,8},{10,11... | collective-permute-start | bytes 491528 | tf_op jit(solution)/shard_map/ppermute | solution.py:456
